TPU v7x, 128 devices: a whole 4x4x4 slice. The times are simulated.
128 devices in a mesh: wide: 8 (over x, core), narrow: 16 (over z, y).
Axes of the slice: x: 4, y: 4, z: 4, core: 2. Of those that a mesh axis runs over, the one named last changes fastest.
Arguments:
- basis_t: bfloat16 [8192, 64, 256], P(('wide', 'narrow')), may hold values from -0.375 to 0.375
- nested_transfer_matrices: float32 [64, 64, 16384], P(None, None, ('wide', 'narrow')), may hold values from -0.22 to 0.93
- leaf_coupling: float32 [64, 64, 65536], P(None, None, ('wide', 'narrow')), may hold values from -6 to 6
- leaf_columns: int32 [65536], P(('wide', 'narrow')), may hold values from 0 to 8191, as said below
- far_coupling: float32 [64, 64, 2048], P(None, None, ('wide', 'narrow')), may hold values from -6 to 6
- far_columns: int32 [2048], P(('wide', 'narrow')), may hold values from 0 to 7, as said below
Outputs:
- leaf_coupled: float32 [64, 64, 65536], P(None, None, ('wide', 'narrow'))
- far_coupled: float32 [64, 64, 2048], P(None, None, ('wide', 'narrow'))
- group_factors: float32 [128, 64, 64], P(('wide', 'narrow'))
Inputs may be any that keep to these rules, and one draw needn't show every extreme that they name: `leaf_columns`: block b's column leaf lies 2 to 64 leaves away from its row leaf b // 8; on every device some block lies exactly 64 leaves away. `far_columns`: block f's column branch differs from its row branch f // 256.
All inputs are finite; a program needn't handle non-finite values.
Results may differ from a plain program's by a relative error of at most 0.0003.
Values sent between devices are 32-bit elements; how exact they have to be, the bound alone decides.
No kernel may reach another device: no remote copies, remote signals or barrier semaphores. Data moves between devices by JAX's collectives and lax.ppermute only.
A program may use at most 192 MiB of HBM per device.

v0:
```python
import functools

import jax
import jax.numpy as jnp
from jax import lax
from jax.experimental import pallas as pl
from jax.experimental.pallas import tpu as pltpu
from jax.sharding import PartitionSpec as P

F32 = jnp.float32
BF16 = jnp.bfloat16
ANY = pl.BlockSpec(memory_space=pl.ANY)
VMEM = pl.BlockSpec(memory_space=pltpu.VMEM)
SMEM = pl.BlockSpec(memory_space=pltpu.SMEM)


def params(mib):
    return pltpu.CompilerParams(vmem_limit_bytes=mib * 2**20)


def cost(us):
    return pl.CostEstimate(flops=int(us * 1.15e9), bytes_accessed=4096, transcendentals=0)


def split(x):
    hi = x.astype(BF16)
    lo = (x - hi.astype(F32)).astype(BF16)
    return hi, lo


def mm(a, b):
    return lax.dot_general(a, b, (((1,), (0,)), ((), ())), preferred_element_type=F32)


def mm_nt(a, b):
    return lax.dot_general(a, b, (((1,), (1,)), ((), ())), preferred_element_type=F32)


def mm_tn(a, b):
    return lax.dot_general(a, b, (((0,), (0,)), ((), ())), preferred_element_type=F32)


def lanes(*parts):
    return jnp.concatenate(parts, axis=1)


def rows(*parts):
    return jnp.concatenate(parts, axis=0)


def first_half(shape=(64, 128)):
    return lax.broadcasted_iota(jnp.int32, shape, 1) % 128 < 64


def left_of(m):
    h, l = split(m)
    v = jnp.where(first_half(), h, l)
    return lanes(v, v)


def right_of(m):
    return lanes(*split(m))


def twice(m):
    return rows(m, m)


def climb_kernel(b_hbm, t_hbm, g_ref, top_ref, pay_ref, b_ref, t_ref, e_ref, v_ref, sem):
    t_copies = [
        pltpu.make_async_copy(
            t_hbm.at[pl.ds(16 * n, 16)], t_ref.at[pl.ds(16 * n, 16)], sem.at[n]
        )
        for n in range(4)
    ]
    b_copies = [
        pltpu.make_async_copy(
            b_hbm.at[pl.ds(32 * n, 32)], b_ref.at[pl.ds(32 * n, 32)], sem.at[4 + n]
        )
        for n in range(2)
    ]
    for copy in t_copies + b_copies:
        copy.start()
    first = first_half()

    def turn(k, _):
        x = t_ref[k]
        e_ref[k] = rows(x, x).T
        return 0

    for n in range(4):
        t_copies[n].wait()
        lax.fori_loop(16 * n, 16 * n + 16, turn, 0, unroll=8)

    row = lax.broadcasted_iota(jnp.int32, (64, 128), 0)
    col = lax.broadcasted_iota(jnp.int32, (64, 128), 1)
    eye = (row == col).astype(F32)
    v_ref[1, :, 0:128] = lanes(eye[:, 0:64], eye[:, 0:64]).astype(BF16)
    v_ref[1, :, 128:256] = jnp.zeros((64, 128), BF16)

    def down(p, _):
        v = jnp.where(first, v_ref[p, :, 0:128], v_ref[p, :, 128:256])
        r0 = right_of(e_ref[:, 2 * p, :])
        r1 = right_of(e_ref[:, 2 * p + 1, :])
        z = mm_nt(lanes(v, v), rows(r0, r0, r1, r1))
        for c in range(2):
            v_ref[2 * p + c] = right_of(z[:, 128 * c : 128 * c + 128])
        return 0

    for level in range(6):
        n = 2**level
        lax.fori_loop(n, 2 * n, down, 0, unroll=min(8, n))
    for copy in b_copies:
        copy.wait()

    def leaf(q, acc):
        grams, prods, vs = [], [], []
        for c in range(2):
            t = q + 32 * c
            b = b_ref[t]
            g = mm_nt(b, twice(b))
            grams.append(g)
            v = v_ref[64 + t]
            vs.append(v)
            vv = jnp.where(first, v[:, 0:128], v[:, 128:256])
            prods.append(mm_nt(lanes(vv, vv), twice(right_of(g))))
        g_ref[q] = jnp.where(first, grams[0], grams[1])
        ph, pl_ = split(jnp.where(first, prods[0], prods[1]))
        vh = jnp.where(first, vs[0][:, 0:128], vs[1][:, 0:128])
        vl = jnp.where(first, vs[0][:, 128:256], vs[1][:, 128:256])
        right = lanes(vh, vh, vl)
        return acc + mm_nt(lanes(ph, pl_, ph), twice(right))

    top = lax.fori_loop(0, 32, leaf, jnp.zeros((64, 128), F32), unroll=8)
    top_ref[...] = top
    e = e_ref[:, 1, :]
    v = mm_nt(lanes(eye, eye).astype(BF16)[:, 0:128], twice(split(e)[0])) + mm_nt(
        eye.astype(BF16), twice(split(e)[1])
    )
    prod = mm_nt(left_of(v), twice(right_of(top)))
    vh, vl = split(v)
    term = mm_nt(left_of(prod), twice(lanes(vh, vl)))
    pay_ref[...] = jnp.where(first, term, e_ref[:, 0, :])


def climb(basis, transfers):
    return pl.pallas_call(
        climb_kernel,
        out_shape=(
            jax.ShapeDtypeStruct((32, 64, 128), F32),
            jax.ShapeDtypeStruct((64, 128), F32),
            jax.ShapeDtypeStruct((64, 128), F32),
        ),
        in_specs=[pl.BlockSpec(memory_space=pltpu.HBM)] * 2,
        out_specs=(VMEM,) * 3,
        scratch_shapes=[
            pltpu.VMEM((64, 64, 256), BF16),
            pltpu.VMEM((64, 64, 128), F32),
            pltpu.VMEM((64, 128, 128), F32),
            pltpu.VMEM((128, 64, 256), BF16),
            pltpu.SemaphoreType.DMA((6,)),
        ],
        compiler_params=params(20),
        cost_estimate=cost(10),
        name="climb",
    )(basis, transfers)


def chol_lanes(a_ref, count=64, panel=8):
    sub = lax.broadcasted_iota(jnp.int32, (8, 128), 0)
    for p in range(count // panel):
        base = p * panel
        if p > 0:
            for it in range(p, count // 8):

                def body(k, accs):
                    lv = a_ref[k, it * 8 : it * 8 + 8, :]
                    return tuple(
                        accs[j] - lv * a_ref[k, pl.ds(base + j, 8, stride=0), :]
                        for j in range(panel)
                    )

                accs = tuple(
                    a_ref[base + j, it * 8 : it * 8 + 8, :] for j in range(panel)
                )
                accs = lax.fori_loop(0, base, body, accs, unroll=8)
                for j in range(panel):
                    a_ref[base + j, it * 8 : it * 8 + 8, :] = accs[j]
        d = [a_ref[base + j, base : base + 8, :] for j in range(8)]
        invs = []
        for j in range(8):
            piv = jnp.broadcast_to(d[j][j : j + 1, :], (8, 128))
            inv = lax.rsqrt(piv)
            invs.append(inv)
            d[j] = jnp.where(sub >= j, d[j] * inv, 0.0)
            for m in range(j + 1, 8):
                d[m] = d[m] - d[j] * jnp.broadcast_to(d[j][m : m + 1, :], (8, 128))
            a_ref[base + j, base : base + 8, :] = d[j]
            if base > 0:
                a_ref[base + j, 0:base, :] = jnp.zeros((base, 128), F32)
        bc = {}
        for j in range(8):
            for m in range(j + 1, 8):
                bc[j, m] = jnp.broadcast_to(d[j][m : m + 1, :], (8, 128))
        for it in range(p + 1, count // 8):
            v = [a_ref[base + j, it * 8 : it * 8 + 8, :] for j in range(8)]
            for j in range(8):
                v[j] = v[j] * invs[j]
                for m in range(j + 1, 8):
                    v[m] = v[m] - v[j] * bc[j, m]
                a_ref[base + j, it * 8 : it * 8 + 8, :] = v[j]


def leaf_chol_kernel(g_ref, low_ref, a_ref):
    def load(k, _):
        x = g_ref[:, k, :]
        y = pltpu.roll(x, 64, 1)
        a_ref[k] = rows(x, y, x, y).T[0:64]
        return 0

    lax.fori_loop(0, 64, load, 0, unroll=8)
    chol_lanes(a_ref)

    def store(i, _):
        x = a_ref[:, i, :]
        low_ref[i] = rows(x, pltpu.roll(x, 96, 1)).T[0:32]
        return 0

    lax.fori_loop(0, 64, store, 0, unroll=8)


def leaf_chol(gram):
    return pl.pallas_call(
        leaf_chol_kernel,
        out_shape=jax.ShapeDtypeStruct((64, 32, 128), F32),
        in_specs=[VMEM],
        out_specs=VMEM,
        scratch_shapes=[pltpu.VMEM((64, 64, 128), F32)],
        compiler_params=params(8),
        cost_estimate=cost(6),
        name="leaf_chol",
    )(gram)


def half_kernel(c0_ref, c1_ref, low_ref, y_ref, s_ref, part):
    step = pl.program_id(0)

    def turn(k, _):
        s_ref[step * 16 + k] = rows(c0_ref[k], c1_ref[k]).T
        return 0

    lax.fori_loop(0, 16, turn, 0, unroll=8)

    @pl.when(step == 3)
    def _():
        first = first_half((64, 1024))

        def leaf(t, _):
            w = lanes(*[s_ref[:, t * 8 + n, :] for n in range(8)])
            wh, wl = split(w)
            lh, ll = split(low_ref[:, 16 * part + t, :])
            z = mm_tn(rows(lh, ll, lh), rows(wh, wh, wl))
            yh, yl = split(jnp.where(first, z[0:64], z[64:128]))
            for n in range(8):
                y_ref[t * 8 + n, :, 0:128] = yh[:, n * 128 : n * 128 + 128]
                y_ref[t * 8 + n, :, 128:256] = yl[:, n * 128 : n * 128 + 128]
            return 0

        lax.fori_loop(0, 16, leaf, 0, unroll=2)


def half_leaf(coupling, low, part):
    return pl.pallas_call(
        functools.partial(half_kernel, part=part),
        out_shape=jax.ShapeDtypeStruct((128, 64, 256), BF16),
        grid=(4,),
        in_specs=[
            pl.BlockSpec((16, 64, 128), lambda s: (s, 0, part)),
            pl.BlockSpec((16, 64, 128), lambda s: (s, 0, part + 2)),
            pl.BlockSpec((64, 32, 128), lambda s: (0, 0, 0)),
        ],
        out_specs=pl.BlockSpec((128, 64, 256), lambda s: (0, 0, 0)),
        scratch_shapes=[pltpu.VMEM((64, 128, 128), F32)],
        compiler_params=params(22),
        cost_estimate=cost(6),
    )(coupling, coupling, low)


def prep_kernel(before_ref, own_ref, after_ref, d_ref):
    first = first_half()
    for group, ref in enumerate((before_ref, own_ref, after_ref)):

        def pair(q, _, ref=ref, group=group):
            x = ref[:, q, :]
            y = pltpu.roll(x, 64, 1)
            d_ref[group * 64 + q] = right_of(jnp.where(first, x, y))
            d_ref[group * 64 + 32 + q] = right_of(jnp.where(first, y, x))
            return 0

        lax.fori_loop(0, 32, pair, 0, unroll=8)


def prep(before, own, after):
    return pl.pallas_call(
        prep_kernel,
        out_shape=jax.ShapeDtypeStruct((192, 64, 256), BF16),
        in_specs=[VMEM] * 3,
        out_specs=VMEM,
        compiler_params=params(16),
        cost_estimate=cost(3),
        name="prep",
    )(before, own, after)


def full_kernel(cols_ref, y_ref, d_ref, *refs, part, mode):
    out_ref, s_ref, o_ref, sem = refs[-4:]
    lane = lax.broadcasted_iota(jnp.int32, (64, 256), 1)
    keep = ((lane % 128) < 64).astype(BF16)
    drop = ((lane % 128) >= 64).astype(BF16)
    zero = jnp.zeros((128, 128), BF16)

    def pair(p, _):
        sa = cols_ref[part * 128 + p]
        sb = cols_ref[part * 128 + 256 + p]
        r = rows(d_ref[sa] * keep, d_ref[sb] * drop)
        y = y_ref[p]
        if mode == 0:
            z = mm(y, rows(r, lanes(r[:, 0:128], zero)))
            s_ref[p] = z[:, 0:128] + z[:, 128:256]
        else:
            z = mm(rows(y[:, 0:128], y[:, 128:256]), r)
            s_ref[p] = z[0:64, 0:128] + z[0:64, 128:256] + z[64:128, 0:128]
        return 0

    lax.fori_loop(0, 128, pair, 0, unroll=8)

    def send(n):
        return [
            pltpu.make_async_copy(
                o_ref.at[c, pl.ds(16 * n, 16)],
                out_ref.at[pl.ds(16 * n, 16), :, pl.ds((part + 2 * c) * 128, 128)],
                sem.at[n, c],
            )
            for c in range(2)
        ]

    def turn(i, _):
        x = s_ref[:, i, :].T
        o_ref[0, i] = x[0:64]
        o_ref[1, i] = x[64:128]
        return 0

    for n in range(4):
        lax.fori_loop(16 * n, 16 * n + 16, turn, 0, unroll=8)
        for copy in send(n):
            copy.start()
    for n in range(4):
        for copy in send(n):
            copy.wait()


def full_leaf(cols, y, d, part, into=None, mode=1):
    extra = [] if into is None else [into]
    return pl.pallas_call(
        functools.partial(full_kernel, part=part, mode=mode),
        out_shape=jax.ShapeDtypeStruct((64, 64, 512), F32),
        in_specs=[SMEM, VMEM, VMEM] + [pl.BlockSpec(memory_space=pltpu.HBM)] * len(extra),
        out_specs=pl.BlockSpec(memory_space=pltpu.HBM),
        scratch_shapes=[
            pltpu.VMEM((128, 64, 128), F32),
            pltpu.VMEM((2, 64, 64, 128), F32),
            pltpu.SemaphoreType.DMA((4, 2)),
        ],
        input_output_aliases={} if into is None else {3: 0},
        compiler_params=params(22),
        cost_estimate=cost(8),
    )(cols, y, d, *extra)


def branch_kernel(at_ref, p0, p1, p2, p3, p4, p5, top_ref, gf_ref, low_ref, t_ref, e_ref, n_ref, a_ref):
    at = at_ref[0]
    pick = at_ref[1]
    first = first_half()

    def place(n, x):
        y = pltpu.roll(x, 64, 1)
        t_ref[n] = jnp.where(first, x, y)
        e_ref[n] = jnp.where(first, y, x)

    place(at, p0[...])
    place(at ^ 1, p1[...])
    for i in range(2):
        place(at ^ (2 + i), p2[i])
    for s, ref in enumerate((p3, p4, p5)):
        for i in range(4):
            place((at ^ i) - 4 * (s + 1) & 15, ref[i])
    n_ref[0] = top_ref[...]
    row = lax.broadcasted_iota(jnp.int32, (64, 64), 0)
    col = lax.broadcasted_iota(jnp.int32, (64, 64), 1)
    eye = (row == col).astype(BF16)
    eye = lanes(eye, eye)

    def term(p):
        v = mm_nt(eye, twice(jnp.where(first, *split(e_ref[p]))))
        prod = mm_nt(left_of(v), twice(right_of(n_ref[p])))
        return mm_nt(left_of(prod), twice(right_of(v)))

    for m in range(8):
        n_ref[8 + m] = t_ref[2 * m] + t_ref[2 * m + 1]
    for level in (2, 1, 0):
        for p in range(2**level, 2 ** (level + 1)):
            n_ref[p] = term(2 * p) + term(2 * p + 1)

    both = jnp.where(first, n_ref[pick], n_ref[1])
    lane = lax.broadcasted_iota(jnp.int32, (64, 128), 1)

    def load(k, _):
        a_ref[k] = jnp.take_along_axis(both, (lane & 64) + k, axis=1)
        return 0

    lax.fori_loop(0, 64, load, 0, unroll=8)
    chol_lanes(a_ref)

    def store(k, out):
        return jnp.where((lane & 63) == k, a_ref[k], out)

    out = lax.fori_loop(0, 64, store, jnp.zeros((64, 128), F32), unroll=8)
    gf_ref[0] = out.T[0:64]
    low_ref[...] = jnp.where(first, pltpu.roll(out, 64, 1), out)


def branch(at, parts, top):
    return pl.pallas_call(
        branch_kernel,
        out_shape=(
            jax.ShapeDtypeStruct((1, 64, 64), F32),
            jax.ShapeDtypeStruct((64, 128), F32),
        ),
        in_specs=[SMEM] + [VMEM] * 7,
        out_specs=(VMEM, VMEM),
        scratch_shapes=[
            pltpu.VMEM((16, 64, 128), F32),
            pltpu.VMEM((16, 64, 128), F32),
            pltpu.VMEM((16, 64, 128), F32),
            pltpu.VMEM((64, 64, 128), F32),
        ],
        compiler_params=params(8),
        cost_estimate=cost(5),
        name="branch",
    )(at, *parts, top)


def far_kernel(cols_ref, f_ref, l0, l1, l2, l3, o_ref, l_ref):
    for s, part in enumerate((l0[...], l1[...], l2[0], l2[1], l3[0], l3[1], l3[2], l3[3])):
        h, l = split(part[:, 0:64])
        l_ref[s] = rows(h, h, l)
    lh, ll = split(l0[...].T[0:64])
    left = lanes(lh, ll, lh)
    for f in range(16):
        ch, cl = split(f_ref[:, f, :])
        hh, hl = split(mm(left, rows(ch, ch, cl)))
        o_ref[:, f, :] = mm(lanes(hh, hl, hh), l_ref[cols_ref[f]])


def far(cols, coupling, lowers):
    return pl.pallas_call(
        far_kernel,
        out_shape=jax.ShapeDtypeStruct(coupling.shape, F32),
        in_specs=[SMEM] + [VMEM] * 5,
        out_specs=VMEM,
        scratch_shapes=[pltpu.VMEM((8, 192, 64), BF16)],
        compiler_params=params(6),
        cost_estimate=cost(3),
        name="far",
    )(cols, coupling, *lowers)


def shifted(value, axis, to):
    return lax.ppermute(value, axis, [(i, to(i)) for i in range(lax.axis_size(axis))])


def steps(
    basis_t, nested_transfer_matrices, leaf_coupling, leaf_columns, far_coupling, far_columns
):
    basis_t, nested_transfer_matrices, leaf_coupling = (
        pltpu.with_memory_space_constraint(x, pltpu.HBM)
        for x in (basis_t, nested_transfer_matrices, leaf_coupling)
    )
    both = ("wide", "narrow")
    wide_at = lax.axis_index("wide")
    at = lax.axis_index("narrow")
    gram, top, pay = climb(basis_t, nested_transfer_matrices)
    pay_a = shifted(pay, "narrow", lambda i: i ^ 1)
    low = leaf_chol(gram)
    pair = jnp.stack([pay, pay_a])
    pay_b = shifted(pair, "narrow", lambda i: i ^ 2)
    ends = lax.axis_size(both) - 1
    before = lax.ppermute(low, both, [(i, i + 1) for i in range(ends)])
    after = lax.ppermute(low, both, [(i + 1, i) for i in range(ends)])
    half_a = half_leaf(leaf_coupling, low, 0)
    quad = jnp.concatenate([pair, pay_b])
    pay_c = [shifted(quad, "narrow", lambda i, s=s: (i + 4 * s) % 16) for s in (1, 2, 3)]
    half_b = half_leaf(leaf_coupling, low, 1)
    ones = 1 + sum((at % 2**k == 2**k - 1).astype(jnp.int32) for k in range(1, 5))
    pick = jnp.where(ones <= 4, (16 + at) >> ones, 0)
    place = jnp.stack([at, pick]).astype(jnp.int32)
    group_factors, own = branch(place, [pay, pay_a, pay_b, *pay_c], top)
    own_a = shifted(own, "wide", lambda i: i ^ 1)
    factors = prep(before, low, after)
    two = jnp.stack([own, own_a])
    own_b = shifted(two, "wide", lambda i: i ^ 2)
    cols = leaf_columns - (lax.axis_index(both) * 64 - 64)
    out = full_leaf(cols, half_a, factors, 0)
    four = jnp.concatenate([two, own_b])
    own_c = shifted(four, "wide", lambda i: i ^ 4)
    leaf_coupled = full_leaf(cols, half_b, factors, 1, out)
    far_out = far(
        wide_at ^ far_columns,
        jnp.transpose(far_coupling, (0, 2, 1)),
        [own, own_a, own_b, own_c],
    )
    return leaf_coupled, jnp.transpose(far_out, (0, 2, 1)), group_factors


def solution(mesh):
    spread = P(None, None, ("wide", "narrow"))
    split_first = P(("wide", "narrow"), None, None)
    ids = P(("wide", "narrow"))
    return jax.shard_map(
        steps,
        mesh=mesh,
        in_specs=(split_first, spread, spread, ids, spread, ids),
        out_specs=(spread, spread, split_first),
        check_vma=False,
    )
```

profile of v0, /device:TPU:1, one launch (start us, length us, event | category | flops | bytes accessed | tf_op | source)
XLA Modules:
  0.0 136.0 jit_solution(15730363689743039996)
XLA Ops:
  0.6 26.8 %climb.1 = (f32[32,64,128]{2,1,0:T(8,128)S(1)}, f32[64,128]{1,0:T(8,128)S(1)}, f32[64,128]{1,0:T(8,128)S(1)}) custom-call(bf16[64,64,256]{2,1,0:T(8,128)(2,1)} %b_hbm.1, f32[64,64,128]{2,1,0:T(8,128)} %t_hbm.1), custom_call_target="tpu_custom_call" | custom-call | flops 11500000256 | bytes 4096 | tf_op jit(solution)/shard_map/climb/pallas_call | solution.py:147
  27.4 2.2 %collective-permute-start.2 = (f32[64,128]{1,0:T(8,128)S(1)}, f32[64,128]{1,0:T(8,128)S(1)}, u32[]{:S(2)}, u32[]{:S(2)}) collective-permute-start(f32[64,128]{1,0:T(8,128)S(1)} %get-tuple-element.9.p0), channel_id=1, source_target_pairs={{0,1},{1,0},{2,3},{3,2},{4,5},{5,4},{6,7},{7,6},{8,9},{9,8},{10,11... | collective-permute-start | bytes 98312 | tf_op jit(solution)/shard_map/ppermute | solution.py:479
  29.6 1.3 collective-permute-done.2.p1
  30.9 3.1 %collective-permute-start.3 = (f32[2,64,128]{2,1,0:T(8,128)S(1)}, f32[2,64,128]{2,1,0:T(8,128)S(1)}, u32[]{:S(2)}, u32[]{:S(2)}) collective-permute-start(f32[2,64,128]{2,1,0:T(8,128)S(1)} %pad_maximum_fusion.2), channel_id=1, source_target_pairs={{0,2},{1,3},{2,0},{3,1},{4,6},{5,7},{6,4},{7,5},{8,10},{9,11},{10,... | collective-permute-start | bytes 196616 | tf_op jit(solution)/shard_map/ppermute | solution.py:479
  34.0 7.7 %leaf_chol.1.low_ref.own_ref = f32[64,32,128]{2,1,0:T(8,128)S(1)} custom-call(f32[32,64,128]{2,1,0:T(8,128)S(1)} %get-tuple-element.8.g_ref), custom_call_target="tpu_custom_call" | custom-call | flops 6899999744 | bytes 4096 | tf_op jit(solution)/shard_map/leaf_chol/pallas_call | solution.py:233
  41.7 2.3 %collective-permute-start = (f32[64,32,128]{2,1,0:T(8,128)S(1)}, f32[64,32,128]{2,1,0:T(8,128)S(1)}, u32[]{:S(2)}, u32[]{:S(2)}) collective-permute-start(f32[64,32,128]{2,1,0:T(8,128)S(1)} %leaf_chol.1.low_ref.own_ref), channel_id=1, source_target_pairs={{0,1},{1,2},{2,3},{3,4},{4,5},{5,6},{6,7},{7,8},{8,9},{9,10},{10,1... | collective-permute-start | bytes 3145736 | tf_op jit(solution)/shard_map/ppermute | solution.py:498
  44.1 7.8 %collective-permute-start.1 = (f32[64,32,128]{2,1,0:T(8,128)S(1)}, f32[64,32,128]{2,1,0:T(8,128)S(1)}, u32[]{:S(2)}, u32[]{:S(2)}) collective-permute-start(f32[64,32,128]{2,1,0:T(8,128)S(1)} %leaf_chol.1.low_ref.own_ref), channel_id=1, source_target_pairs={{1,0},{2,1},{3,2},{4,3},{5,4},{6,5},{7,6},{8,7},{9,8},{10,9},{11,1... | collective-permute-start | bytes 3145736 | tf_op jit(solution)/shard_map/ppermute | solution.py:499
  51.8 0.0 collective-permute-done.3.p2
  51.8 0.7 pad_maximum_fusion
  52.5 0.0 collective-permute-start.4
  52.5 2.3 %collective-permute-start.5 = (f32[4,64,128]{2,1,0:T(8,128)}, f32[4,64,128]{2,1,0:T(8,128)}, u32[]{:S(2)}, u32[]{:S(2)}) collective-permute-start(f32[4,64,128]{2,1,0:T(8,128)} %pad_maximum_fusion), channel_id=1, source_target_pairs={{0,8},{1,9},{2,10},{3,11},{4,12},{5,13},{6,14},{7,15},{8,0},{9,1},... | collective-permute-start | bytes 393224 | tf_op jit(solution)/shard_map/ppermute | solution.py:479
  54.8 0.7 collective-permute-start.6
  55.5 9.6 %shard_map.85.y_ref = bf16[128,64,256]{2,1,0:T(8,128)(2,1)S(1)} custom-call(f32[64,64,512]{2,1,0:T(8,128)} %c1_ref.3, f32[64,64,512]{2,1,0:T(8,128)} %c1_ref.3, f32[64,32,128]{2,1,0:T(8,128)S(1)} %leaf_chol.1.low_ref.own_ref), custom_call_target="tpu_custom_call" | custom-call | flops 6899999744 | bytes 4096 | tf_op jit(solution)/shard_map/pallas_call | solution.py:273
  65.1 0.0 copy-start.1
  65.1 1.9 %copy-done.1 = bf16[128,64,256]{2,1,0:T(8,128)(2,1)} copy-done((bf16[128,64,256]{2,1,0:T(8,128)(2,1)}, bf16[128,64,256]{2,1,0:T(8,128)(2,1)S(1)}, u32[]{:S(2)}) %copy-start.1) | copy-done | bytes 4194328
  67.1 0.1 pad_add_fusion.at_ref
  67.1 6.0 %collective-permute-done.4.p3 = f32[4,64,128]{2,1,0:T(8,128)S(1)} collective-permute-done((f32[4,64,128]{2,1,0:T(8,128)}, f32[4,64,128]{2,1,0:T(8,128)S(1)}, u32[]{:S(2)}, u32[]{:S(2)}) %collective-permute-start.4) | collective-permute-done | bytes 131104 | tf_op jit(solution)/shard_map/ppermute | solution.py:479
  73.2 6.8 %collective-permute-done.5.p4 = f32[4,64,128]{2,1,0:T(8,128)} collective-permute-done((f32[4,64,128]{2,1,0:T(8,128)}, f32[4,64,128]{2,1,0:T(8,128)}, u32[]{:S(2)}, u32[]{:S(2)}) %collective-permute-start.5) | collective-permute-done | bytes 131104 | tf_op jit(solution)/shard_map/ppermute | solution.py:479
  80.0 0.0 collective-permute-done.6.p5
  80.0 8.2 %branch.1 = (f32[1,64,64]{2,1,0:T(8,128)}, f32[64,128]{1,0:T(8,128)S(1)}) custom-call(s32[2]{0:T(128)S(1)} %pad_add_fusion.at_ref, f32[64,128]{1,0:T(8,128)S(1)} %get-tuple-element.9.p0, f32[64,128]{1,0:T(8,128)S(1)} %collective-permute-done.2.p1, f32[2,64,128]{2,1,0:T(8,128)S(1)} %collective-permute-done.3.p2, f32[4,64,128]{2,1,0:T(8,128)S(1)} %collective-permute-done.4.p3, ...), custom_call_target="tpu_custom_call" | custom-call | flops 5750000128 | bytes 4096 | tf_op jit(solution)/shard_map/branch/pallas_call | solution.py:433
  88.2 0.0 copy-start.5
  88.2 0.0 copy-start.6
  88.2 0.5 collective-permute-start.7
  88.7 9.6 %shard_map.86.y_ref = bf16[128,64,256]{2,1,0:T(8,128)(2,1)S(1)} custom-call(f32[64,64,512]{2,1,0:T(8,128)} %c1_ref.3, f32[64,64,512]{2,1,0:T(8,128)} %c1_ref.3, f32[64,32,128]{2,1,0:T(8,128)S(1)} %leaf_chol.1.low_ref.own_ref), custom_call_target="tpu_custom_call" | custom-call | flops 6899999744 | bytes 4096 | tf_op jit(solution)/shard_map/pallas_call | solution.py:273
  98.3 0.0 copy-start.3
  98.3 2.0 %copy-done.3 = bf16[128,64,256]{2,1,0:T(8,128)(2,1)} copy-done((bf16[128,64,256]{2,1,0:T(8,128)(2,1)}, bf16[128,64,256]{2,1,0:T(8,128)(2,1)S(1)}, u32[]{:S(2)}) %copy-start.3) | copy-done | bytes 4194328
  100.4 0.0 collective-permute-done.7.l1
  100.4 1.3 collective-permute-start.8
  101.7 0.0 copy-done.5
  101.7 2.4 %collective-permute-done.8.l2 = f32[2,64,128]{2,1,0:T(8,128)S(1)} collective-permute-done((f32[2,64,128]{2,1,0:T(8,128)S(1)}, f32[2,64,128]{2,1,0:T(8,128)S(1)}, u32[]{:S(2)}, u32[]{:S(2)}) %collective-permute-start.8) | collective-permute-done | bytes 65568 | tf_op jit(solution)/shard_map/ppermute | solution.py:479
  104.1 2.8 %collective-permute-start.9 = (f32[4,64,128]{2,1,0:T(8,128)S(1)}, f32[4,64,128]{2,1,0:T(8,128)S(1)}, u32[]{:S(2)}, u32[]{:S(2)}) collective-permute-start(f32[4,64,128]{2,1,0:T(8,128)S(1)} %pad_maximum_fusion.1), channel_id=1, source_target_pairs={{0,64},{16,80},{32,96},{48,112},{64,0},{80,16},{96,32},{112,48},{1... | collective-permute-start | bytes 393224 | tf_op jit(solution)/shard_map/ppermute | solution.py:479
  106.9 0.0 copy-done.6
  106.9 2.9 %collective-permute-done.9.l3 = f32[4,64,128]{2,1,0:T(8,128)S(1)} collective-permute-done((f32[4,64,128]{2,1,0:T(8,128)S(1)}, f32[4,64,128]{2,1,0:T(8,128)S(1)}, u32[]{:S(2)}, u32[]{:S(2)}) %collective-permute-start.9) | collective-permute-done | bytes 131104 | tf_op jit(solution)/shard_map/ppermute | solution.py:479
  109.8 0.0 copy-start
  109.8 1.0 copy-done
  110.9 3.2 %far.1 = f32[64,16,64]{2,1,0:T(8,128)} custom-call(s32[16]{0:T(128)S(1)} %broadcast_xor_fusion.cols_ref, f32[64,16,64]{2,1,0:T(8,128)S(1)} %bitcast.16, f32[64,128]{1,0:T(8,128)S(1)} %get-tuple-element.11.l0, f32[64,128]{1,0:T(8,128)S(1)} %collective-permute-done.7.l1, f32[2,64,128]{2,1,0:T(8,128)S(1)} %collective-permute-done.8.l2, ...), custom_call_target="tpu_custom_call" | custom-call | flops 3449999872 | bytes 4096 | tf_op jit(solution)/shard_map/far/pallas_call | solution.py:466
  114.1 0.0 copy-start.4
  114.1 0.0 collective-permute-done.before_ref
  114.1 0.0 collective-permute-done.1.after_ref
  114.1 3.5 %prep.1.d_ref = bf16[192,64,256]{2,1,0:T(8,128)(2,1)S(1)} custom-call(f32[64,32,128]{2,1,0:T(8,128)S(1)} %collective-permute-done.before_ref, f32[64,32,128]{2,1,0:T(8,128)S(1)} %leaf_chol.1.low_ref.own_ref, f32[64,32,128]{2,1,0:T(8,128)S(1)} %collective-permute-done.1.after_ref), custom_call_target="tpu_custom_call" | custom-call | flops 3449999872 | bytes 4096 | tf_op jit(solution)/shard_map/prep/pallas_call | solution.py:304
  117.6 0.0 copy-done.4
  117.7 0.0 copy-start.2
  117.7 9.0 %shard_map.87.refs_0_ = f32[64,64,512]{2,1,0:T(8,128)} custom-call(s32[512]{0:T(512)S(1)} %broadcast_subtract_fusion.cols_ref, bf16[128,64,256]{2,1,0:T(8,128)(2,1)S(1)} %copy-done.4, bf16[192,64,256]{2,1,0:T(8,128)(2,1)S(1)} %prep.1.d_ref), custom_call_target="tpu_custom_call" | custom-call | flops 9200000000 | bytes 4096 | tf_op jit(solution)/shard_map/pallas_call | solution.py:364
  126.7 0.0 copy-done.2
  126.7 9.1 %shard_map.88 = f32[64,64,512]{2,1,0:T(8,128)} custom-call(s32[512]{0:T(512)S(1)} %broadcast_subtract_fusion.cols_ref, bf16[128,64,256]{2,1,0:T(8,128)(2,1)S(1)} %copy-done.2, bf16[192,64,256]{2,1,0:T(8,128)(2,1)S(1)} %prep.1.d_ref, f32[64,64,512]{2,1,0:T(8,128)} %shard_map.87.refs_0_), custom_call_target="tpu_custom_call", output_to_operand_aliasing={{}: (3, {})} | custom-call | flops 9200000000 | bytes 4096 | tf_op jit(solution)/shard_map/pallas_call | solution.py:364
  (5 shorter events, 0.0 us)
Async XLA Ops:
  27.4 3.5 %collective-permute-start.2 = (f32[64,128]{1,0:T(8,128)S(1)}, f32[64,128]{1,0:T(8,128)S(1)}, u32[]{:S(2)}, u32[]{:S(2)}) collective-permute-start(f32[64,128]{1,0:T(8,128)S(1)} %get-tuple-element.9.p0), channel_id=1, source_target_pairs={{0,1},{1,0},{2,3},{3,2},{4,5},{5,4},{6,7},{7,6},{8,9},{9,8},{10,11... | collective-permute-start | bytes 98312 | tf_op jit(solution)/shard_map/ppermute | solution.py:479
  30.9 20.9 %collective-permute-start.3 = (f32[2,64,128]{2,1,0:T(8,128)S(1)}, f32[2,64,128]{2,1,0:T(8,128)S(1)}, u32[]{:S(2)}, u32[]{:S(2)}) collective-permute-start(f32[2,64,128]{2,1,0:T(8,128)S(1)} %pad_maximum_fusion.2), channel_id=1, source_target_pairs={{0,2},{1,3},{2,0},{3,1},{4,6},{5,7},{6,4},{7,5},{8,10},{9,11},{10,... | collective-permute-start | bytes 196616 | tf_op jit(solution)/shard_map/ppermute | solution.py:479
  41.7 72.4 %collective-permute-start = (f32[64,32,128]{2,1,0:T(8,128)S(1)}, f32[64,32,128]{2,1,0:T(8,128)S(1)}, u32[]{:S(2)}, u32[]{:S(2)}) collective-permute-start(f32[64,32,128]{2,1,0:T(8,128)S(1)} %leaf_chol.1.low_ref.own_ref), channel_id=1, source_target_pairs={{0,1},{1,2},{2,3},{3,4},{4,5},{5,6},{6,7},{7,8},{8,9},{9,10},{10,1... | collective-permute-start | bytes 3145736 | tf_op jit(solution)/shard_map/ppermute | solution.py:498
  44.1 70.1 %collective-permute-start.1 = (f32[64,32,128]{2,1,0:T(8,128)S(1)}, f32[64,32,128]{2,1,0:T(8,128)S(1)}, u32[]{:S(2)}, u32[]{:S(2)}) collective-permute-start(f32[64,32,128]{2,1,0:T(8,128)S(1)} %leaf_chol.1.low_ref.own_ref), channel_id=1, source_target_pairs={{1,0},{2,1},{3,2},{4,3},{5,4},{6,5},{7,6},{8,7},{9,8},{10,9},{11,1... | collective-permute-start | bytes 3145736 | tf_op jit(solution)/shard_map/ppermute | solution.py:499
  52.5 20.7 %collective-permute-start.4 = (f32[4,64,128]{2,1,0:T(8,128)}, f32[4,64,128]{2,1,0:T(8,128)S(1)}, u32[]{:S(2)}, u32[]{:S(2)}) collective-permute-start(f32[4,64,128]{2,1,0:T(8,128)} %pad_maximum_fusion), channel_id=1, source_target_pairs={{0,4},{1,5},{2,6},{3,7},{4,8},{5,9},{6,10},{7,11},{8,12},{9,13},{1... | collective-permute-start | bytes 393224 | tf_op jit(solution)/shard_map/ppermute | solution.py:479
  52.5 27.5 %collective-permute-start.5 = (f32[4,64,128]{2,1,0:T(8,128)}, f32[4,64,128]{2,1,0:T(8,128)}, u32[]{:S(2)}, u32[]{:S(2)}) collective-permute-start(f32[4,64,128]{2,1,0:T(8,128)} %pad_maximum_fusion), channel_id=1, source_target_pairs={{0,8},{1,9},{2,10},{3,11},{4,12},{5,13},{6,14},{7,15},{8,0},{9,1},... | collective-permute-start | bytes 393224 | tf_op jit(solution)/shard_map/ppermute | solution.py:479
  54.8 25.3 %collective-permute-start.6 = (f32[4,64,128]{2,1,0:T(8,128)}, f32[4,64,128]{2,1,0:T(8,128)}, u32[]{:S(2)}, u32[]{:S(2)}) collective-permute-start(f32[4,64,128]{2,1,0:T(8,128)} %pad_maximum_fusion), channel_id=1, source_target_pairs={{0,12},{1,13},{2,14},{3,15},{4,0},{5,1},{6,2},{7,3},{8,4},{9,5},{1... | collective-permute-start | bytes 393224 | tf_op jit(solution)/shard_map/ppermute | solution.py:479
  65.1 2.0 %copy-start.1 = (bf16[128,64,256]{2,1,0:T(8,128)(2,1)}, bf16[128,64,256]{2,1,0:T(8,128)(2,1)S(1)}, u32[]{:S(2)}) copy-start(bf16[128,64,256]{2,1,0:T(8,128)(2,1)S(1)} %shard_map.85.y_ref) | copy-start | bytes 12582916
  88.2 13.4 %copy-start.5 = (s32[512]{0:T(512)S(1)}, s32[512]{0:T(512)}, u32[]{:S(2)}) copy-start(s32[512]{0:T(512)} %param.9) | copy-start | bytes 6148
  88.2 18.7 %copy-start.6 = (s32[16]{0:T(128)S(1)}, s32[16]{0:T(128)}, u32[]{:S(2)}) copy-start(s32[16]{0:T(128)} %param.11) | copy-start | bytes 196
  88.2 12.1 %collective-permute-start.7 = (f32[64,128]{1,0:T(8,128)S(1)}, f32[64,128]{1,0:T(8,128)S(1)}, u32[]{:S(2)}, u32[]{:S(2)}) collective-permute-start(f32[64,128]{1,0:T(8,128)S(1)} %get-tuple-element.11.l0), channel_id=1, source_target_pairs={{0,16},{16,0},{32,48},{48,32},{64,80},{80,64},{96,112},{112,96},{1... | collective-permute-start | bytes 98312 | tf_op jit(solution)/shard_map/ppermute | solution.py:479
  98.3 2.0 %copy-start.3 = (bf16[128,64,256]{2,1,0:T(8,128)(2,1)}, bf16[128,64,256]{2,1,0:T(8,128)(2,1)S(1)}, u32[]{:S(2)}) copy-start(bf16[128,64,256]{2,1,0:T(8,128)(2,1)S(1)} %shard_map.86.y_ref) | copy-start | bytes 12582916
  100.4 3.7 %collective-permute-start.8 = (f32[2,64,128]{2,1,0:T(8,128)S(1)}, f32[2,64,128]{2,1,0:T(8,128)S(1)}, u32[]{:S(2)}, u32[]{:S(2)}) collective-permute-start(f32[2,64,128]{2,1,0:T(8,128)S(1)} %pad_maximum_fusion.3), channel_id=1, source_target_pairs={{0,32},{16,48},{32,0},{48,16},{64,96},{80,112},{96,64},{112,80},{1... | collective-permute-start | bytes 196616 | tf_op jit(solution)/shard_map/ppermute | solution.py:479
  104.1 5.8 %collective-permute-start.9 = (f32[4,64,128]{2,1,0:T(8,128)S(1)}, f32[4,64,128]{2,1,0:T(8,128)S(1)}, u32[]{:S(2)}, u32[]{:S(2)}) collective-permute-start(f32[4,64,128]{2,1,0:T(8,128)S(1)} %pad_maximum_fusion.1), channel_id=1, source_target_pairs={{0,64},{16,80},{32,96},{48,112},{64,0},{80,16},{96,32},{112,48},{1... | collective-permute-start | bytes 393224 | tf_op jit(solution)/shard_map/ppermute | solution.py:479
  109.8 1.0 copy-start
  114.1 3.5 %copy-start.4 = (bf16[128,64,256]{2,1,0:T(8,128)(2,1)S(1)}, bf16[128,64,256]{2,1,0:T(8,128)(2,1)}, u32[]{:S(2)}) copy-start(bf16[128,64,256]{2,1,0:T(8,128)(2,1)} %copy-done.3) | copy-start | bytes 12582916
  117.7 9.1 %copy-start.2 = (bf16[128,64,256]{2,1,0:T(8,128)(2,1)S(1)}, bf16[128,64,256]{2,1,0:T(8,128)(2,1)}, u32[]{:S(2)}) copy-start(bf16[128,64,256]{2,1,0:T(8,128)(2,1)} %copy-done.1) | copy-start | bytes 12582916
where the time goes:
time: 138 us; the launch traced here: 136 us
  Pallas kernels  86.8 us (63%)
  starting transfers between devices  22.9 us (17%)
  waiting for transfers between devices  19.5 us (14%)
  local copies, waits for them, and re-layouts  5.02 us (4%)
    pallas_call x1, Pallas kernels, climb(): pl.pallas_call(climb_kernel, out_shape=(jax.ShapeDtypeStruct((32, 64, 128...  26.8 us
    ppermute x8, waiting for transfers between devices, shifted(): lax.ppermute(value, axis, [(i, to(i)) for i in range(lax.axis_size(axis))])  19.5 us
    pallas_call x2, Pallas kernels, half_leaf(): pl.pallas_call(functools.partial(half_kernel, part=part), out_shape=jax.S...  19.2 us
    pallas_call x2, Pallas kernels, full_leaf(): pl.pallas_call(functools.partial(full_kernel, part=part, mode=mode), out_...  18.2 us
    ppermute x8, starting transfers between devices, shifted(): lax.ppermute(value, axis, [(i, to(i)) for i in range(lax.axis_size(axis))])  12.9 us
    pallas_call x1, Pallas kernels, branch(): pl.pallas_call(branch_kernel, out_shape=(jax.ShapeDtypeStruct((1, 64, 64)...  8.19 us
    ppermute x1, starting transfers between devices, steps(): after = lax.ppermute(low, both, [(i + 1, i) for i in range(ends)])  7.76 us
    pallas_call x1, Pallas kernels, leaf_chol(): pl.pallas_call(leaf_chol_kernel, out_shape=jax.ShapeDtypeStruct((64, 32,...  7.72 us
  transfers between devices with their start and end apart: 10, of which 5 were waited for; matrix products, arithmetic and copies ran while one was open for 1% of the time, Pallas kernels for 28%

commit v1 on v0

--- a/solution.py
+++ b/solution.py
@@ -52,9 +52,13 @@
     return lax.broadcasted_iota(jnp.int32, shape, 1) % 128 < 64
 
 
+def mixed(m):
+    h = m.astype(BF16).astype(F32)
+    return jnp.where(first_half(m.shape), h, m - h).astype(BF16)
+
+
 def left_of(m):
-    h, l = split(m)
-    v = jnp.where(first_half(), h, l)
+    v = mixed(m)
     return lanes(v, v)
 
 
@@ -66,7 +70,14 @@
     return rows(m, m)
 
 
-def climb_kernel(b_hbm, t_hbm, g_ref, top_ref, pay_ref, b_ref, t_ref, e_ref, v_ref, sem):
+LEAVES = 16
+HALF = 4
+PAIRS = 32
+
+
+def climb_kernel(
+    b_hbm, t_hbm, g_ref, top_ref, pay_ref, b_ref, t_ref, u_ref, e_ref, w_ref, sem
+):
     t_copies = [
         pltpu.make_async_copy(
             t_hbm.at[pl.ds(16 * n, 16)], t_ref.at[pl.ds(16 * n, 16)], sem.at[n]
@@ -83,64 +94,72 @@
         copy.start()
     first = first_half()
 
-    def turn(k, _):
-        x = t_ref[k]
-        e_ref[k] = rows(x, x).T
+    def turn(s, _):
+        for r in range(8):
+            x = t_ref[s * 8 + r]
+            u_ref[r] = rows(x, x).T
+        for g in range(16):
+            x = u_ref[:, 8 * g : 8 * g + 8, :]
+            e_ref[8 * g : 8 * g + 8, pl.ds(pl.multiple_of(s * 8, 8), 8), :] = jnp.swapaxes(x, 0, 1)
         return 0
 
     for n in range(4):
         t_copies[n].wait()
-        lax.fori_loop(16 * n, 16 * n + 16, turn, 0, unroll=8)
+        lax.fori_loop(2 * n, 2 * n + 2, turn, 0)
 
     row = lax.broadcasted_iota(jnp.int32, (64, 128), 0)
     col = lax.broadcasted_iota(jnp.int32, (64, 128), 1)
-    eye = (row == col).astype(F32)
-    v_ref[1, :, 0:128] = lanes(eye[:, 0:64], eye[:, 0:64]).astype(BF16)
-    v_ref[1, :, 128:256] = jnp.zeros((64, 128), BF16)
-
-    def down(p, _):
-        v = jnp.where(first, v_ref[p, :, 0:128], v_ref[p, :, 128:256])
-        r0 = right_of(e_ref[:, 2 * p, :])
-        r1 = right_of(e_ref[:, 2 * p + 1, :])
-        z = mm_nt(lanes(v, v), rows(r0, r0, r1, r1))
-        for c in range(2):
-            v_ref[2 * p + c] = right_of(z[:, 128 * c : 128 * c + 128])
-        return 0
-
-    for level in range(6):
+    w_ref[1, 0:64] = (row == col % 64).astype(BF16)
+    w_ref[1, 64:128] = jnp.zeros((64, 128), BF16)
+
+    def right_rows(h):
+        w = w_ref[h]
+        return rows(w[0:64], w[0:64], w[64:128], w[64:128])
+
+    def down(clusters):
+        zs = [
+            mm(rows(left_of(e_ref[2 * p]), left_of(e_ref[2 * p + 1])), right_rows(p))
+            for p in clusters
+        ]
+        for p, z in zip(clusters, zs):
+            for c in range(2):
+                w_ref[2 * p + c] = rows(*split(z[64 * c : 64 * c + 64]))
+
+    def downs(s, _):
+        down([s * 8 + j for j in range(8)])
+        return 0
+
+    for level in range(3):
+        down(range(2**level, 2 ** (level + 1)))
+    for level in range(3, 6):
         n = 2**level
-        lax.fori_loop(n, 2 * n, down, 0, unroll=min(8, n))
+        lax.fori_loop(n // 8, n // 4, downs, 0)
     for copy in b_copies:
         copy.wait()
 
-    def leaf(q, acc):
-        grams, prods, vs = [], [], []
-        for c in range(2):
-            t = q + 32 * c
-            b = b_ref[t]
-            g = mm_nt(b, twice(b))
-            grams.append(g)
-            v = v_ref[64 + t]
-            vs.append(v)
-            vv = jnp.where(first, v[:, 0:128], v[:, 128:256])
-            prods.append(mm_nt(lanes(vv, vv), twice(right_of(g))))
-        g_ref[q] = jnp.where(first, grams[0], grams[1])
-        ph, pl_ = split(jnp.where(first, prods[0], prods[1]))
-        vh = jnp.where(first, vs[0][:, 0:128], vs[1][:, 0:128])
-        vl = jnp.where(first, vs[0][:, 128:256], vs[1][:, 128:256])
-        right = lanes(vh, vh, vl)
-        return acc + mm_nt(lanes(ph, pl_, ph), twice(right))
-
-    top = lax.fori_loop(0, 32, leaf, jnp.zeros((64, 128), F32), unroll=8)
+    def leaves(s, acc):
+        count = LEAVES // 2
+        qs = [s * count + j for j in range(count)]
+        ts = qs + [q + 32 for q in qs]
+        bs = [b_ref[t] for t in ts]
+        grams = [mm_nt(b, twice(b)) for b in bs]
+        for j, q in enumerate(qs):
+            g_ref[q] = jnp.where(first, grams[j], grams[count + j])
+        prods = [mm(left_of(g), right_rows(64 + t)) for g, t in zip(grams, ts)]
+        for p, t in zip(prods, ts):
+            ph, pl_ = split(p)
+            w = w_ref[64 + t][:, 0:64]
+            acc = acc + mm_tn(rows(w, w), rows(ph, ph, pl_, pl_))
+        return acc
+
+    top = lax.fori_loop(0, 64 // LEAVES, leaves, jnp.zeros((64, 128), F32))
     top_ref[...] = top
-    e = e_ref[:, 1, :]
-    v = mm_nt(lanes(eye, eye).astype(BF16)[:, 0:128], twice(split(e)[0])) + mm_nt(
-        eye.astype(BF16), twice(split(e)[1])
-    )
-    prod = mm_nt(left_of(v), twice(right_of(top)))
-    vh, vl = split(v)
-    term = mm_nt(left_of(prod), twice(lanes(vh, vl)))
-    pay_ref[...] = jnp.where(first, term, e_ref[:, 0, :])
+    h, l = split(e_ref[1])
+    prod = mm(left_of(top), rows(h, h, l, l))
+    ph, pl_ = split(prod)
+    up = rows(h, l).T[0:64]
+    term = mm(lanes(up, up), rows(ph, ph, pl_, pl_))
+    pay_ref[...] = jnp.where(first, term, e_ref[0])
 
 
 def climb(basis, transfers):
@@ -156,8 +175,9 @@
         scratch_shapes=[
             pltpu.VMEM((64, 64, 256), BF16),
             pltpu.VMEM((64, 64, 128), F32),
-            pltpu.VMEM((64, 128, 128), F32),
-            pltpu.VMEM((128, 64, 256), BF16),
+            pltpu.VMEM((8, 128, 128), F32),
+            pltpu.VMEM((128, 64, 128), F32),
+            pltpu.VMEM((128, 128, 128), BF16),
             pltpu.SemaphoreType.DMA((6,)),
         ],
         compiler_params=params(20),
@@ -211,62 +231,84 @@
                 a_ref[base + j, it * 8 : it * 8 + 8, :] = v[j]
 
 
-def leaf_chol_kernel(g_ref, low_ref, a_ref):
-    def load(k, _):
-        x = g_ref[:, k, :]
-        y = pltpu.roll(x, 64, 1)
-        a_ref[k] = rows(x, y, x, y).T[0:64]
-        return 0
-
-    lax.fori_loop(0, 64, load, 0, unroll=8)
+def leaf_chol_kernel(g_ref, low_ref, a_ref, u_ref):
+    def load(s, _):
+        at = pl.ds(pl.multiple_of(s * 8, 8), 8)
+        for g in range(4):
+            u_ref[:, 8 * g : 8 * g + 8, :] = jnp.swapaxes(g_ref[8 * g : 8 * g + 8, at, :], 0, 1)
+        for r in range(8):
+            x = u_ref[r, 0:32, :]
+            y = pltpu.roll(x, 64, 1)
+            a_ref[s * 8 + r] = rows(x, y, x, y).T[0:64]
+        return 0
+
+    lax.fori_loop(0, 8, load, 0)
     chol_lanes(a_ref)
 
-    def store(i, _):
-        x = a_ref[:, i, :]
-        low_ref[i] = rows(x, pltpu.roll(x, 96, 1)).T[0:32]
-        return 0
-
-    lax.fori_loop(0, 64, store, 0, unroll=8)
+    def store(s, _):
+        at = pl.ds(pl.multiple_of(s * 8, 8), 8)
+        for g in range(8):
+            u_ref[:, 8 * g : 8 * g + 8, :] = jnp.swapaxes(a_ref[8 * g : 8 * g + 8, at, :], 0, 1)
+        for r in range(8):
+            x = u_ref[r]
+            u_ref[r, 0:32, :] = rows(x, pltpu.roll(x, 96, 1)).T[0:32]
+        for g in range(4):
+            low_ref[8 * g : 8 * g + 8, at, :] = jnp.swapaxes(u_ref[:, 8 * g : 8 * g + 8, :], 0, 1)
+        return 0
+
+    lax.fori_loop(0, 8, store, 0)
 
 
 def leaf_chol(gram):
     return pl.pallas_call(
         leaf_chol_kernel,
-        out_shape=jax.ShapeDtypeStruct((64, 32, 128), F32),
+        out_shape=jax.ShapeDtypeStruct((32, 64, 128), F32),
         in_specs=[VMEM],
         out_specs=VMEM,
-        scratch_shapes=[pltpu.VMEM((64, 64, 128), F32)],
+        scratch_shapes=[pltpu.VMEM((64, 64, 128), F32), pltpu.VMEM((8, 64, 128), F32)],
         compiler_params=params(8),
         cost_estimate=cost(6),
         name="leaf_chol",
     )(gram)
 
 
-def half_kernel(c0_ref, c1_ref, low_ref, y_ref, s_ref, part):
+def half_kernel(c0_ref, c1_ref, low_ref, y_ref, s_ref, u_ref, part):
     step = pl.program_id(0)
 
-    def turn(k, _):
-        s_ref[step * 16 + k] = rows(c0_ref[k], c1_ref[k]).T
-        return 0
-
-    lax.fori_loop(0, 16, turn, 0, unroll=8)
+    def turn(s, _):
+        for r in range(8):
+            u_ref[r] = rows(c0_ref[s * 8 + r], c1_ref[s * 8 + r]).T
+        at = pl.ds(pl.multiple_of(step * 16 + s * 8, 8), 8)
+        for g in range(16):
+            s_ref[8 * g : 8 * g + 8, at, :] = jnp.swapaxes(u_ref[:, 8 * g : 8 * g + 8, :], 0, 1)
+        return 0
+
+    lax.fori_loop(0, 2, turn, 0)
 
     @pl.when(step == 3)
     def _():
-        first = first_half((64, 1024))
-
-        def leaf(t, _):
-            w = lanes(*[s_ref[:, t * 8 + n, :] for n in range(8)])
-            wh, wl = split(w)
-            lh, ll = split(low_ref[:, 16 * part + t, :])
-            z = mm_tn(rows(lh, ll, lh), rows(wh, wh, wl))
-            yh, yl = split(jnp.where(first, z[0:64], z[64:128]))
-            for n in range(8):
-                y_ref[t * 8 + n, :, 0:128] = yh[:, n * 128 : n * 128 + 128]
-                y_ref[t * 8 + n, :, 128:256] = yl[:, n * 128 : n * 128 + 128]
+        first = first_half((64, 256))
+
+        def leaf(s, _):
+            ts = [s * HALF + j for j in range(HALF)]
+            lefts = []
+            for t in ts:
+                lh, ll = split(low_ref[16 * part + t])
+                lefts.append(rows(lh, ll, lh).T)
+            at = [(j, n) for j in range(HALF) for n in range(0, 8, 2)]
+            zs = []
+            for j, n in at:
+                wh, wl = split(lanes(s_ref[ts[j] * 8 + n], s_ref[ts[j] * 8 + n + 1]))
+                zs.append(mm(lefts[j], rows(wh, wh, wl)))
+            for (j, n), z in zip(at, zs):
+                yh, yl = split(jnp.where(first, z[0:64], z[64:128]))
+                for m in range(2):
+                    b = ts[j] * 8 + n + m
+                    y_ref[b, :, 0:128] = yh[:, m * 128 : m * 128 + 128]
+                    y_ref[b, :, 128:256] = yl[:, m * 128 : m * 128 + 128]
             return 0
 
-        lax.fori_loop(0, 16, leaf, 0, unroll=2)
+        lax.fori_loop(0, 16 // HALF, leaf, 0)
 
 
 def half_leaf(coupling, low, part):
@@ -277,10 +319,10 @@
         in_specs=[
             pl.BlockSpec((16, 64, 128), lambda s: (s, 0, part)),
             pl.BlockSpec((16, 64, 128), lambda s: (s, 0, part + 2)),
-            pl.BlockSpec((64, 32, 128), lambda s: (0, 0, 0)),
+            pl.BlockSpec((32, 64, 128), lambda s: (0, 0, 0)),
         ],
         out_specs=pl.BlockSpec((128, 64, 256), lambda s: (0, 0, 0)),
-        scratch_shapes=[pltpu.VMEM((64, 128, 128), F32)],
+        scratch_shapes=[pltpu.VMEM((128, 64, 128), F32), pltpu.VMEM((8, 128, 128), F32)],
         compiler_params=params(22),
         cost_estimate=cost(6),
     )(coupling, coupling, low)
@@ -291,7 +333,7 @@
     for group, ref in enumerate((before_ref, own_ref, after_ref)):
 
         def pair(q, _, ref=ref, group=group):
-            x = ref[:, q, :]
+            x = ref[q]
             y = pltpu.roll(x, 64, 1)
             d_ref[group * 64 + q] = right_of(jnp.where(first, x, y))
             d_ref[group * 64 + 32 + q] = right_of(jnp.where(first, y, x))
@@ -312,27 +354,26 @@
     )(before, own, after)
 
 
-def full_kernel(cols_ref, y_ref, d_ref, *refs, part, mode):
-    out_ref, s_ref, o_ref, sem = refs[-4:]
+def full_kernel(cols_ref, y_ref, d_ref, *refs, part):
+    out_ref, s_ref, u_ref, o_ref, sem = refs[-5:]
     lane = lax.broadcasted_iota(jnp.int32, (64, 256), 1)
     keep = ((lane % 128) < 64).astype(BF16)
     drop = ((lane % 128) >= 64).astype(BF16)
-    zero = jnp.zeros((128, 128), BF16)
-
-    def pair(p, _):
-        sa = cols_ref[part * 128 + p]
-        sb = cols_ref[part * 128 + 256 + p]
-        r = rows(d_ref[sa] * keep, d_ref[sb] * drop)
-        y = y_ref[p]
-        if mode == 0:
-            z = mm(y, rows(r, lanes(r[:, 0:128], zero)))
-            s_ref[p] = z[:, 0:128] + z[:, 128:256]
-        else:
-            z = mm(rows(y[:, 0:128], y[:, 128:256]), r)
+
+    def pair(s, _):
+        ps = [s * PAIRS + j for j in range(PAIRS)]
+        zs = []
+        for p in ps:
+            sa = cols_ref[part * 128 + p]
+            sb = cols_ref[part * 128 + 256 + p]
+            r = rows(d_ref[sa] * keep, d_ref[sb] * drop)
+            y = y_ref[p]
+            zs.append(mm(rows(y[:, 0:128], y[:, 128:256]), r))
+        for p, z in zip(ps, zs):
             s_ref[p] = z[0:64, 0:128] + z[0:64, 128:256] + z[64:128, 0:128]
         return 0
 
-    lax.fori_loop(0, 128, pair, 0, unroll=8)
+    lax.fori_loop(0, 128 // PAIRS, pair, 0)
 
     def send(n):
         return [
@@ -344,14 +385,18 @@
             for c in range(2)
         ]
 
-    def turn(i, _):
-        x = s_ref[:, i, :].T
-        o_ref[0, i] = x[0:64]
-        o_ref[1, i] = x[64:128]
+    def turn(s, _):
+        at = pl.ds(pl.multiple_of(s * 8, 8), 8)
+        for g in range(16):
+            u_ref[:, 8 * g : 8 * g + 8, :] = jnp.swapaxes(s_ref[8 * g : 8 * g + 8, at, :], 0, 1)
+        for r in range(8):
+            x = u_ref[r].T
+            o_ref[0, s * 8 + r] = x[0:64]
+            o_ref[1, s * 8 + r] = x[64:128]
         return 0
 
     for n in range(4):
-        lax.fori_loop(16 * n, 16 * n + 16, turn, 0, unroll=8)
+        lax.fori_loop(2 * n, 2 * n + 2, turn, 0)
         for copy in send(n):
             copy.start()
     for n in range(4):
@@ -359,15 +404,16 @@
             copy.wait()
 
 
-def full_leaf(cols, y, d, part, into=None, mode=1):
+def full_leaf(cols, y, d, part, into=None):
     extra = [] if into is None else [into]
     return pl.pallas_call(
-        functools.partial(full_kernel, part=part, mode=mode),
+        functools.partial(full_kernel, part=part),
         out_shape=jax.ShapeDtypeStruct((64, 64, 512), F32),
         in_specs=[SMEM, VMEM, VMEM] + [pl.BlockSpec(memory_space=pltpu.HBM)] * len(extra),
         out_specs=pl.BlockSpec(memory_space=pltpu.HBM),
         scratch_shapes=[
             pltpu.VMEM((128, 64, 128), F32),
+            pltpu.VMEM((8, 128, 128), F32),
             pltpu.VMEM((2, 64, 64, 128), F32),
             pltpu.SemaphoreType.DMA((4, 2)),
         ],
@@ -395,21 +441,25 @@
         for i in range(4):
             place((at ^ i) - 4 * (s + 1) & 15, ref[i])
     n_ref[0] = top_ref[...]
-    row = lax.broadcasted_iota(jnp.int32, (64, 64), 0)
-    col = lax.broadcasted_iota(jnp.int32, (64, 64), 1)
-    eye = (row == col).astype(BF16)
-    eye = lanes(eye, eye)
-
-    def term(p):
-        v = mm_nt(eye, twice(jnp.where(first, *split(e_ref[p]))))
-        prod = mm_nt(left_of(v), twice(right_of(n_ref[p])))
-        return mm_nt(left_of(prod), twice(right_of(v)))
-
     for m in range(8):
         n_ref[8 + m] = t_ref[2 * m] + t_ref[2 * m + 1]
+    ups = {}
+    for p in range(2, 16):
+        h, l = split(e_ref[p])
+        ups[p] = rows(h, l).T[0:64]
     for level in (2, 1, 0):
-        for p in range(2**level, 2 ** (level + 1)):
-            n_ref[p] = term(2 * p) + term(2 * p + 1)
+        parents = range(2**level, 2 ** (level + 1))
+        children = [c for p in parents for c in (2 * p, 2 * p + 1)]
+        prods = []
+        for c in children:
+            h, l = split(e_ref[c])
+            prods.append(mm(left_of(n_ref[c]), rows(h, h, l, l)))
+        terms = []
+        for c, prod in zip(children, prods):
+            h, l = split(prod)
+            terms.append(mm(lanes(ups[c], ups[c]), rows(h, h, l, l)))
+        for n, p in enumerate(parents):
+            n_ref[p] = terms[2 * n] + terms[2 * n + 1]
 
     both = jnp.where(first, n_ref[pick], n_ref[1])
     lane = lax.broadcasted_iota(jnp.int32, (64, 128), 1)
@@ -450,16 +500,30 @@
     )(at, *parts, top)
 
 
-def far_kernel(cols_ref, f_ref, l0, l1, l2, l3, o_ref, l_ref):
+def far_kernel(cols_ref, f_ref, l0, l1, l2, l3, o_ref, l_ref, c_ref):
     for s, part in enumerate((l0[...], l1[...], l2[0], l2[1], l3[0], l3[1], l3[2], l3[3])):
         h, l = split(part[:, 0:64])
         l_ref[s] = rows(h, h, l)
     lh, ll = split(l0[...].T[0:64])
     left = lanes(lh, ll, lh)
+    halves = []
+    for g in range(2):
+        for s in range(8):
+            x = f_ref[8 * s : 8 * s + 8, 8 * g : 8 * g + 8, :]
+            c_ref[8 * g : 8 * g + 8, 8 * s : 8 * s + 8, :] = jnp.swapaxes(x, 0, 1)
+        for f in range(8 * g, 8 * g + 8):
+            ch, cl = split(c_ref[f])
+            halves.append(mm(left, rows(ch, ch, cl)))
+    outs = []
     for f in range(16):
-        ch, cl = split(f_ref[:, f, :])
-        hh, hl = split(mm(left, rows(ch, ch, cl)))
-        o_ref[:, f, :] = mm(lanes(hh, hl, hh), l_ref[cols_ref[f]])
+        hh, hl = split(halves[f])
+        outs.append(mm(lanes(hh, hl, hh), l_ref[cols_ref[f]]))
+    for f in range(16):
+        c_ref[f] = outs[f]
+    for g in range(2):
+        for s in range(8):
+            x = c_ref[8 * g : 8 * g + 8, 8 * s : 8 * s + 8, :]
+            o_ref[8 * s : 8 * s + 8, 8 * g : 8 * g + 8, :] = jnp.swapaxes(x, 0, 1)
 
 
 def far(cols, coupling, lowers):
@@ -468,7 +532,7 @@
         out_shape=jax.ShapeDtypeStruct(coupling.shape, F32),
         in_specs=[SMEM] + [VMEM] * 5,
         out_specs=VMEM,
-        scratch_shapes=[pltpu.VMEM((8, 192, 64), BF16)],
+        scratch_shapes=[pltpu.VMEM((8, 192, 64), BF16), pltpu.VMEM((16, 64, 64), F32)],
         compiler_params=params(6),
         cost_estimate=cost(3),
         name="far",

time: 138 us -> 108 us (0.78)
  Pallas kernels: 86.8 us -> 52.9 us
  waiting for transfers between devices: 19.5 us -> 22.9 us
    pallas_call x1, Pallas kernels: 26.8 us -> 9.22 us  [climb(): pl.pallas_call(climb_kernel, out_shape=(jax.ShapeDtypeStruct((32, 64, 128...]
    pallas_call x2, Pallas kernels: 19.2 us -> 12.5 us  [half_leaf(): pl.pallas_call(functools.partial(half_kernel, part=part), out_shape=jax.S...]
    pallas_call x3, Pallas kernels: 25.9 us -> 20.4 us  [the longest x2 13.2 us: full_leaf(): pl.pallas_call(functools.partial(full_kernel, part=part), out_shape=jax.S...]
    ppermute x8, waiting for transfers between devices: 19.5 us -> 22.9 us  [shifted(): lax.ppermute(value, axis, [(i, to(i)) for i in range(lax.axis_size(axis))])]
    pallas_call x1, Pallas kernels: 3.51 us -> 1.86 us  [prep(): pl.pallas_call(prep_kernel, out_shape=jax.ShapeDtypeStruct((192, 64, 256)...]
    pallas_call x1, Pallas kernels: 8.19 us -> 6.8 us  [branch(): pl.pallas_call(branch_kernel, out_shape=(jax.ShapeDtypeStruct((1, 64, 64)...]
  transfers between devices with their start and end apart: 10 -> 10, of which waited for: 5 -> 5; matrix products, arithmetic and copies ran while one was open for 1% -> 1% of each run, Pallas kernels for 28% -> 27%
where the time goes in v1:
time: 108 us; the launch traced here: 106 us
  Pallas kernels  52.9 us (49%)
  starting transfers between devices  23.1 us (21%)
  waiting for transfers between devices  22.9 us (21%)
  local copies, waits for them, and re-layouts  5.32 us (5%)
    ppermute x8, waiting for transfers between devices, shifted(): lax.ppermute(value, axis, [(i, to(i)) for i in range(lax.axis_size(axis))])  22.9 us
    pallas_call x2, Pallas kernels, full_leaf(): pl.pallas_call(functools.partial(full_kernel, part=part), out_shape=jax.S...  13.2 us
    ppermute x8, starting transfers between devices, shifted(): lax.ppermute(value, axis, [(i, to(i)) for i in range(lax.axis_size(axis))])  13.1 us
    pallas_call x2, Pallas kernels, half_leaf(): pl.pallas_call(functools.partial(half_kernel, part=part), out_shape=jax.S...  12.5 us
    pallas_call x1, Pallas kernels, climb(): pl.pallas_call(climb_kernel, out_shape=(jax.ShapeDtypeStruct((32, 64, 128...  9.22 us
    ppermute x1, starting transfers between devices, steps(): after = lax.ppermute(low, both, [(i + 1, i) for i in range(ends)])  7.76 us
    pallas_call x1, Pallas kernels, leaf_chol(): pl.pallas_call(leaf_chol_kernel, out_shape=jax.ShapeDtypeStruct((32, 64,...  7.15 us
    pallas_call x1, Pallas kernels, branch(): pl.pallas_call(branch_kernel, out_shape=(jax.ShapeDtypeStruct((1, 64, 64)...  6.8 us
  transfers between devices with their start and end apart: 10, of which 5 were waited for; matrix products, arithmetic and copies ran while one was open for 1% of the time, Pallas kernels for 27%

profile of v1, /device:TPU:1, one launch (start us, length us, event | category | flops | bytes accessed | tf_op | source)
XLA Modules:
  0.0 106.0 jit_solution(7892903781078509697)
XLA Ops:
  0.6 9.2 %climb.1 = (f32[32,64,128]{2,1,0:T(8,128)S(1)}, f32[64,128]{1,0:T(8,128)S(1)}, f32[64,128]{1,0:T(8,128)S(1)}) custom-call(bf16[64,64,256]{2,1,0:T(8,128)(2,1)} %b_hbm.1, f32[64,64,128]{2,1,0:T(8,128)} %t_hbm.1), custom_call_target="tpu_custom_call" | custom-call | flops 11500000256 | bytes 4096 | tf_op jit(solution)/shard_map/climb/pallas_call | solution.py:166
  9.9 2.2 %collective-permute-start.2 = (f32[64,128]{1,0:T(8,128)S(1)}, f32[64,128]{1,0:T(8,128)S(1)}, u32[]{:S(2)}, u32[]{:S(2)}) collective-permute-start(f32[64,128]{1,0:T(8,128)S(1)} %get-tuple-element.9.p0), channel_id=1, source_target_pairs={{0,1},{1,0},{2,3},{3,2},{4,5},{5,4},{6,7},{7,6},{8,9},{9,8},{10,11... | collective-permute-start | bytes 98312 | tf_op jit(solution)/shard_map/ppermute | solution.py:543
  12.1 1.3 %collective-permute-done.2.p1 = f32[64,128]{1,0:T(8,128)S(1)} collective-permute-done((f32[64,128]{1,0:T(8,128)S(1)}, f32[64,128]{1,0:T(8,128)S(1)}, u32[]{:S(2)}, u32[]{:S(2)}) %collective-permute-start.2) | collective-permute-done | bytes 32800 | tf_op jit(solution)/shard_map/ppermute | solution.py:543
  13.4 3.1 %collective-permute-start.3 = (f32[2,64,128]{2,1,0:T(8,128)S(1)}, f32[2,64,128]{2,1,0:T(8,128)S(1)}, u32[]{:S(2)}, u32[]{:S(2)}) collective-permute-start(f32[2,64,128]{2,1,0:T(8,128)S(1)} %pad_maximum_fusion.2), channel_id=1, source_target_pairs={{0,2},{1,3},{2,0},{3,1},{4,6},{5,7},{6,4},{7,5},{8,10},{9,11},{10,... | collective-permute-start | bytes 196616 | tf_op jit(solution)/shard_map/ppermute | solution.py:543
  16.4 7.1 %leaf_chol.1.low_ref.own_ref = f32[32,64,128]{2,1,0:T(8,128)S(1)} custom-call(f32[32,64,128]{2,1,0:T(8,128)S(1)} %get-tuple-element.8.g_ref), custom_call_target="tpu_custom_call" | custom-call | flops 6899999744 | bytes 4096 | tf_op jit(solution)/shard_map/leaf_chol/pallas_call | solution.py:263
  23.6 2.3 %collective-permute-start = (f32[32,64,128]{2,1,0:T(8,128)S(1)}, f32[32,64,128]{2,1,0:T(8,128)S(1)}, u32[]{:S(2)}, u32[]{:S(2)}) collective-permute-start(f32[32,64,128]{2,1,0:T(8,128)S(1)} %leaf_chol.1.low_ref.own_ref), channel_id=1, source_target_pairs={{0,1},{1,2},{2,3},{3,4},{4,5},{5,6},{6,7},{7,8},{8,9},{9,10},{10,1... | collective-permute-start | bytes 3145736 | tf_op jit(solution)/shard_map/ppermute | solution.py:562
  25.9 7.8 %collective-permute-start.1 = (f32[32,64,128]{2,1,0:T(8,128)S(1)}, f32[32,64,128]{2,1,0:T(8,128)S(1)}, u32[]{:S(2)}, u32[]{:S(2)}) collective-permute-start(f32[32,64,128]{2,1,0:T(8,128)S(1)} %leaf_chol.1.low_ref.own_ref), channel_id=1, source_target_pairs={{1,0},{2,1},{3,2},{4,3},{5,4},{6,5},{7,6},{8,7},{9,8},{10,9},{11,1... | collective-permute-start | bytes 3145736 | tf_op jit(solution)/shard_map/ppermute | solution.py:563
  33.7 0.0 collective-permute-done.3.p2
  33.7 0.7 pad_maximum_fusion
  34.4 0.0 collective-permute-start.4
  34.4 2.3 %collective-permute-start.5 = (f32[4,64,128]{2,1,0:T(8,128)}, f32[4,64,128]{2,1,0:T(8,128)}, u32[]{:S(2)}, u32[]{:S(2)}) collective-permute-start(f32[4,64,128]{2,1,0:T(8,128)} %pad_maximum_fusion), channel_id=1, source_target_pairs={{0,8},{1,9},{2,10},{3,11},{4,12},{5,13},{6,14},{7,15},{8,0},{9,1},... | collective-permute-start | bytes 393224 | tf_op jit(solution)/shard_map/ppermute | solution.py:543
  36.6 0.7 collective-permute-start.6
  37.4 6.2 %shard_map.85.y_ref = bf16[128,64,256]{2,1,0:T(8,128)(2,1)S(1)} custom-call(f32[64,64,512]{2,1,0:T(8,128)} %c1_ref.3, f32[64,64,512]{2,1,0:T(8,128)} %c1_ref.3, f32[32,64,128]{2,1,0:T(8,128)S(1)} %leaf_chol.1.low_ref.own_ref), custom_call_target="tpu_custom_call" | custom-call | flops 6899999744 | bytes 4096 | tf_op jit(solution)/shard_map/pallas_call | solution.py:315
  43.6 0.0 copy-start.1
  43.6 1.9 %copy-done.1 = bf16[128,64,256]{2,1,0:T(8,128)(2,1)} copy-done((bf16[128,64,256]{2,1,0:T(8,128)(2,1)}, bf16[128,64,256]{2,1,0:T(8,128)(2,1)S(1)}, u32[]{:S(2)}) %copy-start.1) | copy-done | bytes 4194328
  45.6 0.1 pad_add_fusion.at_ref
  45.6 9.4 %collective-permute-done.4.p3 = f32[4,64,128]{2,1,0:T(8,128)S(1)} collective-permute-done((f32[4,64,128]{2,1,0:T(8,128)}, f32[4,64,128]{2,1,0:T(8,128)S(1)}, u32[]{:S(2)}, u32[]{:S(2)}) %collective-permute-start.4) | collective-permute-done | bytes 131104 | tf_op jit(solution)/shard_map/ppermute | solution.py:543
  55.0 6.8 %collective-permute-done.5.p4 = f32[4,64,128]{2,1,0:T(8,128)} collective-permute-done((f32[4,64,128]{2,1,0:T(8,128)}, f32[4,64,128]{2,1,0:T(8,128)}, u32[]{:S(2)}, u32[]{:S(2)}) %collective-permute-start.5) | collective-permute-done | bytes 131104 | tf_op jit(solution)/shard_map/ppermute | solution.py:543
  61.9 0.0 collective-permute-done.6.p5
  61.9 6.8 %branch.1 = (f32[1,64,64]{2,1,0:T(8,128)}, f32[64,128]{1,0:T(8,128)S(1)}) custom-call(s32[2]{0:T(128)S(1)} %pad_add_fusion.at_ref, f32[64,128]{1,0:T(8,128)S(1)} %get-tuple-element.9.p0, f32[64,128]{1,0:T(8,128)S(1)} %collective-permute-done.2.p1, f32[2,64,128]{2,1,0:T(8,128)S(1)} %collective-permute-done.3.p2, f32[4,64,128]{2,1,0:T(8,128)S(1)} %collective-permute-done.4.p3, ...), custom_call_target="tpu_custom_call" | custom-call | flops 5750000128 | bytes 4096 | tf_op jit(solution)/shard_map/branch/pallas_call | solution.py:483
  68.7 0.0 copy-start.5
  68.7 0.0 copy-start.6
  68.7 0.5 collective-permute-start.7
  69.2 6.2 %shard_map.86.y_ref = bf16[128,64,256]{2,1,0:T(8,128)(2,1)S(1)} custom-call(f32[64,64,512]{2,1,0:T(8,128)} %c1_ref.3, f32[64,64,512]{2,1,0:T(8,128)} %c1_ref.3, f32[32,64,128]{2,1,0:T(8,128)S(1)} %leaf_chol.1.low_ref.own_ref), custom_call_target="tpu_custom_call" | custom-call | flops 6899999744 | bytes 4096 | tf_op jit(solution)/shard_map/pallas_call | solution.py:315
  75.4 0.0 copy-start.3
  75.4 2.0 %copy-done.3 = bf16[128,64,256]{2,1,0:T(8,128)(2,1)} copy-done((bf16[128,64,256]{2,1,0:T(8,128)(2,1)}, bf16[128,64,256]{2,1,0:T(8,128)(2,1)S(1)}, u32[]{:S(2)}) %copy-start.3) | copy-done | bytes 4194328
  77.4 0.0 collective-permute-done.7.l1
  77.5 1.3 %collective-permute-start.8 = (f32[2,64,128]{2,1,0:T(8,128)S(1)}, f32[2,64,128]{2,1,0:T(8,128)S(1)}, u32[]{:S(2)}, u32[]{:S(2)}) collective-permute-start(f32[2,64,128]{2,1,0:T(8,128)S(1)} %pad_maximum_fusion.3), channel_id=1, source_target_pairs={{0,32},{16,48},{32,0},{48,16},{64,96},{80,112},{96,64},{112,80},{1... | collective-permute-start | bytes 196616 | tf_op jit(solution)/shard_map/ppermute | solution.py:543
  78.7 0.0 copy-done.5
  78.7 2.4 %collective-permute-done.8.l2 = f32[2,64,128]{2,1,0:T(8,128)S(1)} collective-permute-done((f32[2,64,128]{2,1,0:T(8,128)S(1)}, f32[2,64,128]{2,1,0:T(8,128)S(1)}, u32[]{:S(2)}, u32[]{:S(2)}) %collective-permute-start.8) | collective-permute-done | bytes 65568 | tf_op jit(solution)/shard_map/ppermute | solution.py:543
  81.2 3.0 %collective-permute-start.9 = (f32[4,64,128]{2,1,0:T(8,128)S(1)}, f32[4,64,128]{2,1,0:T(8,128)S(1)}, u32[]{:S(2)}, u32[]{:S(2)}) collective-permute-start(f32[4,64,128]{2,1,0:T(8,128)S(1)} %pad_maximum_fusion.1), channel_id=1, source_target_pairs={{0,64},{16,80},{32,96},{48,112},{64,0},{80,16},{96,32},{112,48},{1... | collective-permute-start | bytes 393224 | tf_op jit(solution)/shard_map/ppermute | solution.py:543
  84.2 0.0 copy-done.6
  84.2 2.9 %collective-permute-done.9.l3 = f32[4,64,128]{2,1,0:T(8,128)S(1)} collective-permute-done((f32[4,64,128]{2,1,0:T(8,128)S(1)}, f32[4,64,128]{2,1,0:T(8,128)S(1)}, u32[]{:S(2)}, u32[]{:S(2)}) %collective-permute-start.9) | collective-permute-done | bytes 131104 | tf_op jit(solution)/shard_map/ppermute | solution.py:543
  87.1 0.0 copy-start
  87.1 1.0 copy-done
  88.1 2.2 %far.1 = f32[64,16,64]{2,1,0:T(8,128)} custom-call(s32[16]{0:T(128)S(1)} %broadcast_xor_fusion.cols_ref, f32[64,16,64]{2,1,0:T(8,128)S(1)} %bitcast.16, f32[64,128]{1,0:T(8,128)S(1)} %get-tuple-element.11.l0, f32[64,128]{1,0:T(8,128)S(1)} %collective-permute-done.7.l1, f32[2,64,128]{2,1,0:T(8,128)S(1)} %collective-permute-done.8.l2, ...), custom_call_target="tpu_custom_call" | custom-call | flops 3449999872 | bytes 4096 | tf_op jit(solution)/shard_map/far/pallas_call | solution.py:530
  90.4 0.0 copy-start.4
  90.4 0.0 collective-permute-done.before_ref
  90.4 0.0 collective-permute-done.1.after_ref
  90.4 1.9 %prep.1.d_ref = bf16[192,64,256]{2,1,0:T(8,128)(2,1)S(1)} custom-call(f32[32,64,128]{2,1,0:T(8,128)S(1)} %collective-permute-done.before_ref, f32[32,64,128]{2,1,0:T(8,128)S(1)} %leaf_chol.1.low_ref.own_ref, f32[32,64,128]{2,1,0:T(8,128)S(1)} %collective-permute-done.1.after_ref), custom_call_target="tpu_custom_call" | custom-call | flops 3449999872 | bytes 4096 | tf_op jit(solution)/shard_map/prep/pallas_call | solution.py:346
  92.2 0.3 copy-done.4
  92.5 0.0 copy-start.2
  92.5 6.6 %shard_map.87.refs_0_ = f32[64,64,512]{2,1,0:T(8,128)} custom-call(s32[512]{0:T(512)S(1)} %broadcast_subtract_fusion.cols_ref, bf16[128,64,256]{2,1,0:T(8,128)(2,1)S(1)} %copy-done.4, bf16[192,64,256]{2,1,0:T(8,128)(2,1)S(1)} %prep.1.d_ref), custom_call_target="tpu_custom_call" | custom-call | flops 9200000000 | bytes 4096 | tf_op jit(solution)/shard_map/pallas_call | solution.py:409
  99.2 0.0 copy-done.2
  99.2 6.6 %shard_map.88 = f32[64,64,512]{2,1,0:T(8,128)} custom-call(s32[512]{0:T(512)S(1)} %broadcast_subtract_fusion.cols_ref, bf16[128,64,256]{2,1,0:T(8,128)(2,1)S(1)} %copy-done.2, bf16[192,64,256]{2,1,0:T(8,128)(2,1)S(1)} %prep.1.d_ref, f32[64,64,512]{2,1,0:T(8,128)} %shard_map.87.refs_0_), custom_call_target="tpu_custom_call", output_to_operand_aliasing={{}: (3, {})} | custom-call | flops 9200000000 | bytes 4096 | tf_op jit(solution)/shard_map/pallas_call | solution.py:409
  (5 shorter events, 0.0 us)
Async XLA Ops:
  9.9 3.5 %collective-permute-start.2 = (f32[64,128]{1,0:T(8,128)S(1)}, f32[64,128]{1,0:T(8,128)S(1)}, u32[]{:S(2)}, u32[]{:S(2)}) collective-permute-start(f32[64,128]{1,0:T(8,128)S(1)} %get-tuple-element.9.p0), channel_id=1, source_target_pairs={{0,1},{1,0},{2,3},{3,2},{4,5},{5,4},{6,7},{7,6},{8,9},{9,8},{10,11... | collective-permute-start | bytes 98312 | tf_op jit(solution)/shard_map/ppermute | solution.py:543
  13.4 20.3 %collective-permute-start.3 = (f32[2,64,128]{2,1,0:T(8,128)S(1)}, f32[2,64,128]{2,1,0:T(8,128)S(1)}, u32[]{:S(2)}, u32[]{:S(2)}) collective-permute-start(f32[2,64,128]{2,1,0:T(8,128)S(1)} %pad_maximum_fusion.2), channel_id=1, source_target_pairs={{0,2},{1,3},{2,0},{3,1},{4,6},{5,7},{6,4},{7,5},{8,10},{9,11},{10,... | collective-permute-start | bytes 196616 | tf_op jit(solution)/shard_map/ppermute | solution.py:543
  23.6 66.8 %collective-permute-start = (f32[32,64,128]{2,1,0:T(8,128)S(1)}, f32[32,64,128]{2,1,0:T(8,128)S(1)}, u32[]{:S(2)}, u32[]{:S(2)}) collective-permute-start(f32[32,64,128]{2,1,0:T(8,128)S(1)} %leaf_chol.1.low_ref.own_ref), channel_id=1, source_target_pairs={{0,1},{1,2},{2,3},{3,4},{4,5},{5,6},{6,7},{7,8},{8,9},{9,10},{10,1... | collective-permute-start | bytes 3145736 | tf_op jit(solution)/shard_map/ppermute | solution.py:562
  25.9 64.4 %collective-permute-start.1 = (f32[32,64,128]{2,1,0:T(8,128)S(1)}, f32[32,64,128]{2,1,0:T(8,128)S(1)}, u32[]{:S(2)}, u32[]{:S(2)}) collective-permute-start(f32[32,64,128]{2,1,0:T(8,128)S(1)} %leaf_chol.1.low_ref.own_ref), channel_id=1, source_target_pairs={{1,0},{2,1},{3,2},{4,3},{5,4},{6,5},{7,6},{8,7},{9,8},{10,9},{11,1... | collective-permute-start | bytes 3145736 | tf_op jit(solution)/shard_map/ppermute | solution.py:563
  34.4 20.7 %collective-permute-start.4 = (f32[4,64,128]{2,1,0:T(8,128)}, f32[4,64,128]{2,1,0:T(8,128)S(1)}, u32[]{:S(2)}, u32[]{:S(2)}) collective-permute-start(f32[4,64,128]{2,1,0:T(8,128)} %pad_maximum_fusion), channel_id=1, source_target_pairs={{0,4},{1,5},{2,6},{3,7},{4,8},{5,9},{6,10},{7,11},{8,12},{9,13},{1... | collective-permute-start | bytes 393224 | tf_op jit(solution)/shard_map/ppermute | solution.py:543
  34.4 27.5 %collective-permute-start.5 = (f32[4,64,128]{2,1,0:T(8,128)}, f32[4,64,128]{2,1,0:T(8,128)}, u32[]{:S(2)}, u32[]{:S(2)}) collective-permute-start(f32[4,64,128]{2,1,0:T(8,128)} %pad_maximum_fusion), channel_id=1, source_target_pairs={{0,8},{1,9},{2,10},{3,11},{4,12},{5,13},{6,14},{7,15},{8,0},{9,1},... | collective-permute-start | bytes 393224 | tf_op jit(solution)/shard_map/ppermute | solution.py:543
  36.6 25.3 %collective-permute-start.6 = (f32[4,64,128]{2,1,0:T(8,128)}, f32[4,64,128]{2,1,0:T(8,128)}, u32[]{:S(2)}, u32[]{:S(2)}) collective-permute-start(f32[4,64,128]{2,1,0:T(8,128)} %pad_maximum_fusion), channel_id=1, source_target_pairs={{0,12},{1,13},{2,14},{3,15},{4,0},{5,1},{6,2},{7,3},{8,4},{9,5},{1... | collective-permute-start | bytes 393224 | tf_op jit(solution)/shard_map/ppermute | solution.py:543
  43.6 2.0 %copy-start.1 = (bf16[128,64,256]{2,1,0:T(8,128)(2,1)}, bf16[128,64,256]{2,1,0:T(8,128)(2,1)S(1)}, u32[]{:S(2)}) copy-start(bf16[128,64,256]{2,1,0:T(8,128)(2,1)S(1)} %shard_map.85.y_ref) | copy-start | bytes 12582916
  68.7 10.1 %copy-start.5 = (s32[512]{0:T(512)S(1)}, s32[512]{0:T(512)}, u32[]{:S(2)}) copy-start(s32[512]{0:T(512)} %param.9) | copy-start | bytes 6148
  68.7 15.5 %copy-start.6 = (s32[16]{0:T(128)S(1)}, s32[16]{0:T(128)}, u32[]{:S(2)}) copy-start(s32[16]{0:T(128)} %param.11) | copy-start | bytes 196
  68.7 8.8 %collective-permute-start.7 = (f32[64,128]{1,0:T(8,128)S(1)}, f32[64,128]{1,0:T(8,128)S(1)}, u32[]{:S(2)}, u32[]{:S(2)}) collective-permute-start(f32[64,128]{1,0:T(8,128)S(1)} %get-tuple-element.11.l0), channel_id=1, source_target_pairs={{0,16},{16,0},{32,48},{48,32},{64,80},{80,64},{96,112},{112,96},{1... | collective-permute-start | bytes 98312 | tf_op jit(solution)/shard_map/ppermute | solution.py:543
  75.4 2.0 %copy-start.3 = (bf16[128,64,256]{2,1,0:T(8,128)(2,1)}, bf16[128,64,256]{2,1,0:T(8,128)(2,1)S(1)}, u32[]{:S(2)}) copy-start(bf16[128,64,256]{2,1,0:T(8,128)(2,1)S(1)} %shard_map.86.y_ref) | copy-start | bytes 12582916
  77.5 3.7 %collective-permute-start.8 = (f32[2,64,128]{2,1,0:T(8,128)S(1)}, f32[2,64,128]{2,1,0:T(8,128)S(1)}, u32[]{:S(2)}, u32[]{:S(2)}) collective-permute-start(f32[2,64,128]{2,1,0:T(8,128)S(1)} %pad_maximum_fusion.3), channel_id=1, source_target_pairs={{0,32},{16,48},{32,0},{48,16},{64,96},{80,112},{96,64},{112,80},{1... | collective-permute-start | bytes 196616 | tf_op jit(solution)/shard_map/ppermute | solution.py:543
  81.2 5.9 %collective-permute-start.9 = (f32[4,64,128]{2,1,0:T(8,128)S(1)}, f32[4,64,128]{2,1,0:T(8,128)S(1)}, u32[]{:S(2)}, u32[]{:S(2)}) collective-permute-start(f32[4,64,128]{2,1,0:T(8,128)S(1)} %pad_maximum_fusion.1), channel_id=1, source_target_pairs={{0,64},{16,80},{32,96},{48,112},{64,0},{80,16},{96,32},{112,48},{1... | collective-permute-start | bytes 393224 | tf_op jit(solution)/shard_map/ppermute | solution.py:543
  87.1 1.0 copy-start
  90.4 2.2 %copy-start.4 = (bf16[128,64,256]{2,1,0:T(8,128)(2,1)S(1)}, bf16[128,64,256]{2,1,0:T(8,128)(2,1)}, u32[]{:S(2)}) copy-start(bf16[128,64,256]{2,1,0:T(8,128)(2,1)} %copy-done.3) | copy-start | bytes 12582916
  92.5 6.6 %copy-start.2 = (bf16[128,64,256]{2,1,0:T(8,128)(2,1)S(1)}, bf16[128,64,256]{2,1,0:T(8,128)(2,1)}, u32[]{:S(2)}) copy-start(bf16[128,64,256]{2,1,0:T(8,128)(2,1)} %copy-done.1) | copy-start | bytes 12582916

commit v2 on v1

--- a/solution.py
+++ b/solution.py
@@ -186,9 +186,9 @@
     )(basis, transfers)
 
 
-def chol_lanes(a_ref, count=64, panel=8):
+def chol_lanes(a_ref, panels=range(8), count=64, panel=8):
     sub = lax.broadcasted_iota(jnp.int32, (8, 128), 0)
-    for p in range(count // panel):
+    for p in panels:
         base = p * panel
         if p > 0:
             for it in range(p, count // 8):
@@ -231,7 +231,10 @@
                 a_ref[base + j, it * 8 : it * 8 + 8, :] = v[j]
 
 
-def leaf_chol_kernel(g_ref, low_ref, a_ref, u_ref):
+EARLY = 3
+
+
+def chol_head_kernel(g_ref, a_ref, u_ref):
     def load(s, _):
         at = pl.ds(pl.multiple_of(s * 8, 8), 8)
         for g in range(4):
@@ -243,7 +246,25 @@
         return 0
 
     lax.fori_loop(0, 8, load, 0)
-    chol_lanes(a_ref)
+    chol_lanes(a_ref, range(EARLY))
+
+
+def chol_head(gram):
+    return pl.pallas_call(
+        chol_head_kernel,
+        out_shape=jax.ShapeDtypeStruct((64, 64, 128), F32),
+        in_specs=[VMEM],
+        out_specs=VMEM,
+        scratch_shapes=[pltpu.VMEM((8, 64, 128), F32)],
+        compiler_params=params(8),
+        cost_estimate=cost(4),
+        name="chol_head",
+    )(gram)
+
+
+def chol_tail_kernel(i_ref, low_ref, a_ref, u_ref):
+    a_ref[...] = i_ref[...]
+    chol_lanes(a_ref, range(EARLY, 8))
 
     def store(s, _):
         at = pl.ds(pl.multiple_of(s * 8, 8), 8)
@@ -259,17 +280,17 @@
     lax.fori_loop(0, 8, store, 0)
 
 
-def leaf_chol(gram):
-    return pl.pallas_call(
-        leaf_chol_kernel,
+def chol_tail(part):
+    return pl.pallas_call(
+        chol_tail_kernel,
         out_shape=jax.ShapeDtypeStruct((32, 64, 128), F32),
         in_specs=[VMEM],
         out_specs=VMEM,
         scratch_shapes=[pltpu.VMEM((64, 64, 128), F32), pltpu.VMEM((8, 64, 128), F32)],
         compiler_params=params(8),
-        cost_estimate=cost(6),
-        name="leaf_chol",
-    )(gram)
+        cost_estimate=cost(4),
+        name="chol_tail",
+    )(part)
 
 
 def half_kernel(c0_ref, c1_ref, low_ref, y_ref, s_ref, u_ref, part):
@@ -328,30 +349,31 @@
     )(coupling, coupling, low)
 
 
-def prep_kernel(before_ref, own_ref, after_ref, d_ref):
+def prep_kernel(odd_ref, near_ref, own_ref, far_ref, d_ref):
     first = first_half()
-    for group, ref in enumerate((before_ref, own_ref, after_ref)):
-
-        def pair(q, _, ref=ref, group=group):
+    odd = odd_ref[0]
+    for base, ref in ((64, own_ref), (128 - 128 * odd, near_ref), (128 * odd, far_ref)):
+
+        def pair(q, _, ref=ref, base=base):
             x = ref[q]
             y = pltpu.roll(x, 64, 1)
-            d_ref[group * 64 + q] = right_of(jnp.where(first, x, y))
-            d_ref[group * 64 + 32 + q] = right_of(jnp.where(first, y, x))
+            d_ref[base + q] = right_of(jnp.where(first, x, y))
+            d_ref[base + 32 + q] = right_of(jnp.where(first, y, x))
             return 0
 
         lax.fori_loop(0, 32, pair, 0, unroll=8)
 
 
-def prep(before, own, after):
+def prep(odd, near, own, far):
     return pl.pallas_call(
         prep_kernel,
         out_shape=jax.ShapeDtypeStruct((192, 64, 256), BF16),
-        in_specs=[VMEM] * 3,
+        in_specs=[SMEM] + [VMEM] * 3,
         out_specs=VMEM,
         compiler_params=params(16),
         cost_estimate=cost(3),
         name="prep",
-    )(before, own, after)
+    )(odd, near, own, far)
 
 
 def full_kernel(cols_ref, y_ref, d_ref, *refs, part):
@@ -555,22 +577,24 @@
     at = lax.axis_index("narrow")
     gram, top, pay = climb(basis_t, nested_transfer_matrices)
     pay_a = shifted(pay, "narrow", lambda i: i ^ 1)
-    low = leaf_chol(gram)
+    head = chol_head(gram)
     pair = jnp.stack([pay, pay_a])
     pay_b = shifted(pair, "narrow", lambda i: i ^ 2)
-    ends = lax.axis_size(both) - 1
-    before = lax.ppermute(low, both, [(i, i + 1) for i in range(ends)])
-    after = lax.ppermute(low, both, [(i + 1, i) for i in range(ends)])
-    half_a = half_leaf(leaf_coupling, low, 0)
+    low = chol_tail(head)
     quad = jnp.concatenate([pair, pay_b])
     pay_c = [shifted(quad, "narrow", lambda i, s=s: (i + 4 * s) % 16) for s in (1, 2, 3)]
+    count = lax.axis_size(both)
+    low_near = lax.ppermute(low, both, [(i, i ^ 1) for i in range(count)])
+    later = [(i, i + 1) for i in range(1, count - 1, 2)]
+    low_far = lax.ppermute(low, both, later + [(j, i) for i, j in later])
+    half_a = half_leaf(leaf_coupling, low, 0)
     half_b = half_leaf(leaf_coupling, low, 1)
     ones = 1 + sum((at % 2**k == 2**k - 1).astype(jnp.int32) for k in range(1, 5))
     pick = jnp.where(ones <= 4, (16 + at) >> ones, 0)
     place = jnp.stack([at, pick]).astype(jnp.int32)
     group_factors, own = branch(place, [pay, pay_a, pay_b, *pay_c], top)
     own_a = shifted(own, "wide", lambda i: i ^ 1)
-    factors = prep(before, low, after)
+    factors = prep(at.reshape(1) % 2, low_near, low, low_far)
     two = jnp.stack([own, own_a])
     own_b = shifted(two, "wide", lambda i: i ^ 2)
     cols = leaf_columns - (lax.axis_index(both) * 64 - 64)

time: 108 us -> 104 us (0.963); the launches traced: 106 us -> 104 us
  starting transfers between devices: 23.1 us -> 20.6 us
    ppermute x2, starting transfers between devices: 10.1 us -> 7.47 us  [the longest x1 7.39 us: steps(): low_far = lax.ppermute(low, both, later + [(j, i) for i, j in later])]
    pallas_call x1 -> x2, Pallas kernels: 7.15 us -> 7.28 us  [the longest x1 4.5 us: chol_tail(): pl.pallas_call(chol_tail_kernel, out_shape=jax.ShapeDtypeStruct((32, 64,...]
  transfers between devices with their start and end apart: 10 -> 10, of which waited for: 5 -> 4; matrix products, arithmetic and copies ran while one was open for 1% -> 1% of each run, Pallas kernels for 27% -> 28%
where the time goes in v2:
time: 104 us
  Pallas kernels  53 us (51%)
  waiting for transfers between devices  23.1 us (22%)
  starting transfers between devices  20.6 us (20%)
  local copies, waits for them, and re-layouts  5.32 us (5%)
    ppermute x8, waiting for transfers between devices, shifted(): lax.ppermute(value, axis, [(i, to(i)) for i in range(lax.axis_size(axis))])  23.1 us
    pallas_call x2, Pallas kernels, full_leaf(): pl.pallas_call(functools.partial(full_kernel, part=part), out_shape=jax.S...  13.2 us
    ppermute x8, starting transfers between devices, shifted(): lax.ppermute(value, axis, [(i, to(i)) for i in range(lax.axis_size(axis))])  13.1 us
    pallas_call x2, Pallas kernels, half_leaf(): pl.pallas_call(functools.partial(half_kernel, part=part), out_shape=jax.S...  12.4 us
    pallas_call x1, Pallas kernels, climb(): pl.pallas_call(climb_kernel, out_shape=(jax.ShapeDtypeStruct((32, 64, 128...  9.22 us
    ppermute x1, starting transfers between devices, steps(): low_far = lax.ppermute(low, both, later + [(j, i) for i, j in later])  7.39 us
    pallas_call x1, Pallas kernels, branch(): pl.pallas_call(branch_kernel, out_shape=(jax.ShapeDtypeStruct((1, 64, 64)...  6.8 us
    unnamed x14, local copies, waits for them, and re-layouts  5.32 us
  transfers between devices with their start and end apart: 10, of which 4 were waited for; matrix products, arithmetic and copies ran while one was open for 1% of the time, Pallas kernels for 28%

profile of v2, /device:TPU:1, one launch (start us, length us, event | category | flops | bytes accessed | tf_op | source)
XLA Modules:
  0.0 103.8 jit_solution(3731209333579762812)
XLA Ops:
  0.6 9.2 %climb.1 = (f32[32,64,128]{2,1,0:T(8,128)S(1)}, f32[64,128]{1,0:T(8,128)S(1)}, f32[64,128]{1,0:T(8,128)S(1)}) custom-call(bf16[64,64,256]{2,1,0:T(8,128)(2,1)} %b_hbm.1, f32[64,64,128]{2,1,0:T(8,128)} %t_hbm.1), custom_call_target="tpu_custom_call" | custom-call | flops 11500000256 | bytes 4096 | tf_op jit(solution)/shard_map/climb/pallas_call | solution.py:166
  9.9 2.2 %collective-permute-start.2 = (f32[64,128]{1,0:T(8,128)S(1)}, f32[64,128]{1,0:T(8,128)S(1)}, u32[]{:S(2)}, u32[]{:S(2)}) collective-permute-start(f32[64,128]{1,0:T(8,128)S(1)} %get-tuple-element.9.p0), channel_id=1, source_target_pairs={{0,1},{1,0},{2,3},{3,2},{4,5},{5,4},{6,7},{7,6},{8,9},{9,8},{10,11... | collective-permute-start | bytes 98312 | tf_op jit(solution)/shard_map/ppermute | solution.py:565
  12.1 2.8 %chol_head.1.i_ref = f32[64,64,128]{2,1,0:T(8,128)S(1)} custom-call(f32[32,64,128]{2,1,0:T(8,128)S(1)} %get-tuple-element.8.g_ref), custom_call_target="tpu_custom_call" | custom-call | flops 4600000000 | bytes 4096 | tf_op jit(solution)/shard_map/chol_head/pallas_call | solution.py:253
  14.8 0.0 collective-permute-done.2.p1
  14.9 2.7 %collective-permute-start.3 = (f32[2,64,128]{2,1,0:T(8,128)S(1)}, f32[2,64,128]{2,1,0:T(8,128)S(1)}, u32[]{:S(2)}, u32[]{:S(2)}) collective-permute-start(f32[2,64,128]{2,1,0:T(8,128)S(1)} %pad_maximum_fusion.2), channel_id=1, source_target_pairs={{0,2},{1,3},{2,0},{3,1},{4,6},{5,7},{6,4},{7,5},{8,10},{9,11},{10,... | collective-permute-start | bytes 196616 | tf_op jit(solution)/shard_map/ppermute | solution.py:565
  17.6 4.5 %chol_tail.1.low_ref.own_ref = f32[32,64,128]{2,1,0:T(8,128)S(1)} custom-call(f32[64,64,128]{2,1,0:T(8,128)S(1)} %chol_head.1.i_ref), custom_call_target="tpu_custom_call" | custom-call | flops 4600000000 | bytes 4096 | tf_op jit(solution)/shard_map/chol_tail/pallas_call | solution.py:284
  22.1 0.1 collective-permute-start
  22.2 7.4 %collective-permute-start.1 = (f32[32,64,128]{2,1,0:T(8,128)S(1)}, f32[32,64,128]{2,1,0:T(8,128)S(1)}, u32[]{:S(2)}, u32[]{:S(2)}) collective-permute-start(f32[32,64,128]{2,1,0:T(8,128)S(1)} %chol_tail.1.low_ref.own_ref), channel_id=1, source_target_pairs={{1,2},{3,4},{5,6},{7,8},{9,10},{11,12},{13,14},{15,16},{17,18},{19... | collective-permute-start | bytes 3145736 | tf_op jit(solution)/shard_map/ppermute | solution.py:589
  29.6 0.0 collective-permute-done.3.p2
  29.6 0.7 pad_maximum_fusion
  30.2 0.0 collective-permute-start.4
  30.2 0.0 collective-permute-start.5
  30.2 2.7 %collective-permute-start.6 = (f32[4,64,128]{2,1,0:T(8,128)}, f32[4,64,128]{2,1,0:T(8,128)}, u32[]{:S(2)}, u32[]{:S(2)}) collective-permute-start(f32[4,64,128]{2,1,0:T(8,128)} %pad_maximum_fusion), channel_id=1, source_target_pairs={{0,12},{1,13},{2,14},{3,15},{4,0},{5,1},{6,2},{7,3},{8,4},{9,5},{1... | collective-permute-start | bytes 393224 | tf_op jit(solution)/shard_map/ppermute | solution.py:565
  32.9 6.2 %shard_map.85.y_ref = bf16[128,64,256]{2,1,0:T(8,128)(2,1)S(1)} custom-call(f32[64,64,512]{2,1,0:T(8,128)} %c1_ref.3, f32[64,64,512]{2,1,0:T(8,128)} %c1_ref.3, f32[32,64,128]{2,1,0:T(8,128)S(1)} %chol_tail.1.low_ref.own_ref), custom_call_target="tpu_custom_call" | custom-call | flops 6899999744 | bytes 4096 | tf_op jit(solution)/shard_map/pallas_call | solution.py:336
  39.1 0.0 copy-start.1
  39.1 1.9 %copy-done.1 = bf16[128,64,256]{2,1,0:T(8,128)(2,1)} copy-done((bf16[128,64,256]{2,1,0:T(8,128)(2,1)}, bf16[128,64,256]{2,1,0:T(8,128)(2,1)S(1)}, u32[]{:S(2)}) %copy-start.1) | copy-done | bytes 4194328
  41.1 0.1 pad_add_fusion.at_ref
  41.2 12.6 %collective-permute-done.4.p3 = f32[4,64,128]{2,1,0:T(8,128)S(1)} collective-permute-done((f32[4,64,128]{2,1,0:T(8,128)}, f32[4,64,128]{2,1,0:T(8,128)S(1)}, u32[]{:S(2)}, u32[]{:S(2)}) %collective-permute-start.4) | collective-permute-done | bytes 131104 | tf_op jit(solution)/shard_map/ppermute | solution.py:565
  53.8 5.2 %collective-permute-done.5.p4 = f32[4,64,128]{2,1,0:T(8,128)} collective-permute-done((f32[4,64,128]{2,1,0:T(8,128)}, f32[4,64,128]{2,1,0:T(8,128)}, u32[]{:S(2)}, u32[]{:S(2)}) %collective-permute-start.5) | collective-permute-done | bytes 131104 | tf_op jit(solution)/shard_map/ppermute | solution.py:565
  58.9 0.0 collective-permute-done.6.p5
  58.9 6.8 %branch.1 = (f32[1,64,64]{2,1,0:T(8,128)}, f32[64,128]{1,0:T(8,128)S(1)}) custom-call(s32[2]{0:T(128)S(1)} %pad_add_fusion.at_ref, f32[64,128]{1,0:T(8,128)S(1)} %get-tuple-element.9.p0, f32[64,128]{1,0:T(8,128)S(1)} %collective-permute-done.2.p1, f32[2,64,128]{2,1,0:T(8,128)S(1)} %collective-permute-done.3.p2, f32[4,64,128]{2,1,0:T(8,128)S(1)} %collective-permute-done.4.p3, ...), custom_call_target="tpu_custom_call" | custom-call | flops 5750000128 | bytes 4096 | tf_op jit(solution)/shard_map/branch/pallas_call | solution.py:505
  65.7 0.0 copy-start.5
  65.7 0.0 copy-start.6
  65.8 1.2 %collective-permute-start.7 = (f32[64,128]{1,0:T(8,128)S(1)}, f32[64,128]{1,0:T(8,128)S(1)}, u32[]{:S(2)}, u32[]{:S(2)}) collective-permute-start(f32[64,128]{1,0:T(8,128)S(1)} %get-tuple-element.11.l0), channel_id=1, source_target_pairs={{0,16},{16,0},{32,48},{48,32},{64,80},{80,64},{96,112},{112,96},{1... | collective-permute-start | bytes 98312 | tf_op jit(solution)/shard_map/ppermute | solution.py:565
  67.0 6.2 %shard_map.86.y_ref = bf16[128,64,256]{2,1,0:T(8,128)(2,1)S(1)} custom-call(f32[64,64,512]{2,1,0:T(8,128)} %c1_ref.3, f32[64,64,512]{2,1,0:T(8,128)} %c1_ref.3, f32[32,64,128]{2,1,0:T(8,128)S(1)} %chol_tail.1.low_ref.own_ref), custom_call_target="tpu_custom_call" | custom-call | flops 6899999744 | bytes 4096 | tf_op jit(solution)/shard_map/pallas_call | solution.py:336
  73.2 0.0 copy-start.3
  73.2 2.0 %copy-done.3 = bf16[128,64,256]{2,1,0:T(8,128)(2,1)} copy-done((bf16[128,64,256]{2,1,0:T(8,128)(2,1)}, bf16[128,64,256]{2,1,0:T(8,128)(2,1)S(1)}, u32[]{:S(2)}) %copy-start.3) | copy-done | bytes 4194328
  75.2 0.0 collective-permute-done.7.l1
  75.3 1.3 %collective-permute-start.8 = (f32[2,64,128]{2,1,0:T(8,128)S(1)}, f32[2,64,128]{2,1,0:T(8,128)S(1)}, u32[]{:S(2)}, u32[]{:S(2)}) collective-permute-start(f32[2,64,128]{2,1,0:T(8,128)S(1)} %pad_maximum_fusion.3), channel_id=1, source_target_pairs={{0,32},{16,48},{32,0},{48,16},{64,96},{80,112},{96,64},{112,80},{1... | collective-permute-start | bytes 196616 | tf_op jit(solution)/shard_map/ppermute | solution.py:565
  76.5 0.0 copy-done.5
  76.6 2.4 %collective-permute-done.8.l2 = f32[2,64,128]{2,1,0:T(8,128)S(1)} collective-permute-done((f32[2,64,128]{2,1,0:T(8,128)S(1)}, f32[2,64,128]{2,1,0:T(8,128)S(1)}, u32[]{:S(2)}, u32[]{:S(2)}) %collective-permute-start.8) | collective-permute-done | bytes 65568 | tf_op jit(solution)/shard_map/ppermute | solution.py:565
  79.0 3.0 %collective-permute-start.9 = (f32[4,64,128]{2,1,0:T(8,128)S(1)}, f32[4,64,128]{2,1,0:T(8,128)S(1)}, u32[]{:S(2)}, u32[]{:S(2)}) collective-permute-start(f32[4,64,128]{2,1,0:T(8,128)S(1)} %pad_maximum_fusion.1), channel_id=1, source_target_pairs={{0,64},{16,80},{32,96},{48,112},{64,0},{80,16},{96,32},{112,48},{1... | collective-permute-start | bytes 393224 | tf_op jit(solution)/shard_map/ppermute | solution.py:565
  82.0 0.0 copy-done.6
  82.0 2.9 %collective-permute-done.9.l3 = f32[4,64,128]{2,1,0:T(8,128)S(1)} collective-permute-done((f32[4,64,128]{2,1,0:T(8,128)S(1)}, f32[4,64,128]{2,1,0:T(8,128)S(1)}, u32[]{:S(2)}, u32[]{:S(2)}) %collective-permute-start.9) | collective-permute-done | bytes 131104 | tf_op jit(solution)/shard_map/ppermute | solution.py:565
  84.9 0.0 copy-start
  84.9 1.0 %copy-done = f32[64,64,16]{1,2,0:T(8,128)S(1)} copy-done((f32[64,64,16]{1,2,0:T(8,128)S(1)}, f32[64,64,16]{1,2,0:T(8,128)}, u32[]{:S(2)}) %copy-start) | copy-done | bytes 262168
  86.0 2.2 %far.1 = f32[64,16,64]{2,1,0:T(8,128)} custom-call(s32[16]{0:T(128)S(1)} %broadcast_xor_fusion.cols_ref, f32[64,16,64]{2,1,0:T(8,128)S(1)} %bitcast.16, f32[64,128]{1,0:T(8,128)S(1)} %get-tuple-element.11.l0, f32[64,128]{1,0:T(8,128)S(1)} %collective-permute-done.7.l1, f32[2,64,128]{2,1,0:T(8,128)S(1)} %collective-permute-done.8.l2, ...), custom_call_target="tpu_custom_call" | custom-call | flops 3449999872 | bytes 4096 | tf_op jit(solution)/shard_map/far/pallas_call | solution.py:552
  88.2 0.0 copy-start.4
  88.2 0.0 collective-permute-done.near_ref
  88.2 0.0 collective-permute-done.1.far_ref
  88.2 1.9 %prep.1.d_ref = bf16[192,64,256]{2,1,0:T(8,128)(2,1)S(1)} custom-call(s32[1]{0:T(128)S(6)} %select_n.29.odd_ref, f32[32,64,128]{2,1,0:T(8,128)S(1)} %collective-permute-done.near_ref, f32[32,64,128]{2,1,0:T(8,128)S(1)} %chol_tail.1.low_ref.own_ref, f32[32,64,128]{2,1,0:T(8,128)S(1)} %collective-permute-done.1.far_ref), custom_call_target="tpu_custom_call" | custom-call | flops 3449999872 | bytes 4096 | tf_op jit(solution)/shard_map/prep/pallas_call | solution.py:368
  90.0 0.3 copy-done.4
  90.4 0.0 copy-start.2
  90.4 6.6 %shard_map.87.refs_0_ = f32[64,64,512]{2,1,0:T(8,128)} custom-call(s32[512]{0:T(512)S(1)} %broadcast_subtract_fusion.cols_ref, bf16[128,64,256]{2,1,0:T(8,128)(2,1)S(1)} %copy-done.4, bf16[192,64,256]{2,1,0:T(8,128)(2,1)S(1)} %prep.1.d_ref), custom_call_target="tpu_custom_call" | custom-call | flops 9200000000 | bytes 4096 | tf_op jit(solution)/shard_map/pallas_call | solution.py:431
  97.0 0.0 copy-done.2
  97.0 6.6 %shard_map.88 = f32[64,64,512]{2,1,0:T(8,128)} custom-call(s32[512]{0:T(512)S(1)} %broadcast_subtract_fusion.cols_ref, bf16[128,64,256]{2,1,0:T(8,128)(2,1)S(1)} %copy-done.2, bf16[192,64,256]{2,1,0:T(8,128)(2,1)S(1)} %prep.1.d_ref, f32[64,64,512]{2,1,0:T(8,128)} %shard_map.87.refs_0_), custom_call_target="tpu_custom_call", output_to_operand_aliasing={{}: (3, {})} | custom-call | flops 9200000000 | bytes 4096 | tf_op jit(solution)/shard_map/pallas_call | solution.py:431
  (5 shorter events, 0.0 us)
Async XLA Ops:
  9.9 5.0 %collective-permute-start.2 = (f32[64,128]{1,0:T(8,128)S(1)}, f32[64,128]{1,0:T(8,128)S(1)}, u32[]{:S(2)}, u32[]{:S(2)}) collective-permute-start(f32[64,128]{1,0:T(8,128)S(1)} %get-tuple-element.9.p0), channel_id=1, source_target_pairs={{0,1},{1,0},{2,3},{3,2},{4,5},{5,4},{6,7},{7,6},{8,9},{9,8},{10,11... | collective-permute-start | bytes 98312 | tf_op jit(solution)/shard_map/ppermute | solution.py:565
  14.9 14.7 %collective-permute-start.3 = (f32[2,64,128]{2,1,0:T(8,128)S(1)}, f32[2,64,128]{2,1,0:T(8,128)S(1)}, u32[]{:S(2)}, u32[]{:S(2)}) collective-permute-start(f32[2,64,128]{2,1,0:T(8,128)S(1)} %pad_maximum_fusion.2), channel_id=1, source_target_pairs={{0,2},{1,3},{2,0},{3,1},{4,6},{5,7},{6,4},{7,5},{8,10},{9,11},{10,... | collective-permute-start | bytes 196616 | tf_op jit(solution)/shard_map/ppermute | solution.py:565
  22.1 66.1 %collective-permute-start = (f32[32,64,128]{2,1,0:T(8,128)S(1)}, f32[32,64,128]{2,1,0:T(8,128)S(1)}, u32[]{:S(2)}, u32[]{:S(2)}) collective-permute-start(f32[32,64,128]{2,1,0:T(8,128)S(1)} %chol_tail.1.low_ref.own_ref), channel_id=1, source_target_pairs={{0,1},{1,0},{2,3},{3,2},{4,5},{5,4},{6,7},{7,6},{8,9},{9,8},{10,11... | collective-permute-start | bytes 3145736 | tf_op jit(solution)/shard_map/ppermute | solution.py:587
  22.2 66.0 %collective-permute-start.1 = (f32[32,64,128]{2,1,0:T(8,128)S(1)}, f32[32,64,128]{2,1,0:T(8,128)S(1)}, u32[]{:S(2)}, u32[]{:S(2)}) collective-permute-start(f32[32,64,128]{2,1,0:T(8,128)S(1)} %chol_tail.1.low_ref.own_ref), channel_id=1, source_target_pairs={{1,2},{3,4},{5,6},{7,8},{9,10},{11,12},{13,14},{15,16},{17,18},{19... | collective-permute-start | bytes 3145736 | tf_op jit(solution)/shard_map/ppermute | solution.py:589
  30.2 23.6 %collective-permute-start.4 = (f32[4,64,128]{2,1,0:T(8,128)}, f32[4,64,128]{2,1,0:T(8,128)S(1)}, u32[]{:S(2)}, u32[]{:S(2)}) collective-permute-start(f32[4,64,128]{2,1,0:T(8,128)} %pad_maximum_fusion), channel_id=1, source_target_pairs={{0,4},{1,5},{2,6},{3,7},{4,8},{5,9},{6,10},{7,11},{8,12},{9,13},{1... | collective-permute-start | bytes 393224 | tf_op jit(solution)/shard_map/ppermute | solution.py:565
  30.2 28.7 %collective-permute-start.5 = (f32[4,64,128]{2,1,0:T(8,128)}, f32[4,64,128]{2,1,0:T(8,128)}, u32[]{:S(2)}, u32[]{:S(2)}) collective-permute-start(f32[4,64,128]{2,1,0:T(8,128)} %pad_maximum_fusion), channel_id=1, source_target_pairs={{0,8},{1,9},{2,10},{3,11},{4,12},{5,13},{6,14},{7,15},{8,0},{9,1},... | collective-permute-start | bytes 393224 | tf_op jit(solution)/shard_map/ppermute | solution.py:565
  30.2 28.7 %collective-permute-start.6 = (f32[4,64,128]{2,1,0:T(8,128)}, f32[4,64,128]{2,1,0:T(8,128)}, u32[]{:S(2)}, u32[]{:S(2)}) collective-permute-start(f32[4,64,128]{2,1,0:T(8,128)} %pad_maximum_fusion), channel_id=1, source_target_pairs={{0,12},{1,13},{2,14},{3,15},{4,0},{5,1},{6,2},{7,3},{8,4},{9,5},{1... | collective-permute-start | bytes 393224 | tf_op jit(solution)/shard_map/ppermute | solution.py:565
  39.1 2.0 %copy-start.1 = (bf16[128,64,256]{2,1,0:T(8,128)(2,1)}, bf16[128,64,256]{2,1,0:T(8,128)(2,1)S(1)}, u32[]{:S(2)}) copy-start(bf16[128,64,256]{2,1,0:T(8,128)(2,1)S(1)} %shard_map.85.y_ref) | copy-start | bytes 12582916
  65.7 10.8 %copy-start.5 = (s32[512]{0:T(512)S(1)}, s32[512]{0:T(512)}, u32[]{:S(2)}) copy-start(s32[512]{0:T(512)} %param.9) | copy-start | bytes 6148
  65.7 16.2 %copy-start.6 = (s32[16]{0:T(128)S(1)}, s32[16]{0:T(128)}, u32[]{:S(2)}) copy-start(s32[16]{0:T(128)} %param.11) | copy-start | bytes 196
  65.8 9.5 %collective-permute-start.7 = (f32[64,128]{1,0:T(8,128)S(1)}, f32[64,128]{1,0:T(8,128)S(1)}, u32[]{:S(2)}, u32[]{:S(2)}) collective-permute-start(f32[64,128]{1,0:T(8,128)S(1)} %get-tuple-element.11.l0), channel_id=1, source_target_pairs={{0,16},{16,0},{32,48},{48,32},{64,80},{80,64},{96,112},{112,96},{1... | collective-permute-start | bytes 98312 | tf_op jit(solution)/shard_map/ppermute | solution.py:565
  73.2 2.0 %copy-start.3 = (bf16[128,64,256]{2,1,0:T(8,128)(2,1)}, bf16[128,64,256]{2,1,0:T(8,128)(2,1)S(1)}, u32[]{:S(2)}) copy-start(bf16[128,64,256]{2,1,0:T(8,128)(2,1)S(1)} %shard_map.86.y_ref) | copy-start | bytes 12582916
  75.3 3.7 %collective-permute-start.8 = (f32[2,64,128]{2,1,0:T(8,128)S(1)}, f32[2,64,128]{2,1,0:T(8,128)S(1)}, u32[]{:S(2)}, u32[]{:S(2)}) collective-permute-start(f32[2,64,128]{2,1,0:T(8,128)S(1)} %pad_maximum_fusion.3), channel_id=1, source_target_pairs={{0,32},{16,48},{32,0},{48,16},{64,96},{80,112},{96,64},{112,80},{1... | collective-permute-start | bytes 196616 | tf_op jit(solution)/shard_map/ppermute | solution.py:565
  79.0 5.9 %collective-permute-start.9 = (f32[4,64,128]{2,1,0:T(8,128)S(1)}, f32[4,64,128]{2,1,0:T(8,128)S(1)}, u32[]{:S(2)}, u32[]{:S(2)}) collective-permute-start(f32[4,64,128]{2,1,0:T(8,128)S(1)} %pad_maximum_fusion.1), channel_id=1, source_target_pairs={{0,64},{16,80},{32,96},{48,112},{64,0},{80,16},{96,32},{112,48},{1... | collective-permute-start | bytes 393224 | tf_op jit(solution)/shard_map/ppermute | solution.py:565
  84.9 1.0 %copy-start = (f32[64,64,16]{1,2,0:T(8,128)S(1)}, f32[64,64,16]{1,2,0:T(8,128)}, u32[]{:S(2)}) copy-start(f32[64,64,16]{1,2,0:T(8,128)} %param.10) | copy-start | bytes 786436
  88.2 2.2 %copy-start.4 = (bf16[128,64,256]{2,1,0:T(8,128)(2,1)S(1)}, bf16[128,64,256]{2,1,0:T(8,128)(2,1)}, u32[]{:S(2)}) copy-start(bf16[128,64,256]{2,1,0:T(8,128)(2,1)} %copy-done.3) | copy-start | bytes 12582916
  90.4 6.6 %copy-start.2 = (bf16[128,64,256]{2,1,0:T(8,128)(2,1)S(1)}, bf16[128,64,256]{2,1,0:T(8,128)(2,1)}, u32[]{:S(2)}) copy-start(bf16[128,64,256]{2,1,0:T(8,128)(2,1)} %copy-done.1) | copy-start | bytes 12582916

commit v3 on v2

--- a/solution.py
+++ b/solution.py
@@ -262,33 +262,65 @@
     )(gram)
 
 
-def chol_tail_kernel(i_ref, low_ref, a_ref, u_ref):
+def chol_tail_kernel(i_ref, low_ref, pack_ref, a_ref, u_ref, v_ref):
     a_ref[...] = i_ref[...]
     chol_lanes(a_ref, range(EARLY, 8))
-
-    def store(s, _):
+    below = lax.broadcasted_iota(jnp.int32, (32, 128), 0)
+
+    def paired(x):
+        return rows(x, pltpu.roll(x, 96, 1)).T[0:32]
+
+    def gather(s):
         at = pl.ds(pl.multiple_of(s * 8, 8), 8)
         for g in range(8):
             u_ref[:, 8 * g : 8 * g + 8, :] = jnp.swapaxes(a_ref[8 * g : 8 * g + 8, at, :], 0, 1)
+
+    def spread(ref, to, s):
+        at = pl.ds(pl.multiple_of(s * 8, 8), 8)
+        for g in range(4):
+            to[8 * g : 8 * g + 8, at, :] = jnp.swapaxes(ref[:, 8 * g : 8 * g + 8, :], 0, 1)
+
+    def upper(s, _):
+        gather(s)
         for r in range(8):
-            x = u_ref[r]
-            u_ref[r, 0:32, :] = rows(x, pltpu.roll(x, 96, 1)).T[0:32]
-        for g in range(4):
-            low_ref[8 * g : 8 * g + 8, at, :] = jnp.swapaxes(u_ref[:, 8 * g : 8 * g + 8, :], 0, 1)
-        return 0
-
-    lax.fori_loop(0, 8, store, 0)
+            v_ref[r] = paired(u_ref[r])
+        spread(v_ref, low_ref, s)
+        return 0
+
+    def lower(s, _):
+        gather(s + 4)
+        for r in range(8):
+            v_ref[r] = paired(u_ref[r])
+        spread(v_ref, low_ref, s + 4)
+        for r in range(8):
+            a = s * 8 + r
+            free = jnp.where(below <= a, u_ref[r, 32:64, :], a_ref[a, 0:32, :])
+            v_ref[r] = paired(rows(u_ref[r, 0:32, :], free))
+        spread(v_ref, pack_ref, s)
+        return 0
+
+    lax.fori_loop(0, 4, upper, 0)
+    lax.fori_loop(0, 4, lower, 0)
+    diagonal = rows(*[a_ref[b, b : b + 1, :] for b in range(32)])
+    pack_ref[32] = paired(rows(jnp.zeros((32, 128), F32), diagonal))
 
 
 def chol_tail(part):
     return pl.pallas_call(
         chol_tail_kernel,
-        out_shape=jax.ShapeDtypeStruct((32, 64, 128), F32),
+        out_shape=(
+            jax.ShapeDtypeStruct((32, 64, 128), F32),
+            jax.ShapeDtypeStruct((33, 32, 128), F32),
+        ),
         in_specs=[VMEM],
-        out_specs=VMEM,
-        scratch_shapes=[pltpu.VMEM((64, 64, 128), F32), pltpu.VMEM((8, 64, 128), F32)],
-        compiler_params=params(8),
-        cost_estimate=cost(4),
+        out_specs=(VMEM, VMEM),
+        scratch_shapes=[
+            pltpu.VMEM((64, 64, 128), F32),
+            pltpu.VMEM((8, 64, 128), F32),
+            pltpu.VMEM((8, 32, 128), F32),
+        ],
+        compiler_params=params(10),
+        cost_estimate=cost(5),
         name="chol_tail",
     )(part)
 
@@ -352,16 +384,48 @@
 def prep_kernel(odd_ref, near_ref, own_ref, far_ref, d_ref):
     first = first_half()
     odd = odd_ref[0]
-    for base, ref in ((64, own_ref), (128 - 128 * odd, near_ref), (128 * odd, far_ref)):
-
-        def pair(q, _, ref=ref, base=base):
-            x = ref[q]
-            y = pltpu.roll(x, 64, 1)
-            d_ref[base + q] = right_of(jnp.where(first, x, y))
-            d_ref[base + 32 + q] = right_of(jnp.where(first, y, x))
+
+    def plain(q, _):
+        x = own_ref[q]
+        y = pltpu.roll(x, 64, 1)
+        d_ref[64 + q] = right_of(jnp.where(first, x, y))
+        d_ref[96 + q] = right_of(jnp.where(first, y, x))
+        return 0
+
+    lax.fori_loop(0, 32, plain, 0, unroll=8)
+    half = first[0:32]
+    row = lax.broadcasted_iota(jnp.int32, (32, 128), 0)
+    col = lax.broadcasted_iota(jnp.int32, (32, 128), 1) % 64 - 32
+    for base, ref in ((128 - 128 * odd, near_ref), (128 * odd, far_ref)):
+
+        def packed(s, _, ref=ref, base=base):
+            qs = [s * 4 + j for j in range(4)]
+            ups = []
+            for q in qs:
+                diagonal = ref[32, pl.ds(q, 32, stride=0), :]
+                rest = jnp.where(col == row, diagonal, 0.0)
+                ups.append(jnp.where(col > row, ref[q], rest))
+            turned = rows(*ups).T
+            shifts = [
+                [turned[64 * c + 32 : 64 * c + 64]]
+                + [
+                    pltpu.roll(turned[64 * c + 32 : 64 * c + 64], 32 * n, 1)
+                    for n in range(1, 4)
+                ]
+                for c in range(2)
+            ]
+            for j, q in enumerate(qs):
+                x = jnp.where(col <= row, ref[q], 0.0)
+                y = pltpu.roll(x, 64, 1)
+                for c in range(2):
+                    at = shifts[c]
+                    top = jnp.where(half, at[(4 - j) % 4], at[(6 - j) % 4])
+                    top = jnp.where(col < 0, top, 0.0)
+                    low = jnp.where(half, x, y) if c == 0 else jnp.where(half, y, x)
+                    d_ref[base + 32 * c + q] = right_of(rows(top, low))
             return 0
 
-        lax.fori_loop(0, 32, pair, 0, unroll=8)
+        lax.fori_loop(0, 8, packed, 0, unroll=2)
 
 
 def prep(odd, near, own, far):
@@ -580,13 +644,13 @@
     head = chol_head(gram)
     pair = jnp.stack([pay, pay_a])
     pay_b = shifted(pair, "narrow", lambda i: i ^ 2)
-    low = chol_tail(head)
+    low, pack = chol_tail(head)
     quad = jnp.concatenate([pair, pay_b])
     pay_c = [shifted(quad, "narrow", lambda i, s=s: (i + 4 * s) % 16) for s in (1, 2, 3)]
     count = lax.axis_size(both)
-    low_near = lax.ppermute(low, both, [(i, i ^ 1) for i in range(count)])
+    low_near = lax.ppermute(pack, both, [(i, i ^ 1) for i in range(count)])
     later = [(i, i + 1) for i in range(1, count - 1, 2)]
-    low_far = lax.ppermute(low, both, later + [(j, i) for i, j in later])
+    low_far = lax.ppermute(pack, both, later + [(j, i) for i, j in later])
     half_a = half_leaf(leaf_coupling, low, 0)
     half_b = half_leaf(leaf_coupling, low, 1)
     ones = 1 + sum((at % 2**k == 2**k - 1).astype(jnp.int32) for k in range(1, 5))

time: 104 us -> 92.9 us (0.89)
  waiting for transfers between devices: 23.1 us -> 10.9 us
  Pallas kernels: 53 us -> 54.6 us
  local copies, waits for them, and re-layouts: 5.32 us -> 3.97 us
    ppermute x8, waiting for transfers between devices: 23.1 us -> 10.9 us  [shifted(): lax.ppermute(value, axis, [(i, to(i)) for i in range(lax.axis_size(axis))])]
    unnamed x14, local copies, waits for them, and re-layouts: 5.32 us -> 3.97 us
  transfers between devices with their start and end apart: 10 -> 10, of which waited for: 4 -> 4; matrix products, arithmetic and copies ran while one was open for 1% -> 0% of each run, Pallas kernels for 28% -> 32%
where the time goes in v3:
time: 92.9 us; the launch traced here: 91.9 us
  Pallas kernels  54.6 us (59%)
  starting transfers between devices  21.3 us (23%)
  waiting for transfers between devices  10.9 us (12%)
  local copies, waits for them, and re-layouts  3.97 us (4%)
  between operations  0.96 us (1%)
    ppermute x8, starting transfers between devices, shifted(): lax.ppermute(value, axis, [(i, to(i)) for i in range(lax.axis_size(axis))])  13.9 us
    pallas_call x2, Pallas kernels, full_leaf(): pl.pallas_call(functools.partial(full_kernel, part=part), out_shape=jax.S...  13.2 us
    pallas_call x2, Pallas kernels, half_leaf(): pl.pallas_call(functools.partial(half_kernel, part=part), out_shape=jax.S...  12.4 us
    ppermute x8, waiting for transfers between devices, shifted(): lax.ppermute(value, axis, [(i, to(i)) for i in range(lax.axis_size(axis))])  10.9 us
    pallas_call x1, Pallas kernels, climb(): pl.pallas_call(climb_kernel, out_shape=(jax.ShapeDtypeStruct((32, 64, 128...  9.22 us
    ppermute x1, starting transfers between devices, steps(): low_far = lax.ppermute(pack, both, later + [(j, i) for i, j in later])  7.39 us
    pallas_call x1, Pallas kernels, branch(): pl.pallas_call(branch_kernel, out_shape=(jax.ShapeDtypeStruct((1, 64, 64)...  6.37 us
    pallas_call x1, Pallas kernels, chol_tail(): pl.pallas_call(chol_tail_kernel, out_shape=(jax.ShapeDtypeStruct((32, 64,...  5.49 us
  transfers between devices with their start and end apart: 10, of which 4 were waited for; matrix products, arithmetic and copies ran while one was open for 0% of the time, Pallas kernels for 32%

profile of v3, /device:TPU:1, one launch (start us, length us, event | category | flops | bytes accessed | tf_op | source)
XLA Modules:
  0.0 91.9 jit_solution(14464737053585926450)
XLA Ops:
  0.6 9.2 %climb.1 = (f32[32,64,128]{2,1,0:T(8,128)S(1)}, f32[64,128]{1,0:T(8,128)S(1)}, f32[64,128]{1,0:T(8,128)S(1)}) custom-call(bf16[64,64,256]{2,1,0:T(8,128)(2,1)} %b_hbm.1, f32[64,64,128]{2,1,0:T(8,128)} %t_hbm.1), custom_call_target="tpu_custom_call" | custom-call | flops 11500000256 | bytes 4096 | tf_op jit(solution)/shard_map/climb/pallas_call | solution.py:166
  9.9 2.2 %collective-permute-start.2 = (f32[64,128]{1,0:T(8,128)S(1)}, f32[64,128]{1,0:T(8,128)S(1)}, u32[]{:S(2)}, u32[]{:S(2)}) collective-permute-start(f32[64,128]{1,0:T(8,128)S(1)} %get-tuple-element.13.p0), channel_id=1, source_target_pairs={{0,1},{1,0},{2,3},{3,2},{4,5},{5,4},{6,7},{7,6},{8,9},{9,8},{10,11... | collective-permute-start | bytes 98312 | tf_op jit(solution)/shard_map/ppermute | solution.py:629
  12.1 2.8 %chol_head.1.i_ref = f32[64,64,128]{2,1,0:T(8,128)S(1)} custom-call(f32[32,64,128]{2,1,0:T(8,128)S(1)} %get-tuple-element.10.g_ref), custom_call_target="tpu_custom_call" | custom-call | flops 4600000000 | bytes 4096 | tf_op jit(solution)/shard_map/chol_head/pallas_call | solution.py:253
  14.8 0.0 collective-permute-done.2.p1
  14.9 2.7 %collective-permute-start.3 = (f32[2,64,128]{2,1,0:T(8,128)S(1)}, f32[2,64,128]{2,1,0:T(8,128)S(1)}, u32[]{:S(2)}, u32[]{:S(2)}) collective-permute-start(f32[2,64,128]{2,1,0:T(8,128)S(1)} %pad_maximum_fusion.2), channel_id=1, source_target_pairs={{0,2},{1,3},{2,0},{3,1},{4,6},{5,7},{6,4},{7,5},{8,10},{9,11},{10,... | collective-permute-start | bytes 196616 | tf_op jit(solution)/shard_map/ppermute | solution.py:629
  17.6 5.5 %chol_tail.1 = (f32[32,64,128]{2,1,0:T(8,128)S(1)}, f32[33,32,128]{2,1,0:T(8,128)S(1)}) custom-call(f32[64,64,128]{2,1,0:T(8,128)S(1)} %chol_head.1.i_ref), custom_call_target="tpu_custom_call" | custom-call | flops 5750000128 | bytes 4096 | tf_op jit(solution)/shard_map/chol_tail/pallas_call | solution.py:309
  23.1 0.1 collective-permute-start
  23.1 7.4 %collective-permute-start.1 = (f32[33,32,128]{2,1,0:T(8,128)S(1)}, f32[33,32,128]{2,1,0:T(8,128)S(1)}, u32[]{:S(2)}, u32[]{:S(2)}) collective-permute-start(f32[33,32,128]{2,1,0:T(8,128)S(1)} %get-tuple-element.12), channel_id=1, source_target_pairs={{1,2},{3,4},{5,6},{7,8},{9,10},{11,12},{13,14},{15,16},{17,18},{19... | collective-permute-start | bytes 1622024 | tf_op jit(solution)/shard_map/ppermute | solution.py:653
  30.5 0.0 collective-permute-done.3.p2
  30.6 0.1 collective-permute-start.4
  30.6 0.1 collective-permute-start.5
  30.7 2.6 %collective-permute-start.6 = (f32[4,64,128]{2,1,0:T(8,128)S(1)}, f32[4,64,128]{2,1,0:T(8,128)S(1)}, u32[]{:S(2)}, u32[]{:S(2)}) collective-permute-start(f32[4,64,128]{2,1,0:T(8,128)S(1)} %pad_maximum_fusion), channel_id=1, source_target_pairs={{0,12},{1,13},{2,14},{3,15},{4,0},{5,1},{6,2},{7,3},{8,4},{9,5},{1... | collective-permute-start | bytes 393224 | tf_op jit(solution)/shard_map/ppermute | solution.py:629
  33.3 6.2 %shard_map.85.y_ref = bf16[128,64,256]{2,1,0:T(8,128)(2,1)S(1)} custom-call(f32[64,64,512]{2,1,0:T(8,128)} %c1_ref.3, f32[64,64,512]{2,1,0:T(8,128)} %c1_ref.3, f32[32,64,128]{2,1,0:T(8,128)S(1)} %get-tuple-element.11.low_ref.own_ref), custom_call_target="tpu_custom_call" | custom-call | flops 6899999744 | bytes 4096 | tf_op jit(solution)/shard_map/pallas_call | solution.py:368
  39.5 0.0 copy-start.1
  39.5 1.9 %copy-done.1 = bf16[128,64,256]{2,1,0:T(8,128)(2,1)} copy-done((bf16[128,64,256]{2,1,0:T(8,128)(2,1)}, bf16[128,64,256]{2,1,0:T(8,128)(2,1)S(1)}, u32[]{:S(2)}) %copy-start.1) | copy-done | bytes 4194328
  41.5 0.1 pad_add_fusion.at_ref
  41.6 2.2 %collective-permute-done.4.p3 = f32[4,64,128]{2,1,0:T(8,128)S(1)} collective-permute-done((f32[4,64,128]{2,1,0:T(8,128)S(1)}, f32[4,64,128]{2,1,0:T(8,128)S(1)}, u32[]{:S(2)}, u32[]{:S(2)}) %collective-permute-start.4) | collective-permute-done | bytes 131104 | tf_op jit(solution)/shard_map/ppermute | solution.py:629
  43.8 4.0 %collective-permute-done.5.p4 = f32[4,64,128]{2,1,0:T(8,128)S(1)} collective-permute-done((f32[4,64,128]{2,1,0:T(8,128)S(1)}, f32[4,64,128]{2,1,0:T(8,128)S(1)}, u32[]{:S(2)}, u32[]{:S(2)}) %collective-permute-start.5) | collective-permute-done | bytes 131104 | tf_op jit(solution)/shard_map/ppermute | solution.py:629
  47.8 0.0 collective-permute-done.6.p5
  47.8 6.4 %branch.1 = (f32[1,64,64]{2,1,0:T(8,128)}, f32[64,128]{1,0:T(8,128)S(1)}) custom-call(s32[2]{0:T(128)S(1)} %pad_add_fusion.at_ref, f32[64,128]{1,0:T(8,128)S(1)} %get-tuple-element.13.p0, f32[64,128]{1,0:T(8,128)S(1)} %collective-permute-done.2.p1, f32[2,64,128]{2,1,0:T(8,128)S(1)} %collective-permute-done.3.p2, ...), custom_call_target="tpu_custom_call" | custom-call | flops 5750000128 | bytes 4096 | tf_op jit(solution)/shard_map/branch/pallas_call | solution.py:569
  54.2 0.0 copy-start.5
  54.2 0.0 copy-start.6
  54.2 0.0 copy-start
  54.2 1.7 %collective-permute-start.7 = (f32[64,128]{1,0:T(8,128)S(1)}, f32[64,128]{1,0:T(8,128)S(1)}, u32[]{:S(2)}, u32[]{:S(2)}) collective-permute-start(f32[64,128]{1,0:T(8,128)S(1)} %get-tuple-element.15.l0), channel_id=1, source_target_pairs={{0,16},{16,0},{32,48},{48,32},{64,80},{80,64},{96,112},{112,96},{1... | collective-permute-start | bytes 98312 | tf_op jit(solution)/shard_map/ppermute | solution.py:629
  55.9 6.2 %shard_map.86.y_ref = bf16[128,64,256]{2,1,0:T(8,128)(2,1)S(1)} custom-call(f32[64,64,512]{2,1,0:T(8,128)} %c1_ref.3, f32[64,64,512]{2,1,0:T(8,128)} %c1_ref.3, f32[32,64,128]{2,1,0:T(8,128)S(1)} %get-tuple-element.11.low_ref.own_ref), custom_call_target="tpu_custom_call" | custom-call | flops 6899999744 | bytes 4096 | tf_op jit(solution)/shard_map/pallas_call | solution.py:368
  62.1 0.0 copy-start.3
  62.1 2.0 %copy-done.3 = bf16[128,64,256]{2,1,0:T(8,128)(2,1)} copy-done((bf16[128,64,256]{2,1,0:T(8,128)(2,1)}, bf16[128,64,256]{2,1,0:T(8,128)(2,1)S(1)}, u32[]{:S(2)}) %copy-start.3) | copy-done | bytes 4194328
  64.1 0.0 collective-permute-done.7.l1
  64.1 1.4 %collective-permute-start.8 = (f32[2,64,128]{2,1,0:T(8,128)S(1)}, f32[2,64,128]{2,1,0:T(8,128)S(1)}, u32[]{:S(2)}, u32[]{:S(2)}) collective-permute-start(f32[2,64,128]{2,1,0:T(8,128)S(1)} %pad_maximum_fusion.3), channel_id=1, source_target_pairs={{0,32},{16,48},{32,0},{48,16},{64,96},{80,112},{96,64},{112,80},{1... | collective-permute-start | bytes 196616 | tf_op jit(solution)/shard_map/ppermute | solution.py:629
  65.5 0.0 copy-done.5
  65.6 2.2 %collective-permute-done.8.l2 = f32[2,64,128]{2,1,0:T(8,128)S(1)} collective-permute-done((f32[2,64,128]{2,1,0:T(8,128)S(1)}, f32[2,64,128]{2,1,0:T(8,128)S(1)}, u32[]{:S(2)}, u32[]{:S(2)}) %collective-permute-start.8) | collective-permute-done | bytes 65568 | tf_op jit(solution)/shard_map/ppermute | solution.py:629
  67.8 3.1 %collective-permute-start.9 = (f32[4,64,128]{2,1,0:T(8,128)S(1)}, f32[4,64,128]{2,1,0:T(8,128)S(1)}, u32[]{:S(2)}, u32[]{:S(2)}) collective-permute-start(f32[4,64,128]{2,1,0:T(8,128)S(1)} %pad_maximum_fusion.1), channel_id=1, source_target_pairs={{0,64},{16,80},{32,96},{48,112},{64,0},{80,16},{96,32},{112,48},{1... | collective-permute-start | bytes 393224 | tf_op jit(solution)/shard_map/ppermute | solution.py:629
  70.8 0.0 copy-done.6
  70.9 2.5 %collective-permute-done.9.l3 = f32[4,64,128]{2,1,0:T(8,128)S(1)} collective-permute-done((f32[4,64,128]{2,1,0:T(8,128)S(1)}, f32[4,64,128]{2,1,0:T(8,128)S(1)}, u32[]{:S(2)}, u32[]{:S(2)}) %collective-permute-start.9) | collective-permute-done | bytes 131104 | tf_op jit(solution)/shard_map/ppermute | solution.py:629
  73.3 0.0 copy-done
  73.3 2.2 %far.1 = f32[64,16,64]{2,1,0:T(8,128)} custom-call(s32[16]{0:T(128)S(1)} %broadcast_xor_fusion.cols_ref, f32[64,16,64]{2,1,0:T(8,128)S(1)} %bitcast.16, f32[64,128]{1,0:T(8,128)S(1)} %get-tuple-element.15.l0, f32[64,128]{1,0:T(8,128)S(1)} %collective-permute-done.7.l1, f32[2,64,128]{2,1,0:T(8,128)S(1)} %collective-permute-done.8.l2, ...), custom_call_target="tpu_custom_call" | custom-call | flops 3449999872 | bytes 4096 | tf_op jit(solution)/shard_map/far/pallas_call | solution.py:616
  75.5 0.0 copy-start.4
  75.5 0.0 collective-permute-done.near_ref
  75.6 0.0 collective-permute-done.1.far_ref
  75.6 2.8 %prep.1.d_ref = bf16[192,64,256]{2,1,0:T(8,128)(2,1)S(1)} custom-call(s32[1]{0:T(128)S(6)} %select_n.29.odd_ref, f32[33,32,128]{2,1,0:T(8,128)S(1)} %collective-permute-done.near_ref, f32[32,64,128]{2,1,0:T(8,128)S(1)} %get-tuple-element.11.low_ref.own_ref, f32[33,32,128]{2,1,0:T(8,128)S(1)} %collective-permute-done.1.far_ref), custom_call_target="tpu_custom_call" | custom-call | flops 3449999872 | bytes 4096 | tf_op jit(solution)/shard_map/prep/pallas_call | solution.py:432
  78.4 0.0 copy-done.4
  78.4 0.0 copy-start.2
  78.4 6.6 %shard_map.87.refs_0_ = f32[64,64,512]{2,1,0:T(8,128)} custom-call(s32[512]{0:T(512)S(1)} %broadcast_subtract_fusion.cols_ref, bf16[128,64,256]{2,1,0:T(8,128)(2,1)S(1)} %copy-done.4, bf16[192,64,256]{2,1,0:T(8,128)(2,1)S(1)} %prep.1.d_ref), custom_call_target="tpu_custom_call" | custom-call | flops 9200000000 | bytes 4096 | tf_op jit(solution)/shard_map/pallas_call | solution.py:495
  85.1 0.0 copy-done.2
  85.1 6.6 %shard_map.88 = f32[64,64,512]{2,1,0:T(8,128)} custom-call(s32[512]{0:T(512)S(1)} %broadcast_subtract_fusion.cols_ref, bf16[128,64,256]{2,1,0:T(8,128)(2,1)S(1)} %copy-done.2, bf16[192,64,256]{2,1,0:T(8,128)(2,1)S(1)} %prep.1.d_ref, f32[64,64,512]{2,1,0:T(8,128)} %shard_map.87.refs_0_), custom_call_target="tpu_custom_call", output_to_operand_aliasing={{}: (3, {})} | custom-call | flops 9200000000 | bytes 4096 | tf_op jit(solution)/shard_map/pallas_call | solution.py:495
  (6 shorter events, 0.0 us)
Async XLA Ops:
  9.9 5.0 %collective-permute-start.2 = (f32[64,128]{1,0:T(8,128)S(1)}, f32[64,128]{1,0:T(8,128)S(1)}, u32[]{:S(2)}, u32[]{:S(2)}) collective-permute-start(f32[64,128]{1,0:T(8,128)S(1)} %get-tuple-element.13.p0), channel_id=1, source_target_pairs={{0,1},{1,0},{2,3},{3,2},{4,5},{5,4},{6,7},{7,6},{8,9},{9,8},{10,11... | collective-permute-start | bytes 98312 | tf_op jit(solution)/shard_map/ppermute | solution.py:629
  14.9 15.7 %collective-permute-start.3 = (f32[2,64,128]{2,1,0:T(8,128)S(1)}, f32[2,64,128]{2,1,0:T(8,128)S(1)}, u32[]{:S(2)}, u32[]{:S(2)}) collective-permute-start(f32[2,64,128]{2,1,0:T(8,128)S(1)} %pad_maximum_fusion.2), channel_id=1, source_target_pairs={{0,2},{1,3},{2,0},{3,1},{4,6},{5,7},{6,4},{7,5},{8,10},{9,11},{10,... | collective-permute-start | bytes 196616 | tf_op jit(solution)/shard_map/ppermute | solution.py:629
  23.1 52.5 %collective-permute-start = (f32[33,32,128]{2,1,0:T(8,128)S(1)}, f32[33,32,128]{2,1,0:T(8,128)S(1)}, u32[]{:S(2)}, u32[]{:S(2)}) collective-permute-start(f32[33,32,128]{2,1,0:T(8,128)S(1)} %get-tuple-element.12), channel_id=1, source_target_pairs={{0,1},{1,0},{2,3},{3,2},{4,5},{5,4},{6,7},{7,6},{8,9},{9,8},{10,11... | collective-permute-start | bytes 1622024 | tf_op jit(solution)/shard_map/ppermute | solution.py:651
  23.1 52.4 %collective-permute-start.1 = (f32[33,32,128]{2,1,0:T(8,128)S(1)}, f32[33,32,128]{2,1,0:T(8,128)S(1)}, u32[]{:S(2)}, u32[]{:S(2)}) collective-permute-start(f32[33,32,128]{2,1,0:T(8,128)S(1)} %get-tuple-element.12), channel_id=1, source_target_pairs={{1,2},{3,4},{5,6},{7,8},{9,10},{11,12},{13,14},{15,16},{17,18},{19... | collective-permute-start | bytes 1622024 | tf_op jit(solution)/shard_map/ppermute | solution.py:653
  30.6 13.2 %collective-permute-start.4 = (f32[4,64,128]{2,1,0:T(8,128)S(1)}, f32[4,64,128]{2,1,0:T(8,128)S(1)}, u32[]{:S(2)}, u32[]{:S(2)}) collective-permute-start(f32[4,64,128]{2,1,0:T(8,128)S(1)} %pad_maximum_fusion), channel_id=1, source_target_pairs={{0,4},{1,5},{2,6},{3,7},{4,8},{5,9},{6,10},{7,11},{8,12},{9,13},{1... | collective-permute-start | bytes 393224 | tf_op jit(solution)/shard_map/ppermute | solution.py:629
  30.6 17.2 %collective-permute-start.5 = (f32[4,64,128]{2,1,0:T(8,128)S(1)}, f32[4,64,128]{2,1,0:T(8,128)S(1)}, u32[]{:S(2)}, u32[]{:S(2)}) collective-permute-start(f32[4,64,128]{2,1,0:T(8,128)S(1)} %pad_maximum_fusion), channel_id=1, source_target_pairs={{0,8},{1,9},{2,10},{3,11},{4,12},{5,13},{6,14},{7,15},{8,0},{9,1},... | collective-permute-start | bytes 393224 | tf_op jit(solution)/shard_map/ppermute | solution.py:629
  30.7 17.1 %collective-permute-start.6 = (f32[4,64,128]{2,1,0:T(8,128)S(1)}, f32[4,64,128]{2,1,0:T(8,128)S(1)}, u32[]{:S(2)}, u32[]{:S(2)}) collective-permute-start(f32[4,64,128]{2,1,0:T(8,128)S(1)} %pad_maximum_fusion), channel_id=1, source_target_pairs={{0,12},{1,13},{2,14},{3,15},{4,0},{5,1},{6,2},{7,3},{8,4},{9,5},{1... | collective-permute-start | bytes 393224 | tf_op jit(solution)/shard_map/ppermute | solution.py:629
  39.5 2.0 %copy-start.1 = (bf16[128,64,256]{2,1,0:T(8,128)(2,1)}, bf16[128,64,256]{2,1,0:T(8,128)(2,1)S(1)}, u32[]{:S(2)}) copy-start(bf16[128,64,256]{2,1,0:T(8,128)(2,1)S(1)} %shard_map.85.y_ref) | copy-start | bytes 12582916
  54.2 11.4 %copy-start.5 = (s32[512]{0:T(512)S(1)}, s32[512]{0:T(512)}, u32[]{:S(2)}) copy-start(s32[512]{0:T(512)} %param.9) | copy-start | bytes 6148
  54.2 16.7 %copy-start.6 = (s32[16]{0:T(128)S(1)}, s32[16]{0:T(128)}, u32[]{:S(2)}) copy-start(s32[16]{0:T(128)} %param.11) | copy-start | bytes 196
  54.2 19.2 %copy-start = (f32[64,64,16]{1,2,0:T(8,128)S(1)}, f32[64,64,16]{1,2,0:T(8,128)}, u32[]{:S(2)}) copy-start(f32[64,64,16]{1,2,0:T(8,128)} %param.10) | copy-start | bytes 786436
  54.2 9.9 %collective-permute-start.7 = (f32[64,128]{1,0:T(8,128)S(1)}, f32[64,128]{1,0:T(8,128)S(1)}, u32[]{:S(2)}, u32[]{:S(2)}) collective-permute-start(f32[64,128]{1,0:T(8,128)S(1)} %get-tuple-element.15.l0), channel_id=1, source_target_pairs={{0,16},{16,0},{32,48},{48,32},{64,80},{80,64},{96,112},{112,96},{1... | collective-permute-start | bytes 98312 | tf_op jit(solution)/shard_map/ppermute | solution.py:629
  62.1 2.0 %copy-start.3 = (bf16[128,64,256]{2,1,0:T(8,128)(2,1)}, bf16[128,64,256]{2,1,0:T(8,128)(2,1)S(1)}, u32[]{:S(2)}) copy-start(bf16[128,64,256]{2,1,0:T(8,128)(2,1)S(1)} %shard_map.86.y_ref) | copy-start | bytes 12582916
  64.1 3.6 %collective-permute-start.8 = (f32[2,64,128]{2,1,0:T(8,128)S(1)}, f32[2,64,128]{2,1,0:T(8,128)S(1)}, u32[]{:S(2)}, u32[]{:S(2)}) collective-permute-start(f32[2,64,128]{2,1,0:T(8,128)S(1)} %pad_maximum_fusion.3), channel_id=1, source_target_pairs={{0,32},{16,48},{32,0},{48,16},{64,96},{80,112},{96,64},{112,80},{1... | collective-permute-start | bytes 196616 | tf_op jit(solution)/shard_map/ppermute | solution.py:629
  67.8 5.6 %collective-permute-start.9 = (f32[4,64,128]{2,1,0:T(8,128)S(1)}, f32[4,64,128]{2,1,0:T(8,128)S(1)}, u32[]{:S(2)}, u32[]{:S(2)}) collective-permute-start(f32[4,64,128]{2,1,0:T(8,128)S(1)} %pad_maximum_fusion.1), channel_id=1, source_target_pairs={{0,64},{16,80},{32,96},{48,112},{64,0},{80,16},{96,32},{112,48},{1... | collective-permute-start | bytes 393224 | tf_op jit(solution)/shard_map/ppermute | solution.py:629
  75.5 2.9 %copy-start.4 = (bf16[128,64,256]{2,1,0:T(8,128)(2,1)S(1)}, bf16[128,64,256]{2,1,0:T(8,128)(2,1)}, u32[]{:S(2)}) copy-start(bf16[128,64,256]{2,1,0:T(8,128)(2,1)} %copy-done.3) | copy-start | bytes 12582916
  78.4 6.6 %copy-start.2 = (bf16[128,64,256]{2,1,0:T(8,128)(2,1)S(1)}, bf16[128,64,256]{2,1,0:T(8,128)(2,1)}, u32[]{:S(2)}) copy-start(bf16[128,64,256]{2,1,0:T(8,128)(2,1)} %copy-done.1) | copy-start | bytes 12582916

commit v4 on v3

--- a/solution.py
+++ b/solution.py
@@ -509,7 +509,7 @@
     )(cols, y, d, *extra)
 
 
-def branch_kernel(at_ref, p0, p1, p2, p3, p4, p5, top_ref, gf_ref, low_ref, t_ref, e_ref, n_ref, a_ref):
+def branch_kernel(at_ref, p0, p1, p2, p3, p4, top_ref, gf_ref, low_ref, t_ref, e_ref, n_ref, a_ref):
     at = at_ref[0]
     pick = at_ref[1]
     first = first_half()
@@ -521,11 +521,13 @@
 
     place(at, p0[...])
     place(at ^ 1, p1[...])
+    near = (0, 1, 3, 2)
     for i in range(2):
-        place(at ^ (2 + i), p2[i])
-    for s, ref in enumerate((p3, p4, p5)):
-        for i in range(4):
-            place((at ^ i) - 4 * (s + 1) & 15, ref[i])
+        place(at ^ near[2 + i], p2[i])
+    for i in range(4):
+        place(at ^ 4 ^ near[i], p3[i])
+    for i in range(8):
+        place(at ^ (12, 8)[i // 4] ^ near[i % 4], p4[i])
     n_ref[0] = top_ref[...]
     for m in range(8):
         n_ref[8 + m] = t_ref[2 * m] + t_ref[2 * m + 1]
@@ -572,7 +574,7 @@
             jax.ShapeDtypeStruct((1, 64, 64), F32),
             jax.ShapeDtypeStruct((64, 128), F32),
         ),
-        in_specs=[SMEM] + [VMEM] * 7,
+        in_specs=[SMEM] + [VMEM] * 6,
         out_specs=(VMEM, VMEM),
         scratch_shapes=[
             pltpu.VMEM((16, 64, 128), F32),
@@ -587,7 +589,7 @@
 
 
 def far_kernel(cols_ref, f_ref, l0, l1, l2, l3, o_ref, l_ref, c_ref):
-    for s, part in enumerate((l0[...], l1[...], l2[0], l2[1], l3[0], l3[1], l3[2], l3[3])):
+    for s, part in enumerate((l0[...], l1[...], l2[0], l2[1], l3[2], l3[3], l3[0], l3[1])):
         h, l = split(part[:, 0:64])
         l_ref[s] = rows(h, h, l)
     lh, ll = split(l0[...].T[0:64])
@@ -643,20 +645,22 @@
     pay_a = shifted(pay, "narrow", lambda i: i ^ 1)
     head = chol_head(gram)
     pair = jnp.stack([pay, pay_a])
-    pay_b = shifted(pair, "narrow", lambda i: i ^ 2)
+    pay_b = shifted(pair, "narrow", lambda i: i ^ 3)
     low, pack = chol_tail(head)
     quad = jnp.concatenate([pair, pay_b])
-    pay_c = [shifted(quad, "narrow", lambda i, s=s: (i + 4 * s) % 16) for s in (1, 2, 3)]
+    pay_c = shifted(quad, "narrow", lambda i: i ^ 4)
     count = lax.axis_size(both)
     low_near = lax.ppermute(pack, both, [(i, i ^ 1) for i in range(count)])
     later = [(i, i + 1) for i in range(1, count - 1, 2)]
     low_far = lax.ppermute(pack, both, later + [(j, i) for i, j in later])
     half_a = half_leaf(leaf_coupling, low, 0)
+    octet = jnp.concatenate([quad, pay_c])
+    pay_d = shifted(octet, "narrow", lambda i: i ^ 12)
     half_b = half_leaf(leaf_coupling, low, 1)
     ones = 1 + sum((at % 2**k == 2**k - 1).astype(jnp.int32) for k in range(1, 5))
     pick = jnp.where(ones <= 4, (16 + at) >> ones, 0)
     place = jnp.stack([at, pick]).astype(jnp.int32)
-    group_factors, own = branch(place, [pay, pay_a, pay_b, *pay_c], top)
+    group_factors, own = branch(place, [pay, pay_a, pay_b, pay_c, pay_d], top)
     own_a = shifted(own, "wide", lambda i: i ^ 1)
     factors = prep(at.reshape(1) % 2, low_near, low, low_far)
     two = jnp.stack([own, own_a])
@@ -664,7 +668,7 @@
     cols = leaf_columns - (lax.axis_index(both) * 64 - 64)
     out = full_leaf(cols, half_a, factors, 0)
     four = jnp.concatenate([two, own_b])
-    own_c = shifted(four, "wide", lambda i: i ^ 4)
+    own_c = shifted(four, "wide", lambda i: i ^ 6)
     leaf_coupled = full_leaf(cols, half_b, factors, 1, out)
     far_out = far(
         wide_at ^ far_columns,

time: 92.9 us -> 90.5 us (0.974)
  starting transfers between devices: 21.3 us -> 16.8 us
  waiting for transfers between devices: 10.9 us -> 13.9 us
    ppermute x8 -> x7, starting transfers between devices: 13.9 us -> 7.3 us  [shifted(): lax.ppermute(value, axis, [(i, to(i)) for i in range(lax.axis_size(axis))])]
    ppermute x8 -> x7, waiting for transfers between devices: 10.9 us -> 13.9 us  [shifted(): lax.ppermute(value, axis, [(i, to(i)) for i in range(lax.axis_size(axis))])]
    ppermute x1, starting transfers between devices: 7.39 us -> 9.38 us  [steps(): low_far = lax.ppermute(pack, both, later + [(j, i) for i, j in later])]
  transfers between devices with their start and end apart: 10 -> 9, of which waited for: 4 -> 3; matrix products, arithmetic and copies ran while one was open for 0% -> 0% of each run, Pallas kernels for 32% -> 48%
where the time goes in v4:
time: 90.5 us; the launch traced here: 90.3 us
  Pallas kernels  54.6 us (60%)
  starting transfers between devices  16.8 us (19%)
  waiting for transfers between devices  13.9 us (15%)
  local copies, waits for them, and re-layouts  3.98 us (4%)
    ppermute x7, waiting for transfers between devices, shifted(): lax.ppermute(value, axis, [(i, to(i)) for i in range(lax.axis_size(axis))])  13.9 us
    pallas_call x2, Pallas kernels, full_leaf(): pl.pallas_call(functools.partial(full_kernel, part=part), out_shape=jax.S...  13.4 us
    pallas_call x2, Pallas kernels, half_leaf(): pl.pallas_call(functools.partial(half_kernel, part=part), out_shape=jax.S...  12.4 us
    ppermute x1, starting transfers between devices, steps(): low_far = lax.ppermute(pack, both, later + [(j, i) for i, j in later])  9.38 us
    pallas_call x1, Pallas kernels, climb(): pl.pallas_call(climb_kernel, out_shape=(jax.ShapeDtypeStruct((32, 64, 128...  9.22 us
    ppermute x7, starting transfers between devices, shifted(): lax.ppermute(value, axis, [(i, to(i)) for i in range(lax.axis_size(axis))])  7.3 us
    pallas_call x1, Pallas kernels, branch(): pl.pallas_call(branch_kernel, out_shape=(jax.ShapeDtypeStruct((1, 64, 64)...  6.37 us
    pallas_call x1, Pallas kernels, chol_tail(): pl.pallas_call(chol_tail_kernel, out_shape=(jax.ShapeDtypeStruct((32, 64,...  5.5 us
  transfers between devices with their start and end apart: 9, of which 3 were waited for; matrix products, arithmetic and copies ran while one was open for 0% of the time, Pallas kernels for 48%

profile of v4, /device:TPU:1, one launch (start us, length us, event | category | flops | bytes accessed | tf_op | source)
XLA Modules:
  0.0 90.3 jit_solution(6460282398141725667)
XLA Ops:
  0.6 9.2 %climb.1 = (f32[32,64,128]{2,1,0:T(8,128)S(1)}, f32[64,128]{1,0:T(8,128)S(1)}, f32[64,128]{1,0:T(8,128)S(1)}) custom-call(bf16[64,64,256]{2,1,0:T(8,128)(2,1)} %b_hbm.1, f32[64,64,128]{2,1,0:T(8,128)} %t_hbm.1), custom_call_target="tpu_custom_call" | custom-call | flops 11500000256 | bytes 4096 | tf_op jit(solution)/shard_map/climb/pallas_call | solution.py:166
  9.9 2.2 %collective-permute-start.2 = (f32[64,128]{1,0:T(8,128)S(1)}, f32[64,128]{1,0:T(8,128)S(1)}, u32[]{:S(2)}, u32[]{:S(2)}) collective-permute-start(f32[64,128]{1,0:T(8,128)S(1)} %get-tuple-element.13.p0), channel_id=1, source_target_pairs={{0,1},{1,0},{2,3},{3,2},{4,5},{5,4},{6,7},{7,6},{8,9},{9,8},{10,11... | collective-permute-start | bytes 98312 | tf_op jit(solution)/shard_map/ppermute | solution.py:631
  12.1 2.8 %chol_head.1.i_ref = f32[64,64,128]{2,1,0:T(8,128)S(1)} custom-call(f32[32,64,128]{2,1,0:T(8,128)S(1)} %get-tuple-element.10.g_ref), custom_call_target="tpu_custom_call" | custom-call | flops 4600000000 | bytes 4096 | tf_op jit(solution)/shard_map/chol_head/pallas_call | solution.py:253
  14.8 5.5 %chol_tail.1 = (f32[32,64,128]{2,1,0:T(8,128)S(1)}, f32[33,32,128]{2,1,0:T(8,128)S(1)}) custom-call(f32[64,64,128]{2,1,0:T(8,128)S(1)} %chol_head.1.i_ref), custom_call_target="tpu_custom_call" | custom-call | flops 5750000128 | bytes 4096 | tf_op jit(solution)/shard_map/chol_tail/pallas_call | solution.py:309
  20.3 0.1 collective-permute-start
  20.4 9.4 %collective-permute-start.1 = (f32[33,32,128]{2,1,0:T(8,128)S(1)}, f32[33,32,128]{2,1,0:T(8,128)S(1)}, u32[]{:S(2)}, u32[]{:S(2)}) collective-permute-start(f32[33,32,128]{2,1,0:T(8,128)S(1)} %get-tuple-element.12), channel_id=1, source_target_pairs={{1,2},{3,4},{5,6},{7,8},{9,10},{11,12},{13,14},{15,16},{17,18},{19... | collective-permute-start | bytes 1622024 | tf_op jit(solution)/shard_map/ppermute | solution.py:655
  29.8 0.0 collective-permute-done.2.p1
  29.8 0.1 collective-permute-start.3
  29.9 6.2 %shard_map.85.y_ref = bf16[128,64,256]{2,1,0:T(8,128)(2,1)S(1)} custom-call(f32[64,64,512]{2,1,0:T(8,128)} %c1_ref.3, f32[64,64,512]{2,1,0:T(8,128)} %c1_ref.3, f32[32,64,128]{2,1,0:T(8,128)S(1)} %get-tuple-element.11.low_ref.own_ref), custom_call_target="tpu_custom_call" | custom-call | flops 6899999744 | bytes 4096 | tf_op jit(solution)/shard_map/pallas_call | solution.py:368
  36.1 0.0 copy-start.1
  36.1 1.9 %copy-done.1 = bf16[128,64,256]{2,1,0:T(8,128)(2,1)} copy-done((bf16[128,64,256]{2,1,0:T(8,128)(2,1)}, bf16[128,64,256]{2,1,0:T(8,128)(2,1)S(1)}, u32[]{:S(2)}) %copy-start.1) | copy-done | bytes 4194328
  38.1 4.5 %collective-permute-done.3.p2 = f32[2,64,128]{2,1,0:T(8,128)S(1)} collective-permute-done((f32[2,64,128]{2,1,0:T(8,128)S(1)}, f32[2,64,128]{2,1,0:T(8,128)S(1)}, u32[]{:S(2)}, u32[]{:S(2)}) %collective-permute-start.3) | collective-permute-done | bytes 65568 | tf_op jit(solution)/shard_map/ppermute | solution.py:631
  42.6 0.0 copy-start.5
  42.6 0.1 collective-permute-start.4
  42.7 6.2 %shard_map.86.y_ref = bf16[128,64,256]{2,1,0:T(8,128)(2,1)S(1)} custom-call(f32[64,64,512]{2,1,0:T(8,128)} %c1_ref.3, f32[64,64,512]{2,1,0:T(8,128)} %c1_ref.3, f32[32,64,128]{2,1,0:T(8,128)S(1)} %get-tuple-element.11.low_ref.own_ref), custom_call_target="tpu_custom_call" | custom-call | flops 6899999744 | bytes 4096 | tf_op jit(solution)/shard_map/pallas_call | solution.py:368
  48.9 0.0 copy-start.3
  48.9 2.0 %copy-done.3 = bf16[128,64,256]{2,1,0:T(8,128)(2,1)} copy-done((bf16[128,64,256]{2,1,0:T(8,128)(2,1)}, bf16[128,64,256]{2,1,0:T(8,128)(2,1)S(1)}, u32[]{:S(2)}) %copy-start.3) | copy-done | bytes 4194328
  50.9 0.0 collective-permute-done.4.p3
  50.9 0.1 collective-permute-start.5
  51.0 0.1 pad_add_fusion.at_ref
  51.1 0.0 copy-done.5
  51.1 8.6 %collective-permute-done.5.p4 = f32[8,64,128]{2,1,0:T(8,128)S(1)} collective-permute-done((f32[8,64,128]{2,1,0:T(8,128)S(1)}, f32[8,64,128]{2,1,0:T(8,128)S(1)}, u32[]{:S(2)}, u32[]{:S(2)}) %collective-permute-start.5) | collective-permute-done | bytes 262176 | tf_op jit(solution)/shard_map/ppermute | solution.py:631
  59.7 0.0 copy-start.6
  59.7 6.4 %branch.1 = (f32[1,64,64]{2,1,0:T(8,128)}, f32[64,128]{1,0:T(8,128)S(1)}) custom-call(s32[2]{0:T(128)S(1)} %pad_add_fusion.at_ref, f32[64,128]{1,0:T(8,128)S(1)} %get-tuple-element.13.p0, f32[64,128]{1,0:T(8,128)S(1)} %collective-permute-done.2.p1, f32[2,64,128]{2,1,0:T(8,128)S(1)} %collective-permute-done.3.p2, ...), custom_call_target="tpu_custom_call" | custom-call | flops 5750000128 | bytes 4096 | tf_op jit(solution)/shard_map/branch/pallas_call | solution.py:571
  66.0 1.3 %collective-permute-start.6 = (f32[64,128]{1,0:T(8,128)S(1)}, f32[64,128]{1,0:T(8,128)S(1)}, u32[]{:S(2)}, u32[]{:S(2)}) collective-permute-start(f32[64,128]{1,0:T(8,128)S(1)} %get-tuple-element.15.l0), channel_id=1, source_target_pairs={{0,16},{16,0},{32,48},{48,32},{64,80},{80,64},{96,112},{112,96},{1... | collective-permute-start | bytes 98312 | tf_op jit(solution)/shard_map/ppermute | solution.py:631
  67.3 0.0 copy-done.6
  67.3 0.9 collective-permute-done.6.l1
  68.2 0.0 copy-start.4
  68.2 1.7 %collective-permute-start.7 = (f32[2,64,128]{2,1,0:T(8,128)S(1)}, f32[2,64,128]{2,1,0:T(8,128)S(1)}, u32[]{:S(2)}, u32[]{:S(2)}) collective-permute-start(f32[2,64,128]{2,1,0:T(8,128)S(1)} %pad_maximum_fusion.4), channel_id=1, source_target_pairs={{0,32},{16,48},{32,0},{48,16},{64,96},{80,112},{96,64},{112,80},{1... | collective-permute-start | bytes 196616 | tf_op jit(solution)/shard_map/ppermute | solution.py:631
  69.9 0.0 collective-permute-done.near_ref
  69.9 0.0 collective-permute-done.1.far_ref
  69.9 2.8 %prep.1.d_ref = bf16[192,64,256]{2,1,0:T(8,128)(2,1)S(1)} custom-call(s32[1]{0:T(128)S(6)} %select_n.29.odd_ref, f32[33,32,128]{2,1,0:T(8,128)S(1)} %collective-permute-done.near_ref, f32[32,64,128]{2,1,0:T(8,128)S(1)} %get-tuple-element.11.low_ref.own_ref, f32[33,32,128]{2,1,0:T(8,128)S(1)} %collective-permute-done.1.far_ref), custom_call_target="tpu_custom_call" | custom-call | flops 3449999872 | bytes 4096 | tf_op jit(solution)/shard_map/prep/pallas_call | solution.py:432
  72.7 0.0 copy-done.4
  72.7 0.0 copy-start.2
  72.8 6.7 %shard_map.87.refs_0_ = f32[64,64,512]{2,1,0:T(8,128)} custom-call(s32[512]{0:T(512)S(1)} %broadcast_subtract_fusion.cols_ref, bf16[128,64,256]{2,1,0:T(8,128)(2,1)S(1)} %copy-done.4, bf16[192,64,256]{2,1,0:T(8,128)(2,1)S(1)} %prep.1.d_ref), custom_call_target="tpu_custom_call" | custom-call | flops 9200000000 | bytes 4096 | tf_op jit(solution)/shard_map/pallas_call | solution.py:495
  79.5 0.0 collective-permute-done.7.l2
  79.5 0.0 copy-start
  79.5 1.9 %collective-permute-start.8 = (f32[4,64,128]{2,1,0:T(8,128)S(1)}, f32[4,64,128]{2,1,0:T(8,128)S(1)}, u32[]{:S(2)}, u32[]{:S(2)}) collective-permute-start(f32[4,64,128]{2,1,0:T(8,128)S(1)} %pad_maximum_fusion.2), channel_id=1, source_target_pairs={{0,96},{16,112},{32,64},{48,80},{64,32},{80,48},{96,0},{112,16},{1... | collective-permute-start | bytes 393224 | tf_op jit(solution)/shard_map/ppermute | solution.py:631
  81.4 0.0 copy-done.2
  81.4 6.6 %shard_map.88 = f32[64,64,512]{2,1,0:T(8,128)} custom-call(s32[512]{0:T(512)S(1)} %broadcast_subtract_fusion.cols_ref, bf16[128,64,256]{2,1,0:T(8,128)(2,1)S(1)} %copy-done.2, bf16[192,64,256]{2,1,0:T(8,128)(2,1)S(1)} %prep.1.d_ref, f32[64,64,512]{2,1,0:T(8,128)} %shard_map.87.refs_0_), custom_call_target="tpu_custom_call", output_to_operand_aliasing={{}: (3, {})} | custom-call | flops 9200000000 | bytes 4096 | tf_op jit(solution)/shard_map/pallas_call | solution.py:495
  88.1 0.0 collective-permute-done.8.l3
  88.1 0.0 copy-done
  88.1 2.2 %far.1 = f32[64,16,64]{2,1,0:T(8,128)} custom-call(s32[16]{0:T(128)S(1)} %broadcast_xor_fusion.cols_ref, f32[64,16,64]{2,1,0:T(8,128)S(1)} %bitcast.18, f32[64,128]{1,0:T(8,128)S(1)} %get-tuple-element.15.l0, f32[64,128]{1,0:T(8,128)S(1)} %collective-permute-done.6.l1, f32[2,64,128]{2,1,0:T(8,128)S(1)} %collective-permute-done.7.l2, ...), custom_call_target="tpu_custom_call" | custom-call | flops 3449999872 | bytes 4096 | tf_op jit(solution)/shard_map/far/pallas_call | solution.py:618
  (7 shorter events, 0.1 us)
Async XLA Ops:
  9.9 19.9 %collective-permute-start.2 = (f32[64,128]{1,0:T(8,128)S(1)}, f32[64,128]{1,0:T(8,128)S(1)}, u32[]{:S(2)}, u32[]{:S(2)}) collective-permute-start(f32[64,128]{1,0:T(8,128)S(1)} %get-tuple-element.13.p0), channel_id=1, source_target_pairs={{0,1},{1,0},{2,3},{3,2},{4,5},{5,4},{6,7},{7,6},{8,9},{9,8},{10,11... | collective-permute-start | bytes 98312 | tf_op jit(solution)/shard_map/ppermute | solution.py:631
  20.3 49.5 %collective-permute-start = (f32[33,32,128]{2,1,0:T(8,128)S(1)}, f32[33,32,128]{2,1,0:T(8,128)S(1)}, u32[]{:S(2)}, u32[]{:S(2)}) collective-permute-start(f32[33,32,128]{2,1,0:T(8,128)S(1)} %get-tuple-element.12), channel_id=1, source_target_pairs={{0,1},{1,0},{2,3},{3,2},{4,5},{5,4},{6,7},{7,6},{8,9},{9,8},{10,11... | collective-permute-start | bytes 1622024 | tf_op jit(solution)/shard_map/ppermute | solution.py:653
  20.4 49.5 %collective-permute-start.1 = (f32[33,32,128]{2,1,0:T(8,128)S(1)}, f32[33,32,128]{2,1,0:T(8,128)S(1)}, u32[]{:S(2)}, u32[]{:S(2)}) collective-permute-start(f32[33,32,128]{2,1,0:T(8,128)S(1)} %get-tuple-element.12), channel_id=1, source_target_pairs={{1,2},{3,4},{5,6},{7,8},{9,10},{11,12},{13,14},{15,16},{17,18},{19... | collective-permute-start | bytes 1622024 | tf_op jit(solution)/shard_map/ppermute | solution.py:655
  29.8 12.7 %collective-permute-start.3 = (f32[2,64,128]{2,1,0:T(8,128)S(1)}, f32[2,64,128]{2,1,0:T(8,128)S(1)}, u32[]{:S(2)}, u32[]{:S(2)}) collective-permute-start(f32[2,64,128]{2,1,0:T(8,128)S(1)} %pad_maximum_fusion.3), channel_id=1, source_target_pairs={{0,3},{1,2},{2,1},{3,0},{4,7},{5,6},{6,5},{7,4},{8,11},{9,10},{10,... | collective-permute-start | bytes 196616 | tf_op jit(solution)/shard_map/ppermute | solution.py:631
  36.1 2.0 %copy-start.1 = (bf16[128,64,256]{2,1,0:T(8,128)(2,1)}, bf16[128,64,256]{2,1,0:T(8,128)(2,1)S(1)}, u32[]{:S(2)}) copy-start(bf16[128,64,256]{2,1,0:T(8,128)(2,1)S(1)} %shard_map.85.y_ref) | copy-start | bytes 12582916
  42.6 8.5 %copy-start.5 = (s32[512]{0:T(512)S(1)}, s32[512]{0:T(512)}, u32[]{:S(2)}) copy-start(s32[512]{0:T(512)} %param.9) | copy-start | bytes 6148
  42.6 8.3 %collective-permute-start.4 = (f32[4,64,128]{2,1,0:T(8,128)S(1)}, f32[4,64,128]{2,1,0:T(8,128)S(1)}, u32[]{:S(2)}, u32[]{:S(2)}) collective-permute-start(f32[4,64,128]{2,1,0:T(8,128)S(1)} %pad_maximum_fusion.1), channel_id=1, source_target_pairs={{0,4},{1,5},{2,6},{3,7},{4,0},{5,1},{6,2},{7,3},{8,12},{9,13},{10,... | collective-permute-start | bytes 393224 | tf_op jit(solution)/shard_map/ppermute | solution.py:631
  48.9 2.0 %copy-start.3 = (bf16[128,64,256]{2,1,0:T(8,128)(2,1)}, bf16[128,64,256]{2,1,0:T(8,128)(2,1)S(1)}, u32[]{:S(2)}) copy-start(bf16[128,64,256]{2,1,0:T(8,128)(2,1)S(1)} %shard_map.86.y_ref) | copy-start | bytes 12582916
  50.9 8.7 %collective-permute-start.5 = (f32[8,64,128]{2,1,0:T(8,128)S(1)}, f32[8,64,128]{2,1,0:T(8,128)S(1)}, u32[]{:S(2)}, u32[]{:S(2)}) collective-permute-start(f32[8,64,128]{2,1,0:T(8,128)S(1)} %pad_maximum_fusion), channel_id=1, source_target_pairs={{0,12},{1,13},{2,14},{3,15},{4,8},{5,9},{6,10},{7,11},{8,4},{9,5},... | collective-permute-start | bytes 786440 | tf_op jit(solution)/shard_map/ppermute | solution.py:631
  59.7 7.6 %copy-start.6 = (s32[16]{0:T(128)S(1)}, s32[16]{0:T(128)}, u32[]{:S(2)}) copy-start(s32[16]{0:T(128)} %param.11) | copy-start | bytes 196
  66.0 2.1 %collective-permute-start.6 = (f32[64,128]{1,0:T(8,128)S(1)}, f32[64,128]{1,0:T(8,128)S(1)}, u32[]{:S(2)}, u32[]{:S(2)}) collective-permute-start(f32[64,128]{1,0:T(8,128)S(1)} %get-tuple-element.15.l0), channel_id=1, source_target_pairs={{0,16},{16,0},{32,48},{48,32},{64,80},{80,64},{96,112},{112,96},{1... | collective-permute-start | bytes 98312 | tf_op jit(solution)/shard_map/ppermute | solution.py:631
  68.2 4.6 %copy-start.4 = (bf16[128,64,256]{2,1,0:T(8,128)(2,1)S(1)}, bf16[128,64,256]{2,1,0:T(8,128)(2,1)}, u32[]{:S(2)}) copy-start(bf16[128,64,256]{2,1,0:T(8,128)(2,1)} %copy-done.3) | copy-start | bytes 12582916
  68.2 11.3 %collective-permute-start.7 = (f32[2,64,128]{2,1,0:T(8,128)S(1)}, f32[2,64,128]{2,1,0:T(8,128)S(1)}, u32[]{:S(2)}, u32[]{:S(2)}) collective-permute-start(f32[2,64,128]{2,1,0:T(8,128)S(1)} %pad_maximum_fusion.4), channel_id=1, source_target_pairs={{0,32},{16,48},{32,0},{48,16},{64,96},{80,112},{96,64},{112,80},{1... | collective-permute-start | bytes 196616 | tf_op jit(solution)/shard_map/ppermute | solution.py:631
  72.7 8.7 %copy-start.2 = (bf16[128,64,256]{2,1,0:T(8,128)(2,1)S(1)}, bf16[128,64,256]{2,1,0:T(8,128)(2,1)}, u32[]{:S(2)}) copy-start(bf16[128,64,256]{2,1,0:T(8,128)(2,1)} %copy-done.1) | copy-start | bytes 12582916
  79.5 8.5 %copy-start = (f32[64,64,16]{1,2,0:T(8,128)S(1)}, f32[64,64,16]{1,2,0:T(8,128)}, u32[]{:S(2)}) copy-start(f32[64,64,16]{1,2,0:T(8,128)} %param.10) | copy-start | bytes 786436
  79.5 8.5 %collective-permute-start.8 = (f32[4,64,128]{2,1,0:T(8,128)S(1)}, f32[4,64,128]{2,1,0:T(8,128)S(1)}, u32[]{:S(2)}, u32[]{:S(2)}) collective-permute-start(f32[4,64,128]{2,1,0:T(8,128)S(1)} %pad_maximum_fusion.2), channel_id=1, source_target_pairs={{0,96},{16,112},{32,64},{48,80},{64,32},{80,48},{96,0},{112,16},{1... | collective-permute-start | bytes 393224 | tf_op jit(solution)/shard_map/ppermute | solution.py:631

commit v5 on v4

--- a/solution.py
+++ b/solution.py
@@ -70,9 +70,9 @@
     return rows(m, m)
 
 
-LEAVES = 16
-HALF = 4
-PAIRS = 32
+LEAVES = 32
+HALF = 8
+PAIRS = 64
 
 
 def climb_kernel(

time: 90.5 us -> 89.4 us (0.988)
  Pallas kernels: 54.6 us -> 53.2 us
  transfers between devices with their start and end apart: 9 -> 9, of which waited for: 3 -> 3; matrix products, arithmetic and copies ran while one was open for 0% -> 0% of each run, Pallas kernels for 48% -> 47%
where the time goes in v5:
time: 89.4 us; the launch traced here: 89.1 us
  Pallas kernels  53.2 us (60%)
  starting transfers between devices  16.8 us (19%)
  waiting for transfers between devices  14.2 us (16%)
  local copies, waits for them, and re-layouts  3.98 us (4%)
    ppermute x7, waiting for transfers between devices, shifted(): lax.ppermute(value, axis, [(i, to(i)) for i in range(lax.axis_size(axis))])  14.2 us
    pallas_call x2, Pallas kernels, full_leaf(): pl.pallas_call(functools.partial(full_kernel, part=part), out_shape=jax.S...  12.8 us
    pallas_call x2, Pallas kernels, half_leaf(): pl.pallas_call(functools.partial(half_kernel, part=part), out_shape=jax.S...  11.9 us
    ppermute x1, starting transfers between devices, steps(): low_far = lax.ppermute(pack, both, later + [(j, i) for i, j in later])  9.38 us
    pallas_call x1, Pallas kernels, climb(): pl.pallas_call(climb_kernel, out_shape=(jax.ShapeDtypeStruct((32, 64, 128...  8.92 us
    ppermute x7, starting transfers between devices, shifted(): lax.ppermute(value, axis, [(i, to(i)) for i in range(lax.axis_size(axis))])  7.33 us
    pallas_call x1, Pallas kernels, branch(): pl.pallas_call(branch_kernel, out_shape=(jax.ShapeDtypeStruct((1, 64, 64)...  6.36 us
    pallas_call x1, Pallas kernels, chol_tail(): pl.pallas_call(chol_tail_kernel, out_shape=(jax.ShapeDtypeStruct((32, 64,...  5.5 us
  transfers between devices with their start and end apart: 9, of which 3 were waited for; matrix products, arithmetic and copies ran while one was open for 0% of the time, Pallas kernels for 47%

profile of v5, /device:TPU:1, one launch (start us, length us, event | category | flops | bytes accessed | tf_op | source)
XLA Modules:
  0.0 89.1 jit_solution(7701369189849758197)
XLA Ops:
  0.6 8.9 %climb.1 = (f32[32,64,128]{2,1,0:T(8,128)S(1)}, f32[64,128]{1,0:T(8,128)S(1)}, f32[64,128]{1,0:T(8,128)S(1)}) custom-call(bf16[64,64,256]{2,1,0:T(8,128)(2,1)} %b_hbm.1, f32[64,64,128]{2,1,0:T(8,128)} %t_hbm.1), custom_call_target="tpu_custom_call" | custom-call | flops 11500000256 | bytes 4096 | tf_op jit(solution)/shard_map/climb/pallas_call | solution.py:166
  9.6 2.2 %collective-permute-start.2 = (f32[64,128]{1,0:T(8,128)S(1)}, f32[64,128]{1,0:T(8,128)S(1)}, u32[]{:S(2)}, u32[]{:S(2)}) collective-permute-start(f32[64,128]{1,0:T(8,128)S(1)} %get-tuple-element.13.p0), channel_id=1, source_target_pairs={{0,1},{1,0},{2,3},{3,2},{4,5},{5,4},{6,7},{7,6},{8,9},{9,8},{10,11... | collective-permute-start | bytes 98312 | tf_op jit(solution)/shard_map/ppermute | solution.py:631
  11.8 2.8 %chol_head.1.i_ref = f32[64,64,128]{2,1,0:T(8,128)S(1)} custom-call(f32[32,64,128]{2,1,0:T(8,128)S(1)} %get-tuple-element.10.g_ref), custom_call_target="tpu_custom_call" | custom-call | flops 4600000000 | bytes 4096 | tf_op jit(solution)/shard_map/chol_head/pallas_call | solution.py:253
  14.5 5.5 %chol_tail.1 = (f32[32,64,128]{2,1,0:T(8,128)S(1)}, f32[33,32,128]{2,1,0:T(8,128)S(1)}) custom-call(f32[64,64,128]{2,1,0:T(8,128)S(1)} %chol_head.1.i_ref), custom_call_target="tpu_custom_call" | custom-call | flops 5750000128 | bytes 4096 | tf_op jit(solution)/shard_map/chol_tail/pallas_call | solution.py:309
  20.0 0.1 collective-permute-start
  20.1 9.4 %collective-permute-start.1 = (f32[33,32,128]{2,1,0:T(8,128)S(1)}, f32[33,32,128]{2,1,0:T(8,128)S(1)}, u32[]{:S(2)}, u32[]{:S(2)}) collective-permute-start(f32[33,32,128]{2,1,0:T(8,128)S(1)} %get-tuple-element.12), channel_id=1, source_target_pairs={{1,2},{3,4},{5,6},{7,8},{9,10},{11,12},{13,14},{15,16},{17,18},{19... | collective-permute-start | bytes 1622024 | tf_op jit(solution)/shard_map/ppermute | solution.py:655
  29.5 0.0 collective-permute-done.2.p1
  29.5 0.1 collective-permute-start.3
  29.6 5.9 %shard_map.85.y_ref = bf16[128,64,256]{2,1,0:T(8,128)(2,1)S(1)} custom-call(f32[64,64,512]{2,1,0:T(8,128)} %c1_ref.3, f32[64,64,512]{2,1,0:T(8,128)} %c1_ref.3, f32[32,64,128]{2,1,0:T(8,128)S(1)} %get-tuple-element.11.low_ref.own_ref), custom_call_target="tpu_custom_call" | custom-call | flops 6899999744 | bytes 4096 | tf_op jit(solution)/shard_map/pallas_call | solution.py:368
  35.6 0.0 copy-start.1
  35.6 1.9 %copy-done.1 = bf16[128,64,256]{2,1,0:T(8,128)(2,1)} copy-done((bf16[128,64,256]{2,1,0:T(8,128)(2,1)}, bf16[128,64,256]{2,1,0:T(8,128)(2,1)S(1)}, u32[]{:S(2)}) %copy-start.1) | copy-done | bytes 4194328
  37.5 4.8 %collective-permute-done.3.p2 = f32[2,64,128]{2,1,0:T(8,128)S(1)} collective-permute-done((f32[2,64,128]{2,1,0:T(8,128)S(1)}, f32[2,64,128]{2,1,0:T(8,128)S(1)}, u32[]{:S(2)}, u32[]{:S(2)}) %collective-permute-start.3) | collective-permute-done | bytes 65568 | tf_op jit(solution)/shard_map/ppermute | solution.py:631
  42.3 0.0 copy-start.5
  42.3 0.1 collective-permute-start.4
  42.4 5.9 %shard_map.86.y_ref = bf16[128,64,256]{2,1,0:T(8,128)(2,1)S(1)} custom-call(f32[64,64,512]{2,1,0:T(8,128)} %c1_ref.3, f32[64,64,512]{2,1,0:T(8,128)} %c1_ref.3, f32[32,64,128]{2,1,0:T(8,128)S(1)} %get-tuple-element.11.low_ref.own_ref), custom_call_target="tpu_custom_call" | custom-call | flops 6899999744 | bytes 4096 | tf_op jit(solution)/shard_map/pallas_call | solution.py:368
  48.3 0.0 copy-start.3
  48.3 2.0 %copy-done.3 = bf16[128,64,256]{2,1,0:T(8,128)(2,1)} copy-done((bf16[128,64,256]{2,1,0:T(8,128)(2,1)}, bf16[128,64,256]{2,1,0:T(8,128)(2,1)S(1)}, u32[]{:S(2)}) %copy-start.3) | copy-done | bytes 4194328
  50.3 0.0 collective-permute-done.4.p3
  50.4 0.1 collective-permute-start.5
  50.5 0.1 pad_add_fusion.at_ref
  50.5 0.0 copy-done.5
  50.5 8.5 %collective-permute-done.5.p4 = f32[8,64,128]{2,1,0:T(8,128)S(1)} collective-permute-done((f32[8,64,128]{2,1,0:T(8,128)S(1)}, f32[8,64,128]{2,1,0:T(8,128)S(1)}, u32[]{:S(2)}, u32[]{:S(2)}) %collective-permute-start.5) | collective-permute-done | bytes 262176 | tf_op jit(solution)/shard_map/ppermute | solution.py:631
  59.1 0.0 copy-start.6
  59.1 6.4 %branch.1 = (f32[1,64,64]{2,1,0:T(8,128)}, f32[64,128]{1,0:T(8,128)S(1)}) custom-call(s32[2]{0:T(128)S(1)} %pad_add_fusion.at_ref, f32[64,128]{1,0:T(8,128)S(1)} %get-tuple-element.13.p0, f32[64,128]{1,0:T(8,128)S(1)} %collective-permute-done.2.p1, f32[2,64,128]{2,1,0:T(8,128)S(1)} %collective-permute-done.3.p2, ...), custom_call_target="tpu_custom_call" | custom-call | flops 5750000128 | bytes 4096 | tf_op jit(solution)/shard_map/branch/pallas_call | solution.py:571
  65.5 1.3 %collective-permute-start.6 = (f32[64,128]{1,0:T(8,128)S(1)}, f32[64,128]{1,0:T(8,128)S(1)}, u32[]{:S(2)}, u32[]{:S(2)}) collective-permute-start(f32[64,128]{1,0:T(8,128)S(1)} %get-tuple-element.15.l0), channel_id=1, source_target_pairs={{0,16},{16,0},{32,48},{48,32},{64,80},{80,64},{96,112},{112,96},{1... | collective-permute-start | bytes 98312 | tf_op jit(solution)/shard_map/ppermute | solution.py:631
  66.7 0.0 copy-done.6
  66.8 0.9 collective-permute-done.6.l1
  67.6 0.0 copy-start.4
  67.6 1.7 %collective-permute-start.7 = (f32[2,64,128]{2,1,0:T(8,128)S(1)}, f32[2,64,128]{2,1,0:T(8,128)S(1)}, u32[]{:S(2)}, u32[]{:S(2)}) collective-permute-start(f32[2,64,128]{2,1,0:T(8,128)S(1)} %pad_maximum_fusion.4), channel_id=1, source_target_pairs={{0,32},{16,48},{32,0},{48,16},{64,96},{80,112},{96,64},{112,80},{1... | collective-permute-start | bytes 196616 | tf_op jit(solution)/shard_map/ppermute | solution.py:631
  69.3 0.0 collective-permute-done.near_ref
  69.3 0.0 collective-permute-done.1.far_ref
  69.3 2.8 %prep.1.d_ref = bf16[192,64,256]{2,1,0:T(8,128)(2,1)S(1)} custom-call(s32[1]{0:T(128)S(6)} %select_n.29.odd_ref, f32[33,32,128]{2,1,0:T(8,128)S(1)} %collective-permute-done.near_ref, f32[32,64,128]{2,1,0:T(8,128)S(1)} %get-tuple-element.11.low_ref.own_ref, f32[33,32,128]{2,1,0:T(8,128)S(1)} %collective-permute-done.1.far_ref), custom_call_target="tpu_custom_call" | custom-call | flops 3449999872 | bytes 4096 | tf_op jit(solution)/shard_map/prep/pallas_call | solution.py:432
  72.2 0.0 copy-done.4
  72.2 0.0 copy-start.2
  72.2 6.4 %shard_map.87.refs_0_ = f32[64,64,512]{2,1,0:T(8,128)} custom-call(s32[512]{0:T(512)S(1)} %broadcast_subtract_fusion.cols_ref, bf16[128,64,256]{2,1,0:T(8,128)(2,1)S(1)} %copy-done.4, bf16[192,64,256]{2,1,0:T(8,128)(2,1)S(1)} %prep.1.d_ref), custom_call_target="tpu_custom_call" | custom-call | flops 9200000000 | bytes 4096 | tf_op jit(solution)/shard_map/pallas_call | solution.py:495
  78.7 0.0 collective-permute-done.7.l2
  78.7 0.0 copy-start
  78.7 1.9 %collective-permute-start.8 = (f32[4,64,128]{2,1,0:T(8,128)S(1)}, f32[4,64,128]{2,1,0:T(8,128)S(1)}, u32[]{:S(2)}, u32[]{:S(2)}) collective-permute-start(f32[4,64,128]{2,1,0:T(8,128)S(1)} %pad_maximum_fusion.2), channel_id=1, source_target_pairs={{0,96},{16,112},{32,64},{48,80},{64,32},{80,48},{96,0},{112,16},{1... | collective-permute-start | bytes 393224 | tf_op jit(solution)/shard_map/ppermute | solution.py:631
  80.6 0.0 copy-done.2
  80.6 6.3 %shard_map.88 = f32[64,64,512]{2,1,0:T(8,128)} custom-call(s32[512]{0:T(512)S(1)} %broadcast_subtract_fusion.cols_ref, bf16[128,64,256]{2,1,0:T(8,128)(2,1)S(1)} %copy-done.2, bf16[192,64,256]{2,1,0:T(8,128)(2,1)S(1)} %prep.1.d_ref, f32[64,64,512]{2,1,0:T(8,128)} %shard_map.87.refs_0_), custom_call_target="tpu_custom_call", output_to_operand_aliasing={{}: (3, {})} | custom-call | flops 9200000000 | bytes 4096 | tf_op jit(solution)/shard_map/pallas_call | solution.py:495
  86.9 0.0 collective-permute-done.8.l3
  86.9 0.0 copy-done
  86.9 2.2 %far.1 = f32[64,16,64]{2,1,0:T(8,128)} custom-call(s32[16]{0:T(128)S(1)} %broadcast_xor_fusion.cols_ref, f32[64,16,64]{2,1,0:T(8,128)S(1)} %bitcast.18, f32[64,128]{1,0:T(8,128)S(1)} %get-tuple-element.15.l0, f32[64,128]{1,0:T(8,128)S(1)} %collective-permute-done.6.l1, f32[2,64,128]{2,1,0:T(8,128)S(1)} %collective-permute-done.7.l2, ...), custom_call_target="tpu_custom_call" | custom-call | flops 3449999872 | bytes 4096 | tf_op jit(solution)/shard_map/far/pallas_call | solution.py:618
  (7 shorter events, 0.1 us)
Async XLA Ops:
  9.6 19.9 %collective-permute-start.2 = (f32[64,128]{1,0:T(8,128)S(1)}, f32[64,128]{1,0:T(8,128)S(1)}, u32[]{:S(2)}, u32[]{:S(2)}) collective-permute-start(f32[64,128]{1,0:T(8,128)S(1)} %get-tuple-element.13.p0), channel_id=1, source_target_pairs={{0,1},{1,0},{2,3},{3,2},{4,5},{5,4},{6,7},{7,6},{8,9},{9,8},{10,11... | collective-permute-start | bytes 98312 | tf_op jit(solution)/shard_map/ppermute | solution.py:631
  20.0 49.3 %collective-permute-start = (f32[33,32,128]{2,1,0:T(8,128)S(1)}, f32[33,32,128]{2,1,0:T(8,128)S(1)}, u32[]{:S(2)}, u32[]{:S(2)}) collective-permute-start(f32[33,32,128]{2,1,0:T(8,128)S(1)} %get-tuple-element.12), channel_id=1, source_target_pairs={{0,1},{1,0},{2,3},{3,2},{4,5},{5,4},{6,7},{7,6},{8,9},{9,8},{10,11... | collective-permute-start | bytes 1622024 | tf_op jit(solution)/shard_map/ppermute | solution.py:653
  20.1 49.2 %collective-permute-start.1 = (f32[33,32,128]{2,1,0:T(8,128)S(1)}, f32[33,32,128]{2,1,0:T(8,128)S(1)}, u32[]{:S(2)}, u32[]{:S(2)}) collective-permute-start(f32[33,32,128]{2,1,0:T(8,128)S(1)} %get-tuple-element.12), channel_id=1, source_target_pairs={{1,2},{3,4},{5,6},{7,8},{9,10},{11,12},{13,14},{15,16},{17,18},{19... | collective-permute-start | bytes 1622024 | tf_op jit(solution)/shard_map/ppermute | solution.py:655
  29.5 12.7 %collective-permute-start.3 = (f32[2,64,128]{2,1,0:T(8,128)S(1)}, f32[2,64,128]{2,1,0:T(8,128)S(1)}, u32[]{:S(2)}, u32[]{:S(2)}) collective-permute-start(f32[2,64,128]{2,1,0:T(8,128)S(1)} %pad_maximum_fusion.3), channel_id=1, source_target_pairs={{0,3},{1,2},{2,1},{3,0},{4,7},{5,6},{6,5},{7,4},{8,11},{9,10},{10,... | collective-permute-start | bytes 196616 | tf_op jit(solution)/shard_map/ppermute | solution.py:631
  35.6 2.0 %copy-start.1 = (bf16[128,64,256]{2,1,0:T(8,128)(2,1)}, bf16[128,64,256]{2,1,0:T(8,128)(2,1)S(1)}, u32[]{:S(2)}) copy-start(bf16[128,64,256]{2,1,0:T(8,128)(2,1)S(1)} %shard_map.85.y_ref) | copy-start | bytes 12582916
  42.3 8.3 %copy-start.5 = (s32[512]{0:T(512)S(1)}, s32[512]{0:T(512)}, u32[]{:S(2)}) copy-start(s32[512]{0:T(512)} %param.9) | copy-start | bytes 6148
  42.3 8.0 %collective-permute-start.4 = (f32[4,64,128]{2,1,0:T(8,128)S(1)}, f32[4,64,128]{2,1,0:T(8,128)S(1)}, u32[]{:S(2)}, u32[]{:S(2)}) collective-permute-start(f32[4,64,128]{2,1,0:T(8,128)S(1)} %pad_maximum_fusion.1), channel_id=1, source_target_pairs={{0,4},{1,5},{2,6},{3,7},{4,0},{5,1},{6,2},{7,3},{8,12},{9,13},{10,... | collective-permute-start | bytes 393224 | tf_op jit(solution)/shard_map/ppermute | solution.py:631
  48.3 2.0 %copy-start.3 = (bf16[128,64,256]{2,1,0:T(8,128)(2,1)}, bf16[128,64,256]{2,1,0:T(8,128)(2,1)S(1)}, u32[]{:S(2)}) copy-start(bf16[128,64,256]{2,1,0:T(8,128)(2,1)S(1)} %shard_map.86.y_ref) | copy-start | bytes 12582916
  50.4 8.7 %collective-permute-start.5 = (f32[8,64,128]{2,1,0:T(8,128)S(1)}, f32[8,64,128]{2,1,0:T(8,128)S(1)}, u32[]{:S(2)}, u32[]{:S(2)}) collective-permute-start(f32[8,64,128]{2,1,0:T(8,128)S(1)} %pad_maximum_fusion), channel_id=1, source_target_pairs={{0,12},{1,13},{2,14},{3,15},{4,8},{5,9},{6,10},{7,11},{8,4},{9,5},... | collective-permute-start | bytes 786440 | tf_op jit(solution)/shard_map/ppermute | solution.py:631
  59.1 7.7 %copy-start.6 = (s32[16]{0:T(128)S(1)}, s32[16]{0:T(128)}, u32[]{:S(2)}) copy-start(s32[16]{0:T(128)} %param.11) | copy-start | bytes 196
  65.5 2.1 %collective-permute-start.6 = (f32[64,128]{1,0:T(8,128)S(1)}, f32[64,128]{1,0:T(8,128)S(1)}, u32[]{:S(2)}, u32[]{:S(2)}) collective-permute-start(f32[64,128]{1,0:T(8,128)S(1)} %get-tuple-element.15.l0), channel_id=1, source_target_pairs={{0,16},{16,0},{32,48},{48,32},{64,80},{80,64},{96,112},{112,96},{1... | collective-permute-start | bytes 98312 | tf_op jit(solution)/shard_map/ppermute | solution.py:631
  67.6 4.6 %copy-start.4 = (bf16[128,64,256]{2,1,0:T(8,128)(2,1)S(1)}, bf16[128,64,256]{2,1,0:T(8,128)(2,1)}, u32[]{:S(2)}) copy-start(bf16[128,64,256]{2,1,0:T(8,128)(2,1)} %copy-done.3) | copy-start | bytes 12582916
  67.6 11.0 %collective-permute-start.7 = (f32[2,64,128]{2,1,0:T(8,128)S(1)}, f32[2,64,128]{2,1,0:T(8,128)S(1)}, u32[]{:S(2)}, u32[]{:S(2)}) collective-permute-start(f32[2,64,128]{2,1,0:T(8,128)S(1)} %pad_maximum_fusion.4), channel_id=1, source_target_pairs={{0,32},{16,48},{32,0},{48,16},{64,96},{80,112},{96,64},{112,80},{1... | collective-permute-start | bytes 196616 | tf_op jit(solution)/shard_map/ppermute | solution.py:631
  72.2 8.4 %copy-start.2 = (bf16[128,64,256]{2,1,0:T(8,128)(2,1)S(1)}, bf16[128,64,256]{2,1,0:T(8,128)(2,1)}, u32[]{:S(2)}) copy-start(bf16[128,64,256]{2,1,0:T(8,128)(2,1)} %copy-done.1) | copy-start | bytes 12582916
  78.7 8.2 %copy-start = (f32[64,64,16]{1,2,0:T(8,128)S(1)}, f32[64,64,16]{1,2,0:T(8,128)}, u32[]{:S(2)}) copy-start(f32[64,64,16]{1,2,0:T(8,128)} %param.10) | copy-start | bytes 786436
  78.7 8.2 %collective-permute-start.8 = (f32[4,64,128]{2,1,0:T(8,128)S(1)}, f32[4,64,128]{2,1,0:T(8,128)S(1)}, u32[]{:S(2)}, u32[]{:S(2)}) collective-permute-start(f32[4,64,128]{2,1,0:T(8,128)S(1)} %pad_maximum_fusion.2), channel_id=1, source_target_pairs={{0,96},{16,112},{32,64},{48,80},{64,32},{80,48},{96,0},{112,16},{1... | collective-permute-start | bytes 393224 | tf_op jit(solution)/shard_map/ppermute | solution.py:631

commit v6 on v5

--- a/solution.py
+++ b/solution.py
@@ -262,9 +262,24 @@
     )(gram)
 
 
-def chol_tail_kernel(i_ref, low_ref, pack_ref, a_ref, u_ref, v_ref):
+def chol_mid_kernel(i_ref, a_ref):
     a_ref[...] = i_ref[...]
     chol_lanes(a_ref, range(EARLY, 8))
+
+
+def chol_mid(part):
+    return pl.pallas_call(
+        chol_mid_kernel,
+        out_shape=jax.ShapeDtypeStruct((64, 64, 128), F32),
+        in_specs=[VMEM],
+        out_specs=VMEM,
+        compiler_params=params(8),
+        cost_estimate=cost(3),
+        name="chol_mid",
+    )(part)
+
+
+def chol_tail_kernel(a_ref, low_ref, pack_ref, u_ref, v_ref):
     below = lax.broadcasted_iota(jnp.int32, (32, 128), 0)
 
     def paired(x):
@@ -315,7 +330,6 @@
         in_specs=[VMEM],
         out_specs=(VMEM, VMEM),
         scratch_shapes=[
-            pltpu.VMEM((64, 64, 128), F32),
             pltpu.VMEM((8, 64, 128), F32),
             pltpu.VMEM((8, 32, 128), F32),
         ],
@@ -646,16 +660,17 @@
     head = chol_head(gram)
     pair = jnp.stack([pay, pay_a])
     pay_b = shifted(pair, "narrow", lambda i: i ^ 3)
-    low, pack = chol_tail(head)
+    mid = chol_mid(head)
     quad = jnp.concatenate([pair, pay_b])
     pay_c = shifted(quad, "narrow", lambda i: i ^ 4)
+    low, pack = chol_tail(mid)
+    octet = jnp.concatenate([quad, pay_c])
+    pay_d = shifted(octet, "narrow", lambda i: i ^ 12)
     count = lax.axis_size(both)
     low_near = lax.ppermute(pack, both, [(i, i ^ 1) for i in range(count)])
     later = [(i, i + 1) for i in range(1, count - 1, 2)]
     low_far = lax.ppermute(pack, both, later + [(j, i) for i, j in later])
     half_a = half_leaf(leaf_coupling, low, 0)
-    octet = jnp.concatenate([quad, pay_c])
-    pay_d = shifted(octet, "narrow", lambda i: i ^ 12)
     half_b = half_leaf(leaf_coupling, low, 1)
     ones = 1 + sum((at % 2**k == 2**k - 1).astype(jnp.int32) for k in range(1, 5))
     pick = jnp.where(ones <= 4, (16 + at) >> ones, 0)

time: 89.4 us -> 89.3 us (level)
    pallas_call x1, Pallas kernels: 5.5 us -> 3.49 us  [chol_tail(): pl.pallas_call(chol_tail_kernel, out_shape=(jax.ShapeDtypeStruct((32, 64,...]
    pallas_call x0 -> x1, Pallas kernels: none -> 1.96 us  [chol_mid(): pl.pallas_call(chol_mid_kernel, out_shape=jax.ShapeDtypeStruct((64, 64, 1...]
where the time goes in v6:
time: 89.3 us; the launch traced here: 89.1 us
  Pallas kernels  53.2 us (60%)
  starting transfers between devices  16.8 us (19%)
  waiting for transfers between devices  14.2 us (16%)
  local copies, waits for them, and re-layouts  3.98 us (4%)
    ppermute x7, waiting for transfers between devices, shifted(): lax.ppermute(value, axis, [(i, to(i)) for i in range(lax.axis_size(axis))])  14.2 us
    pallas_call x2, Pallas kernels, full_leaf(): pl.pallas_call(functools.partial(full_kernel, part=part), out_shape=jax.S...  12.8 us
    pallas_call x2, Pallas kernels, half_leaf(): pl.pallas_call(functools.partial(half_kernel, part=part), out_shape=jax.S...  11.9 us
    ppermute x1, starting transfers between devices, steps(): low_far = lax.ppermute(pack, both, later + [(j, i) for i, j in later])  9.38 us
    pallas_call x1, Pallas kernels, climb(): pl.pallas_call(climb_kernel, out_shape=(jax.ShapeDtypeStruct((32, 64, 128...  8.92 us
    ppermute x7, starting transfers between devices, shifted(): lax.ppermute(value, axis, [(i, to(i)) for i in range(lax.axis_size(axis))])  7.32 us
    pallas_call x1, Pallas kernels, branch(): pl.pallas_call(branch_kernel, out_shape=(jax.ShapeDtypeStruct((1, 64, 64)...  6.36 us
    unnamed x14, local copies, waits for them, and re-layouts  3.98 us
  transfers between devices with their start and end apart: 9, of which 3 were waited for; matrix products, arithmetic and copies ran while one was open for 0% of the time, Pallas kernels for 47%

profile of v6, /device:TPU:1, one launch (start us, length us, event | category | flops | bytes accessed | tf_op | source)
XLA Modules:
  0.0 89.1 jit_solution(4305790627894515476)
XLA Ops:
  0.6 8.9 %climb.1 = (f32[32,64,128]{2,1,0:T(8,128)S(1)}, f32[64,128]{1,0:T(8,128)S(1)}, f32[64,128]{1,0:T(8,128)S(1)}) custom-call(bf16[64,64,256]{2,1,0:T(8,128)(2,1)} %b_hbm.1, f32[64,64,128]{2,1,0:T(8,128)} %t_hbm.1), custom_call_target="tpu_custom_call" | custom-call | flops 11500000256 | bytes 4096 | tf_op jit(solution)/shard_map/climb/pallas_call | solution.py:166
  9.6 2.2 %collective-permute-start.2 = (f32[64,128]{1,0:T(8,128)S(1)}, f32[64,128]{1,0:T(8,128)S(1)}, u32[]{:S(2)}, u32[]{:S(2)}) collective-permute-start(f32[64,128]{1,0:T(8,128)S(1)} %get-tuple-element.13.p0), channel_id=1, source_target_pairs={{0,1},{1,0},{2,3},{3,2},{4,5},{5,4},{6,7},{7,6},{8,9},{9,8},{10,11... | collective-permute-start | bytes 98312 | tf_op jit(solution)/shard_map/ppermute | solution.py:645
  11.8 2.8 %chol_head.1.i_ref = f32[64,64,128]{2,1,0:T(8,128)S(1)} custom-call(f32[32,64,128]{2,1,0:T(8,128)S(1)} %get-tuple-element.10.g_ref), custom_call_target="tpu_custom_call" | custom-call | flops 4600000000 | bytes 4096 | tf_op jit(solution)/shard_map/chol_head/pallas_call | solution.py:253
  14.5 2.0 %chol_mid.1.a_ref = f32[64,64,128]{2,1,0:T(8,128)S(1)} custom-call(f32[64,64,128]{2,1,0:T(8,128)S(1)} %chol_head.1.i_ref), custom_call_target="tpu_custom_call" | custom-call | flops 3449999872 | bytes 4096 | tf_op jit(solution)/shard_map/chol_mid/pallas_call | solution.py:271
  16.5 3.5 %chol_tail.1 = (f32[32,64,128]{2,1,0:T(8,128)S(1)}, f32[33,32,128]{2,1,0:T(8,128)S(1)}) custom-call(f32[64,64,128]{2,1,0:T(8,128)S(1)} %chol_mid.1.a_ref), custom_call_target="tpu_custom_call" | custom-call | flops 5750000128 | bytes 4096 | tf_op jit(solution)/shard_map/chol_tail/pallas_call | solution.py:324
  20.0 0.1 collective-permute-start
  20.1 9.4 %collective-permute-start.1 = (f32[33,32,128]{2,1,0:T(8,128)S(1)}, f32[33,32,128]{2,1,0:T(8,128)S(1)}, u32[]{:S(2)}, u32[]{:S(2)}) collective-permute-start(f32[33,32,128]{2,1,0:T(8,128)S(1)} %get-tuple-element.12), channel_id=1, source_target_pairs={{1,2},{3,4},{5,6},{7,8},{9,10},{11,12},{13,14},{15,16},{17,18},{19... | collective-permute-start | bytes 1622024 | tf_op jit(solution)/shard_map/ppermute | solution.py:672
  29.4 0.0 collective-permute-done.2.p1
  29.5 0.1 collective-permute-start.3
  29.6 5.9 %shard_map.85.y_ref = bf16[128,64,256]{2,1,0:T(8,128)(2,1)S(1)} custom-call(f32[64,64,512]{2,1,0:T(8,128)} %c1_ref.3, f32[64,64,512]{2,1,0:T(8,128)} %c1_ref.3, f32[32,64,128]{2,1,0:T(8,128)S(1)} %get-tuple-element.11.low_ref.own_ref), custom_call_target="tpu_custom_call" | custom-call | flops 6899999744 | bytes 4096 | tf_op jit(solution)/shard_map/pallas_call | solution.py:382
  35.5 0.0 copy-start.1
  35.5 1.9 %copy-done.1 = bf16[128,64,256]{2,1,0:T(8,128)(2,1)} copy-done((bf16[128,64,256]{2,1,0:T(8,128)(2,1)}, bf16[128,64,256]{2,1,0:T(8,128)(2,1)S(1)}, u32[]{:S(2)}) %copy-start.1) | copy-done | bytes 4194328
  37.5 4.8 %collective-permute-done.3.p2 = f32[2,64,128]{2,1,0:T(8,128)S(1)} collective-permute-done((f32[2,64,128]{2,1,0:T(8,128)S(1)}, f32[2,64,128]{2,1,0:T(8,128)S(1)}, u32[]{:S(2)}, u32[]{:S(2)}) %collective-permute-start.3) | collective-permute-done | bytes 65568 | tf_op jit(solution)/shard_map/ppermute | solution.py:645
  42.2 0.0 copy-start.5
  42.2 0.1 collective-permute-start.4
  42.3 5.9 %shard_map.86.y_ref = bf16[128,64,256]{2,1,0:T(8,128)(2,1)S(1)} custom-call(f32[64,64,512]{2,1,0:T(8,128)} %c1_ref.3, f32[64,64,512]{2,1,0:T(8,128)} %c1_ref.3, f32[32,64,128]{2,1,0:T(8,128)S(1)} %get-tuple-element.11.low_ref.own_ref), custom_call_target="tpu_custom_call" | custom-call | flops 6899999744 | bytes 4096 | tf_op jit(solution)/shard_map/pallas_call | solution.py:382
  48.3 0.0 copy-start.3
  48.3 2.0 %copy-done.3 = bf16[128,64,256]{2,1,0:T(8,128)(2,1)} copy-done((bf16[128,64,256]{2,1,0:T(8,128)(2,1)}, bf16[128,64,256]{2,1,0:T(8,128)(2,1)S(1)}, u32[]{:S(2)}) %copy-start.3) | copy-done | bytes 4194328
  50.3 0.0 collective-permute-done.4.p3
  50.3 0.1 collective-permute-start.5
  50.4 0.1 pad_add_fusion.at_ref
  50.5 0.0 copy-done.5
  50.5 8.5 %collective-permute-done.5.p4 = f32[8,64,128]{2,1,0:T(8,128)S(1)} collective-permute-done((f32[8,64,128]{2,1,0:T(8,128)S(1)}, f32[8,64,128]{2,1,0:T(8,128)S(1)}, u32[]{:S(2)}, u32[]{:S(2)}) %collective-permute-start.5) | collective-permute-done | bytes 262176 | tf_op jit(solution)/shard_map/ppermute | solution.py:645
  59.0 0.0 copy-start.6
  59.1 6.4 %branch.1 = (f32[1,64,64]{2,1,0:T(8,128)}, f32[64,128]{1,0:T(8,128)S(1)}) custom-call(s32[2]{0:T(128)S(1)} %pad_add_fusion.at_ref, f32[64,128]{1,0:T(8,128)S(1)} %get-tuple-element.13.p0, f32[64,128]{1,0:T(8,128)S(1)} %collective-permute-done.2.p1, f32[2,64,128]{2,1,0:T(8,128)S(1)} %collective-permute-done.3.p2, ...), custom_call_target="tpu_custom_call" | custom-call | flops 5750000128 | bytes 4096 | tf_op jit(solution)/shard_map/branch/pallas_call | solution.py:585
  65.4 1.3 %collective-permute-start.6 = (f32[64,128]{1,0:T(8,128)S(1)}, f32[64,128]{1,0:T(8,128)S(1)}, u32[]{:S(2)}, u32[]{:S(2)}) collective-permute-start(f32[64,128]{1,0:T(8,128)S(1)} %get-tuple-element.15.l0), channel_id=1, source_target_pairs={{0,16},{16,0},{32,48},{48,32},{64,80},{80,64},{96,112},{112,96},{1... | collective-permute-start | bytes 98312 | tf_op jit(solution)/shard_map/ppermute | solution.py:645
  66.7 0.0 copy-done.6
  66.7 0.9 collective-permute-done.6.l1
  67.6 0.0 copy-start.4
  67.6 1.7 %collective-permute-start.7 = (f32[2,64,128]{2,1,0:T(8,128)S(1)}, f32[2,64,128]{2,1,0:T(8,128)S(1)}, u32[]{:S(2)}, u32[]{:S(2)}) collective-permute-start(f32[2,64,128]{2,1,0:T(8,128)S(1)} %pad_maximum_fusion.4), channel_id=1, source_target_pairs={{0,32},{16,48},{32,0},{48,16},{64,96},{80,112},{96,64},{112,80},{1... | collective-permute-start | bytes 196616 | tf_op jit(solution)/shard_map/ppermute | solution.py:645
  69.3 0.0 collective-permute-done.near_ref
  69.3 0.0 collective-permute-done.1.far_ref
  69.3 2.8 %prep.1.d_ref = bf16[192,64,256]{2,1,0:T(8,128)(2,1)S(1)} custom-call(s32[1]{0:T(128)S(6)} %select_n.29.odd_ref, f32[33,32,128]{2,1,0:T(8,128)S(1)} %collective-permute-done.near_ref, f32[32,64,128]{2,1,0:T(8,128)S(1)} %get-tuple-element.11.low_ref.own_ref, f32[33,32,128]{2,1,0:T(8,128)S(1)} %collective-permute-done.1.far_ref), custom_call_target="tpu_custom_call" | custom-call | flops 3449999872 | bytes 4096 | tf_op jit(solution)/shard_map/prep/pallas_call | solution.py:446
  72.1 0.0 copy-done.4
  72.1 0.0 copy-start.2
  72.1 6.4 %shard_map.87.refs_0_ = f32[64,64,512]{2,1,0:T(8,128)} custom-call(s32[512]{0:T(512)S(1)} %broadcast_subtract_fusion.cols_ref, bf16[128,64,256]{2,1,0:T(8,128)(2,1)S(1)} %copy-done.4, bf16[192,64,256]{2,1,0:T(8,128)(2,1)S(1)} %prep.1.d_ref), custom_call_target="tpu_custom_call" | custom-call | flops 9200000000 | bytes 4096 | tf_op jit(solution)/shard_map/pallas_call | solution.py:509
  78.6 0.0 collective-permute-done.7.l2
  78.6 0.0 copy-start
  78.6 1.9 %collective-permute-start.8 = (f32[4,64,128]{2,1,0:T(8,128)S(1)}, f32[4,64,128]{2,1,0:T(8,128)S(1)}, u32[]{:S(2)}, u32[]{:S(2)}) collective-permute-start(f32[4,64,128]{2,1,0:T(8,128)S(1)} %pad_maximum_fusion.2), channel_id=1, source_target_pairs={{0,96},{16,112},{32,64},{48,80},{64,32},{80,48},{96,0},{112,16},{1... | collective-permute-start | bytes 393224 | tf_op jit(solution)/shard_map/ppermute | solution.py:645
  80.5 0.0 copy-done.2
  80.5 6.3 %shard_map.88 = f32[64,64,512]{2,1,0:T(8,128)} custom-call(s32[512]{0:T(512)S(1)} %broadcast_subtract_fusion.cols_ref, bf16[128,64,256]{2,1,0:T(8,128)(2,1)S(1)} %copy-done.2, bf16[192,64,256]{2,1,0:T(8,128)(2,1)S(1)} %prep.1.d_ref, f32[64,64,512]{2,1,0:T(8,128)} %shard_map.87.refs_0_), custom_call_target="tpu_custom_call", output_to_operand_aliasing={{}: (3, {})} | custom-call | flops 9200000000 | bytes 4096 | tf_op jit(solution)/shard_map/pallas_call | solution.py:509
  86.9 0.0 collective-permute-done.8.l3
  86.9 0.0 copy-done
  86.9 2.2 %far.1 = f32[64,16,64]{2,1,0:T(8,128)} custom-call(s32[16]{0:T(128)S(1)} %broadcast_xor_fusion.cols_ref, f32[64,16,64]{2,1,0:T(8,128)S(1)} %bitcast.18, f32[64,128]{1,0:T(8,128)S(1)} %get-tuple-element.15.l0, f32[64,128]{1,0:T(8,128)S(1)} %collective-permute-done.6.l1, f32[2,64,128]{2,1,0:T(8,128)S(1)} %collective-permute-done.7.l2, ...), custom_call_target="tpu_custom_call" | custom-call | flops 3449999872 | bytes 4096 | tf_op jit(solution)/shard_map/far/pallas_call | solution.py:632
  (7 shorter events, 0.1 us)
Async XLA Ops:
  9.6 19.9 %collective-permute-start.2 = (f32[64,128]{1,0:T(8,128)S(1)}, f32[64,128]{1,0:T(8,128)S(1)}, u32[]{:S(2)}, u32[]{:S(2)}) collective-permute-start(f32[64,128]{1,0:T(8,128)S(1)} %get-tuple-element.13.p0), channel_id=1, source_target_pairs={{0,1},{1,0},{2,3},{3,2},{4,5},{5,4},{6,7},{7,6},{8,9},{9,8},{10,11... | collective-permute-start | bytes 98312 | tf_op jit(solution)/shard_map/ppermute | solution.py:645
  20.0 49.3 %collective-permute-start = (f32[33,32,128]{2,1,0:T(8,128)S(1)}, f32[33,32,128]{2,1,0:T(8,128)S(1)}, u32[]{:S(2)}, u32[]{:S(2)}) collective-permute-start(f32[33,32,128]{2,1,0:T(8,128)S(1)} %get-tuple-element.12), channel_id=1, source_target_pairs={{0,1},{1,0},{2,3},{3,2},{4,5},{5,4},{6,7},{7,6},{8,9},{9,8},{10,11... | collective-permute-start | bytes 1622024 | tf_op jit(solution)/shard_map/ppermute | solution.py:670
  20.1 49.2 %collective-permute-start.1 = (f32[33,32,128]{2,1,0:T(8,128)S(1)}, f32[33,32,128]{2,1,0:T(8,128)S(1)}, u32[]{:S(2)}, u32[]{:S(2)}) collective-permute-start(f32[33,32,128]{2,1,0:T(8,128)S(1)} %get-tuple-element.12), channel_id=1, source_target_pairs={{1,2},{3,4},{5,6},{7,8},{9,10},{11,12},{13,14},{15,16},{17,18},{19... | collective-permute-start | bytes 1622024 | tf_op jit(solution)/shard_map/ppermute | solution.py:672
  29.5 12.7 %collective-permute-start.3 = (f32[2,64,128]{2,1,0:T(8,128)S(1)}, f32[2,64,128]{2,1,0:T(8,128)S(1)}, u32[]{:S(2)}, u32[]{:S(2)}) collective-permute-start(f32[2,64,128]{2,1,0:T(8,128)S(1)} %pad_maximum_fusion.3), channel_id=1, source_target_pairs={{0,3},{1,2},{2,1},{3,0},{4,7},{5,6},{6,5},{7,4},{8,11},{9,10},{10,... | collective-permute-start | bytes 196616 | tf_op jit(solution)/shard_map/ppermute | solution.py:645
  35.5 2.0 %copy-start.1 = (bf16[128,64,256]{2,1,0:T(8,128)(2,1)}, bf16[128,64,256]{2,1,0:T(8,128)(2,1)S(1)}, u32[]{:S(2)}) copy-start(bf16[128,64,256]{2,1,0:T(8,128)(2,1)S(1)} %shard_map.85.y_ref) | copy-start | bytes 12582916
  42.2 8.3 %copy-start.5 = (s32[512]{0:T(512)S(1)}, s32[512]{0:T(512)}, u32[]{:S(2)}) copy-start(s32[512]{0:T(512)} %param.9) | copy-start | bytes 6148
  42.2 8.1 %collective-permute-start.4 = (f32[4,64,128]{2,1,0:T(8,128)S(1)}, f32[4,64,128]{2,1,0:T(8,128)S(1)}, u32[]{:S(2)}, u32[]{:S(2)}) collective-permute-start(f32[4,64,128]{2,1,0:T(8,128)S(1)} %pad_maximum_fusion.1), channel_id=1, source_target_pairs={{0,4},{1,5},{2,6},{3,7},{4,0},{5,1},{6,2},{7,3},{8,12},{9,13},{10,... | collective-permute-start | bytes 393224 | tf_op jit(solution)/shard_map/ppermute | solution.py:645
  48.3 2.0 %copy-start.3 = (bf16[128,64,256]{2,1,0:T(8,128)(2,1)}, bf16[128,64,256]{2,1,0:T(8,128)(2,1)S(1)}, u32[]{:S(2)}) copy-start(bf16[128,64,256]{2,1,0:T(8,128)(2,1)S(1)} %shard_map.86.y_ref) | copy-start | bytes 12582916
  50.3 8.7 %collective-permute-start.5 = (f32[8,64,128]{2,1,0:T(8,128)S(1)}, f32[8,64,128]{2,1,0:T(8,128)S(1)}, u32[]{:S(2)}, u32[]{:S(2)}) collective-permute-start(f32[8,64,128]{2,1,0:T(8,128)S(1)} %pad_maximum_fusion), channel_id=1, source_target_pairs={{0,12},{1,13},{2,14},{3,15},{4,8},{5,9},{6,10},{7,11},{8,4},{9,5},... | collective-permute-start | bytes 786440 | tf_op jit(solution)/shard_map/ppermute | solution.py:645
  59.0 7.7 %copy-start.6 = (s32[16]{0:T(128)S(1)}, s32[16]{0:T(128)}, u32[]{:S(2)}) copy-start(s32[16]{0:T(128)} %param.11) | copy-start | bytes 196
  65.4 2.1 %collective-permute-start.6 = (f32[64,128]{1,0:T(8,128)S(1)}, f32[64,128]{1,0:T(8,128)S(1)}, u32[]{:S(2)}, u32[]{:S(2)}) collective-permute-start(f32[64,128]{1,0:T(8,128)S(1)} %get-tuple-element.15.l0), channel_id=1, source_target_pairs={{0,16},{16,0},{32,48},{48,32},{64,80},{80,64},{96,112},{112,96},{1... | collective-permute-start | bytes 98312 | tf_op jit(solution)/shard_map/ppermute | solution.py:645
  67.6 4.6 %copy-start.4 = (bf16[128,64,256]{2,1,0:T(8,128)(2,1)S(1)}, bf16[128,64,256]{2,1,0:T(8,128)(2,1)}, u32[]{:S(2)}) copy-start(bf16[128,64,256]{2,1,0:T(8,128)(2,1)} %copy-done.3) | copy-start | bytes 12582916
  67.6 11.0 %collective-permute-start.7 = (f32[2,64,128]{2,1,0:T(8,128)S(1)}, f32[2,64,128]{2,1,0:T(8,128)S(1)}, u32[]{:S(2)}, u32[]{:S(2)}) collective-permute-start(f32[2,64,128]{2,1,0:T(8,128)S(1)} %pad_maximum_fusion.4), channel_id=1, source_target_pairs={{0,32},{16,48},{32,0},{48,16},{64,96},{80,112},{96,64},{112,80},{1... | collective-permute-start | bytes 196616 | tf_op jit(solution)/shard_map/ppermute | solution.py:645
  72.1 8.4 %copy-start.2 = (bf16[128,64,256]{2,1,0:T(8,128)(2,1)S(1)}, bf16[128,64,256]{2,1,0:T(8,128)(2,1)}, u32[]{:S(2)}) copy-start(bf16[128,64,256]{2,1,0:T(8,128)(2,1)} %copy-done.1) | copy-start | bytes 12582916
  78.6 8.2 %copy-start = (f32[64,64,16]{1,2,0:T(8,128)S(1)}, f32[64,64,16]{1,2,0:T(8,128)}, u32[]{:S(2)}) copy-start(f32[64,64,16]{1,2,0:T(8,128)} %param.10) | copy-start | bytes 786436
  78.6 8.2 %collective-permute-start.8 = (f32[4,64,128]{2,1,0:T(8,128)S(1)}, f32[4,64,128]{2,1,0:T(8,128)S(1)}, u32[]{:S(2)}, u32[]{:S(2)}) collective-permute-start(f32[4,64,128]{2,1,0:T(8,128)S(1)} %pad_maximum_fusion.2), channel_id=1, source_target_pairs={{0,96},{16,112},{32,64},{48,80},{64,32},{80,48},{96,0},{112,16},{1... | collective-permute-start | bytes 393224 | tf_op jit(solution)/shard_map/ppermute | solution.py:645

commit v7 on v6

--- a/solution.py
+++ b/solution.py
@@ -231,7 +231,7 @@
                 a_ref[base + j, it * 8 : it * 8 + 8, :] = v[j]
 
 
-EARLY = 3
+EARLY = 2
 
 
 def chol_head_kernel(g_ref, a_ref, u_ref):
@@ -339,60 +339,73 @@
     )(part)
 
 
-def half_kernel(c0_ref, c1_ref, low_ref, y_ref, s_ref, u_ref, part):
-    step = pl.program_id(0)
+def half_kernel(c_hbm, low_ref, y_ref, c_ref, s_ref, u_ref, sem, part):
+    copies = [
+        [
+            pltpu.make_async_copy(
+                c_hbm.at[pl.ds(16 * n, 16), :, pl.ds((part + 2 * c) * 128, 128)],
+                c_ref.at[c, pl.ds(16 * n, 16)],
+                sem.at[n, c],
+            )
+            for c in range(2)
+        ]
+        for n in range(4)
+    ]
+    for group in copies:
+        for copy in group:
+            copy.start()
 
     def turn(s, _):
         for r in range(8):
-            u_ref[r] = rows(c0_ref[s * 8 + r], c1_ref[s * 8 + r]).T
-        at = pl.ds(pl.multiple_of(step * 16 + s * 8, 8), 8)
+            u_ref[r] = rows(c_ref[0, s * 8 + r], c_ref[1, s * 8 + r]).T
+        at = pl.ds(pl.multiple_of(s * 8, 8), 8)
         for g in range(16):
             s_ref[8 * g : 8 * g + 8, at, :] = jnp.swapaxes(u_ref[:, 8 * g : 8 * g + 8, :], 0, 1)
         return 0
 
-    lax.fori_loop(0, 2, turn, 0)
-
-    @pl.when(step == 3)
-    def _():
-        first = first_half((64, 256))
-
-        def leaf(s, _):
-            ts = [s * HALF + j for j in range(HALF)]
-            lefts = []
-            for t in ts:
-                lh, ll = split(low_ref[16 * part + t])
-                lefts.append(rows(lh, ll, lh).T)
-            at = [(j, n) for j in range(HALF) for n in range(0, 8, 2)]
-            zs = []
-            for j, n in at:
-                wh, wl = split(lanes(s_ref[ts[j] * 8 + n], s_ref[ts[j] * 8 + n + 1]))
-                zs.append(mm(lefts[j], rows(wh, wh, wl)))
-            for (j, n), z in zip(at, zs):
-                yh, yl = split(jnp.where(first, z[0:64], z[64:128]))
-                for m in range(2):
-                    b = ts[j] * 8 + n + m
-                    y_ref[b, :, 0:128] = yh[:, m * 128 : m * 128 + 128]
-                    y_ref[b, :, 128:256] = yl[:, m * 128 : m * 128 + 128]
-            return 0
-
-        lax.fori_loop(0, 16 // HALF, leaf, 0)
+    for n in range(4):
+        for copy in copies[n]:
+            copy.wait()
+        lax.fori_loop(2 * n, 2 * n + 2, turn, 0)
+    first = first_half((64, 256))
+
+    def leaf(s, _):
+        ts = [s * HALF + j for j in range(HALF)]
+        lefts = []
+        for t in ts:
+            lh, ll = split(low_ref[16 * part + t])
+            lefts.append(rows(lh, ll, lh).T)
+        at = [(j, n) for j in range(HALF) for n in range(0, 8, 2)]
+        zs = []
+        for j, n in at:
+            wh, wl = split(lanes(s_ref[ts[j] * 8 + n], s_ref[ts[j] * 8 + n + 1]))
+            zs.append(mm(lefts[j], rows(wh, wh, wl)))
+        for (j, n), z in zip(at, zs):
+            yh, yl = split(jnp.where(first, z[0:64], z[64:128]))
+            for m in range(2):
+                b = ts[j] * 8 + n + m
+                y_ref[b, :, 0:128] = yh[:, m * 128 : m * 128 + 128]
+                y_ref[b, :, 128:256] = yl[:, m * 128 : m * 128 + 128]
+        return 0
+
+    lax.fori_loop(0, 16 // HALF, leaf, 0)
 
 
 def half_leaf(coupling, low, part):
     return pl.pallas_call(
         functools.partial(half_kernel, part=part),
         out_shape=jax.ShapeDtypeStruct((128, 64, 256), BF16),
-        grid=(4,),
-        in_specs=[
-            pl.BlockSpec((16, 64, 128), lambda s: (s, 0, part)),
-            pl.BlockSpec((16, 64, 128), lambda s: (s, 0, part + 2)),
-            pl.BlockSpec((32, 64, 128), lambda s: (0, 0, 0)),
+        in_specs=[pl.BlockSpec(memory_space=pltpu.HBM), VMEM],
+        out_specs=VMEM,
+        scratch_shapes=[
+            pltpu.VMEM((2, 64, 64, 128), F32),
+            pltpu.VMEM((128, 64, 128), F32),
+            pltpu.VMEM((8, 128, 128), F32),
+            pltpu.SemaphoreType.DMA((4, 2)),
         ],
-        out_specs=pl.BlockSpec((128, 64, 256), lambda s: (0, 0, 0)),
-        scratch_shapes=[pltpu.VMEM((128, 64, 128), F32), pltpu.VMEM((8, 128, 128), F32)],
-        compiler_params=params(22),
+        compiler_params=params(18),
         cost_estimate=cost(6),
-    )(coupling, coupling, low)
+    )(coupling, low)
 
 
 def prep_kernel(odd_ref, near_ref, own_ref, far_ref, d_ref):

time: 89.3 us -> 88.6 us (level)
  Pallas kernels: 53.2 us -> 51.9 us
    pallas_call x2, Pallas kernels: 11.9 us -> 10.4 us  [half_leaf(): pl.pallas_call(functools.partial(half_kernel, part=part), out_shape=jax.S...]
  transfers between devices with their start and end apart: 9 -> 9, of which waited for: 3 -> 3; matrix products, arithmetic and copies ran while one was open for 0% -> 0% of each run, Pallas kernels for 47% -> 46%
where the time goes in v7:
time: 88.6 us; the launch traced here: 88.5 us
  Pallas kernels  51.9 us (59%)
  starting transfers between devices  16.8 us (19%)
  waiting for transfers between devices  14.9 us (17%)
  local copies, waits for them, and re-layouts  3.98 us (4%)
    ppermute x7, waiting for transfers between devices, shifted(): lax.ppermute(value, axis, [(i, to(i)) for i in range(lax.axis_size(axis))])  14.9 us
    pallas_call x2, Pallas kernels, full_leaf(): pl.pallas_call(functools.partial(full_kernel, part=part), out_shape=jax.S...  12.9 us
    pallas_call x2, Pallas kernels, half_leaf(): pl.pallas_call(functools.partial(half_kernel, part=part), out_shape=jax.S...  10.4 us
    ppermute x1, starting transfers between devices, steps(): low_far = lax.ppermute(pack, both, later + [(j, i) for i, j in later])  9.38 us
    pallas_call x1, Pallas kernels, climb(): pl.pallas_call(climb_kernel, out_shape=(jax.ShapeDtypeStruct((32, 64, 128...  8.92 us
    ppermute x7, starting transfers between devices, shifted(): lax.ppermute(value, axis, [(i, to(i)) for i in range(lax.axis_size(axis))])  7.34 us
    pallas_call x1, Pallas kernels, branch(): pl.pallas_call(branch_kernel, out_shape=(jax.ShapeDtypeStruct((1, 64, 64)...  6.37 us
    unnamed x14, local copies, waits for them, and re-layouts  3.98 us
  transfers between devices with their start and end apart: 9, of which 3 were waited for; matrix products, arithmetic and copies ran while one was open for 0% of the time, Pallas kernels for 46%

profile of v7, /device:TPU:1, one launch (start us, length us, event | category | flops | bytes accessed | tf_op | source)
XLA Modules:
  0.0 88.5 jit_solution(2692975130191325715)
XLA Ops:
  0.6 8.9 %climb.1 = (f32[32,64,128]{2,1,0:T(8,128)S(1)}, f32[64,128]{1,0:T(8,128)S(1)}, f32[64,128]{1,0:T(8,128)S(1)}) custom-call(bf16[64,64,256]{2,1,0:T(8,128)(2,1)} %b_hbm.1, f32[64,64,128]{2,1,0:T(8,128)} %t_hbm.1), custom_call_target="tpu_custom_call" | custom-call | flops 11500000256 | bytes 4096 | tf_op jit(solution)/shard_map/climb/pallas_call | solution.py:166
  9.6 2.2 %collective-permute-start.2 = (f32[64,128]{1,0:T(8,128)S(1)}, f32[64,128]{1,0:T(8,128)S(1)}, u32[]{:S(2)}, u32[]{:S(2)}) collective-permute-start(f32[64,128]{1,0:T(8,128)S(1)} %get-tuple-element.13.p0), channel_id=1, source_target_pairs={{0,1},{1,0},{2,3},{3,2},{4,5},{5,4},{6,7},{7,6},{8,9},{9,8},{10,11... | collective-permute-start | bytes 98312 | tf_op jit(solution)/shard_map/ppermute | solution.py:658
  11.8 2.4 %chol_head.1.i_ref = f32[64,64,128]{2,1,0:T(8,128)S(1)} custom-call(f32[32,64,128]{2,1,0:T(8,128)S(1)} %get-tuple-element.10.g_ref), custom_call_target="tpu_custom_call" | custom-call | flops 4600000000 | bytes 4096 | tf_op jit(solution)/shard_map/chol_head/pallas_call | solution.py:253
  14.2 2.3 %chol_mid.1.a_ref = f32[64,64,128]{2,1,0:T(8,128)S(1)} custom-call(f32[64,64,128]{2,1,0:T(8,128)S(1)} %chol_head.1.i_ref), custom_call_target="tpu_custom_call" | custom-call | flops 3449999872 | bytes 4096 | tf_op jit(solution)/shard_map/chol_mid/pallas_call | solution.py:271
  16.5 3.5 %chol_tail.1 = (f32[32,64,128]{2,1,0:T(8,128)S(1)}, f32[33,32,128]{2,1,0:T(8,128)S(1)}) custom-call(f32[64,64,128]{2,1,0:T(8,128)S(1)} %chol_mid.1.a_ref), custom_call_target="tpu_custom_call" | custom-call | flops 5750000128 | bytes 4096 | tf_op jit(solution)/shard_map/chol_tail/pallas_call | solution.py:324
  20.0 0.1 collective-permute-start
  20.1 9.4 %collective-permute-start.1 = (f32[33,32,128]{2,1,0:T(8,128)S(1)}, f32[33,32,128]{2,1,0:T(8,128)S(1)}, u32[]{:S(2)}, u32[]{:S(2)}) collective-permute-start(f32[33,32,128]{2,1,0:T(8,128)S(1)} %get-tuple-element.12), channel_id=1, source_target_pairs={{1,2},{3,4},{5,6},{7,8},{9,10},{11,12},{13,14},{15,16},{17,18},{19... | collective-permute-start | bytes 1622024 | tf_op jit(solution)/shard_map/ppermute | solution.py:685
  29.5 0.0 collective-permute-done.2.p1
  29.5 0.1 collective-permute-start.3
  29.6 5.2 %shard_map.85.y_ref = bf16[128,64,256]{2,1,0:T(8,128)(2,1)S(1)} custom-call(f32[64,64,512]{2,1,0:T(8,128)} %c_hbm.3, f32[32,64,128]{2,1,0:T(8,128)S(1)} %get-tuple-element.11.low_ref.own_ref), custom_call_target="tpu_custom_call" | custom-call | flops 6899999744 | bytes 4096 | tf_op jit(solution)/shard_map/pallas_call | solution.py:395
  34.8 0.0 copy-start.1
  34.8 1.9 %copy-done.1 = bf16[128,64,256]{2,1,0:T(8,128)(2,1)} copy-done((bf16[128,64,256]{2,1,0:T(8,128)(2,1)}, bf16[128,64,256]{2,1,0:T(8,128)(2,1)S(1)}, u32[]{:S(2)}) %copy-start.1) | copy-done | bytes 4194328
  36.7 5.5 %collective-permute-done.3.p2 = f32[2,64,128]{2,1,0:T(8,128)S(1)} collective-permute-done((f32[2,64,128]{2,1,0:T(8,128)S(1)}, f32[2,64,128]{2,1,0:T(8,128)S(1)}, u32[]{:S(2)}, u32[]{:S(2)}) %collective-permute-start.3) | collective-permute-done | bytes 65568 | tf_op jit(solution)/shard_map/ppermute | solution.py:658
  42.2 0.0 copy-start.5
  42.3 0.1 collective-permute-start.4
  42.3 5.2 %shard_map.86.y_ref = bf16[128,64,256]{2,1,0:T(8,128)(2,1)S(1)} custom-call(f32[64,64,512]{2,1,0:T(8,128)} %c_hbm.3, f32[32,64,128]{2,1,0:T(8,128)S(1)} %get-tuple-element.11.low_ref.own_ref), custom_call_target="tpu_custom_call" | custom-call | flops 6899999744 | bytes 4096 | tf_op jit(solution)/shard_map/pallas_call | solution.py:395
  47.6 0.0 copy-start.3
  47.6 2.0 %copy-done.3 = bf16[128,64,256]{2,1,0:T(8,128)(2,1)} copy-done((bf16[128,64,256]{2,1,0:T(8,128)(2,1)}, bf16[128,64,256]{2,1,0:T(8,128)(2,1)S(1)}, u32[]{:S(2)}) %copy-start.3) | copy-done | bytes 4194328
  49.6 0.0 collective-permute-done.4.p3
  49.6 0.3 collective-permute-start.5
  49.9 0.1 pad_add_fusion.at_ref
  50.0 0.0 copy-done.5
  50.0 8.5 %collective-permute-done.5.p4 = f32[8,64,128]{2,1,0:T(8,128)S(1)} collective-permute-done((f32[8,64,128]{2,1,0:T(8,128)S(1)}, f32[8,64,128]{2,1,0:T(8,128)S(1)}, u32[]{:S(2)}, u32[]{:S(2)}) %collective-permute-start.5) | collective-permute-done | bytes 262176 | tf_op jit(solution)/shard_map/ppermute | solution.py:658
  58.5 0.0 copy-start.6
  58.5 6.4 %branch.1 = (f32[1,64,64]{2,1,0:T(8,128)}, f32[64,128]{1,0:T(8,128)S(1)}) custom-call(s32[2]{0:T(128)S(1)} %pad_add_fusion.at_ref, f32[64,128]{1,0:T(8,128)S(1)} %get-tuple-element.13.p0, f32[64,128]{1,0:T(8,128)S(1)} %collective-permute-done.2.p1, f32[2,64,128]{2,1,0:T(8,128)S(1)} %collective-permute-done.3.p2, ...), custom_call_target="tpu_custom_call" | custom-call | flops 5750000128 | bytes 4096 | tf_op jit(solution)/shard_map/branch/pallas_call | solution.py:598
  64.9 1.3 %collective-permute-start.6 = (f32[64,128]{1,0:T(8,128)S(1)}, f32[64,128]{1,0:T(8,128)S(1)}, u32[]{:S(2)}, u32[]{:S(2)}) collective-permute-start(f32[64,128]{1,0:T(8,128)S(1)} %get-tuple-element.15.l0), channel_id=1, source_target_pairs={{0,16},{16,0},{32,48},{48,32},{64,80},{80,64},{96,112},{112,96},{1... | collective-permute-start | bytes 98312 | tf_op jit(solution)/shard_map/ppermute | solution.py:658
  66.2 0.0 copy-done.6
  66.2 0.9 collective-permute-done.6.l1
  67.0 0.0 copy-start.4
  67.0 1.5 %collective-permute-start.7 = (f32[2,64,128]{2,1,0:T(8,128)S(1)}, f32[2,64,128]{2,1,0:T(8,128)S(1)}, u32[]{:S(2)}, u32[]{:S(2)}) collective-permute-start(f32[2,64,128]{2,1,0:T(8,128)S(1)} %pad_maximum_fusion.4), channel_id=1, source_target_pairs={{0,32},{16,48},{32,0},{48,16},{64,96},{80,112},{96,64},{112,80},{1... | collective-permute-start | bytes 196616 | tf_op jit(solution)/shard_map/ppermute | solution.py:658
  68.6 0.0 collective-permute-done.near_ref
  68.6 0.0 collective-permute-done.1.far_ref
  68.6 2.8 %prep.1.d_ref = bf16[192,64,256]{2,1,0:T(8,128)(2,1)S(1)} custom-call(s32[1]{0:T(128)S(6)} %select_n.29.odd_ref, f32[33,32,128]{2,1,0:T(8,128)S(1)} %collective-permute-done.near_ref, f32[32,64,128]{2,1,0:T(8,128)S(1)} %get-tuple-element.11.low_ref.own_ref, f32[33,32,128]{2,1,0:T(8,128)S(1)} %collective-permute-done.1.far_ref), custom_call_target="tpu_custom_call" | custom-call | flops 3449999872 | bytes 4096 | tf_op jit(solution)/shard_map/prep/pallas_call | solution.py:459
  71.4 0.0 copy-done.4
  71.4 0.0 copy-start.2
  71.4 6.4 %shard_map.87.refs_0_ = f32[64,64,512]{2,1,0:T(8,128)} custom-call(s32[512]{0:T(512)S(1)} %broadcast_subtract_fusion.cols_ref, bf16[128,64,256]{2,1,0:T(8,128)(2,1)S(1)} %copy-done.4, bf16[192,64,256]{2,1,0:T(8,128)(2,1)S(1)} %prep.1.d_ref), custom_call_target="tpu_custom_call" | custom-call | flops 9200000000 | bytes 4096 | tf_op jit(solution)/shard_map/pallas_call | solution.py:522
  77.9 0.0 collective-permute-done.7.l2
  77.9 0.0 copy-start
  77.9 1.9 %collective-permute-start.8 = (f32[4,64,128]{2,1,0:T(8,128)S(1)}, f32[4,64,128]{2,1,0:T(8,128)S(1)}, u32[]{:S(2)}, u32[]{:S(2)}) collective-permute-start(f32[4,64,128]{2,1,0:T(8,128)S(1)} %pad_maximum_fusion.2), channel_id=1, source_target_pairs={{0,96},{16,112},{32,64},{48,80},{64,32},{80,48},{96,0},{112,16},{1... | collective-permute-start | bytes 393224 | tf_op jit(solution)/shard_map/ppermute | solution.py:658
  79.8 0.0 copy-done.2
  79.8 6.4 %shard_map.88 = f32[64,64,512]{2,1,0:T(8,128)} custom-call(s32[512]{0:T(512)S(1)} %broadcast_subtract_fusion.cols_ref, bf16[128,64,256]{2,1,0:T(8,128)(2,1)S(1)} %copy-done.2, bf16[192,64,256]{2,1,0:T(8,128)(2,1)S(1)} %prep.1.d_ref, f32[64,64,512]{2,1,0:T(8,128)} %shard_map.87.refs_0_), custom_call_target="tpu_custom_call", output_to_operand_aliasing={{}: (3, {})} | custom-call | flops 9200000000 | bytes 4096 | tf_op jit(solution)/shard_map/pallas_call | solution.py:522
  86.3 0.0 collective-permute-done.8.l3
  86.3 0.0 copy-done
  86.3 2.2 %far.1 = f32[64,16,64]{2,1,0:T(8,128)} custom-call(s32[16]{0:T(128)S(1)} %broadcast_xor_fusion.cols_ref, f32[64,16,64]{2,1,0:T(8,128)S(1)} %bitcast.18, f32[64,128]{1,0:T(8,128)S(1)} %get-tuple-element.15.l0, f32[64,128]{1,0:T(8,128)S(1)} %collective-permute-done.6.l1, f32[2,64,128]{2,1,0:T(8,128)S(1)} %collective-permute-done.7.l2, ...), custom_call_target="tpu_custom_call" | custom-call | flops 3449999872 | bytes 4096 | tf_op jit(solution)/shard_map/far/pallas_call | solution.py:645
  (7 shorter events, 0.1 us)
Async XLA Ops:
  9.6 19.9 %collective-permute-start.2 = (f32[64,128]{1,0:T(8,128)S(1)}, f32[64,128]{1,0:T(8,128)S(1)}, u32[]{:S(2)}, u32[]{:S(2)}) collective-permute-start(f32[64,128]{1,0:T(8,128)S(1)} %get-tuple-element.13.p0), channel_id=1, source_target_pairs={{0,1},{1,0},{2,3},{3,2},{4,5},{5,4},{6,7},{7,6},{8,9},{9,8},{10,11... | collective-permute-start | bytes 98312 | tf_op jit(solution)/shard_map/ppermute | solution.py:658
  20.0 48.6 %collective-permute-start = (f32[33,32,128]{2,1,0:T(8,128)S(1)}, f32[33,32,128]{2,1,0:T(8,128)S(1)}, u32[]{:S(2)}, u32[]{:S(2)}) collective-permute-start(f32[33,32,128]{2,1,0:T(8,128)S(1)} %get-tuple-element.12), channel_id=1, source_target_pairs={{0,1},{1,0},{2,3},{3,2},{4,5},{5,4},{6,7},{7,6},{8,9},{9,8},{10,11... | collective-permute-start | bytes 1622024 | tf_op jit(solution)/shard_map/ppermute | solution.py:683
  20.1 48.5 %collective-permute-start.1 = (f32[33,32,128]{2,1,0:T(8,128)S(1)}, f32[33,32,128]{2,1,0:T(8,128)S(1)}, u32[]{:S(2)}, u32[]{:S(2)}) collective-permute-start(f32[33,32,128]{2,1,0:T(8,128)S(1)} %get-tuple-element.12), channel_id=1, source_target_pairs={{1,2},{3,4},{5,6},{7,8},{9,10},{11,12},{13,14},{15,16},{17,18},{19... | collective-permute-start | bytes 1622024 | tf_op jit(solution)/shard_map/ppermute | solution.py:685
  29.5 12.7 %collective-permute-start.3 = (f32[2,64,128]{2,1,0:T(8,128)S(1)}, f32[2,64,128]{2,1,0:T(8,128)S(1)}, u32[]{:S(2)}, u32[]{:S(2)}) collective-permute-start(f32[2,64,128]{2,1,0:T(8,128)S(1)} %pad_maximum_fusion.3), channel_id=1, source_target_pairs={{0,3},{1,2},{2,1},{3,0},{4,7},{5,6},{6,5},{7,4},{8,11},{9,10},{10,... | collective-permute-start | bytes 196616 | tf_op jit(solution)/shard_map/ppermute | solution.py:658
  34.8 2.0 %copy-start.1 = (bf16[128,64,256]{2,1,0:T(8,128)(2,1)}, bf16[128,64,256]{2,1,0:T(8,128)(2,1)S(1)}, u32[]{:S(2)}) copy-start(bf16[128,64,256]{2,1,0:T(8,128)(2,1)S(1)} %shard_map.85.y_ref) | copy-start | bytes 12582916
  42.2 7.7 %copy-start.5 = (s32[512]{0:T(512)S(1)}, s32[512]{0:T(512)}, u32[]{:S(2)}) copy-start(s32[512]{0:T(512)} %param.9) | copy-start | bytes 6148
  42.3 7.3 %collective-permute-start.4 = (f32[4,64,128]{2,1,0:T(8,128)S(1)}, f32[4,64,128]{2,1,0:T(8,128)S(1)}, u32[]{:S(2)}, u32[]{:S(2)}) collective-permute-start(f32[4,64,128]{2,1,0:T(8,128)S(1)} %pad_maximum_fusion.1), channel_id=1, source_target_pairs={{0,4},{1,5},{2,6},{3,7},{4,0},{5,1},{6,2},{7,3},{8,12},{9,13},{10,... | collective-permute-start | bytes 393224 | tf_op jit(solution)/shard_map/ppermute | solution.py:658
  47.6 2.0 %copy-start.3 = (bf16[128,64,256]{2,1,0:T(8,128)(2,1)}, bf16[128,64,256]{2,1,0:T(8,128)(2,1)S(1)}, u32[]{:S(2)}) copy-start(bf16[128,64,256]{2,1,0:T(8,128)(2,1)S(1)} %shard_map.86.y_ref) | copy-start | bytes 12582916
  49.6 8.9 %collective-permute-start.5 = (f32[8,64,128]{2,1,0:T(8,128)S(1)}, f32[8,64,128]{2,1,0:T(8,128)S(1)}, u32[]{:S(2)}, u32[]{:S(2)}) collective-permute-start(f32[8,64,128]{2,1,0:T(8,128)S(1)} %pad_maximum_fusion), channel_id=1, source_target_pairs={{0,12},{1,13},{2,14},{3,15},{4,8},{5,9},{6,10},{7,11},{8,4},{9,5},... | collective-permute-start | bytes 786440 | tf_op jit(solution)/shard_map/ppermute | solution.py:658
  58.5 7.7 %copy-start.6 = (s32[16]{0:T(128)S(1)}, s32[16]{0:T(128)}, u32[]{:S(2)}) copy-start(s32[16]{0:T(128)} %param.11) | copy-start | bytes 196
  64.9 2.2 %collective-permute-start.6 = (f32[64,128]{1,0:T(8,128)S(1)}, f32[64,128]{1,0:T(8,128)S(1)}, u32[]{:S(2)}, u32[]{:S(2)}) collective-permute-start(f32[64,128]{1,0:T(8,128)S(1)} %get-tuple-element.15.l0), channel_id=1, source_target_pairs={{0,16},{16,0},{32,48},{48,32},{64,80},{80,64},{96,112},{112,96},{1... | collective-permute-start | bytes 98312 | tf_op jit(solution)/shard_map/ppermute | solution.py:658
  67.0 4.4 %copy-start.4 = (bf16[128,64,256]{2,1,0:T(8,128)(2,1)S(1)}, bf16[128,64,256]{2,1,0:T(8,128)(2,1)}, u32[]{:S(2)}) copy-start(bf16[128,64,256]{2,1,0:T(8,128)(2,1)} %copy-done.3) | copy-start | bytes 12582916
  67.0 10.9 %collective-permute-start.7 = (f32[2,64,128]{2,1,0:T(8,128)S(1)}, f32[2,64,128]{2,1,0:T(8,128)S(1)}, u32[]{:S(2)}, u32[]{:S(2)}) collective-permute-start(f32[2,64,128]{2,1,0:T(8,128)S(1)} %pad_maximum_fusion.4), channel_id=1, source_target_pairs={{0,32},{16,48},{32,0},{48,16},{64,96},{80,112},{96,64},{112,80},{1... | collective-permute-start | bytes 196616 | tf_op jit(solution)/shard_map/ppermute | solution.py:658
  71.4 8.4 %copy-start.2 = (bf16[128,64,256]{2,1,0:T(8,128)(2,1)S(1)}, bf16[128,64,256]{2,1,0:T(8,128)(2,1)}, u32[]{:S(2)}) copy-start(bf16[128,64,256]{2,1,0:T(8,128)(2,1)} %copy-done.1) | copy-start | bytes 12582916
  77.9 8.4 %copy-start = (f32[64,64,16]{1,2,0:T(8,128)S(1)}, f32[64,64,16]{1,2,0:T(8,128)}, u32[]{:S(2)}) copy-start(f32[64,64,16]{1,2,0:T(8,128)} %param.10) | copy-start | bytes 786436
  77.9 8.4 %collective-permute-start.8 = (f32[4,64,128]{2,1,0:T(8,128)S(1)}, f32[4,64,128]{2,1,0:T(8,128)S(1)}, u32[]{:S(2)}, u32[]{:S(2)}) collective-permute-start(f32[4,64,128]{2,1,0:T(8,128)S(1)} %pad_maximum_fusion.2), channel_id=1, source_target_pairs={{0,96},{16,112},{32,64},{48,80},{64,32},{80,48},{96,0},{112,16},{1... | collective-permute-start | bytes 393224 | tf_op jit(solution)/shard_map/ppermute | solution.py:658
